TPU v7x, 256 devices: a whole 4x4x8 slice. The times are simulated.
256 devices in a mesh: vel: 32 (over y, x, core), gy: 8 (over z).
Axes of the slice: x: 4, y: 4, z: 8, core: 2. Of those that a mesh axis runs over, the one named last changes fastest.
Arguments:
- distribution: float32 [13824, 2, 32, 128], P('vel', None, 'gy'), may hold values from 0.5 to 1.5
- body_mask: int32 [2, 32, 128], P(None, 'gy'), may hold values from 0 to 1, as said below
- inflow_flags: int32 [2, 32], replicated, may hold values 0 or 1
Outputs:
- advanced: float32 [13824, 2, 32, 128], P('vel', None, 'gy')
Inputs may be any that keep to these rules, and one draw needn't show every extreme that they name: `body_mask`: the body is one ellipse per plane, the same centre in both planes; it never touches the grid's edges.
All inputs are finite; a program needn't handle non-finite values.
Results may differ from a plain program's by a relative error of at most 0.0003.
Values sent between devices are 32-bit elements; how exact they have to be, the bound alone decides.
No kernel may reach another device: no remote copies, remote signals or barrier semaphores. Data moves between devices by JAX's collectives and lax.ppermute only.
A program may use at most 64 MiB of HBM per device.

v0:
```python
import jax
import jax.numpy as jnp
from jax import lax
from jax.sharding import PartitionSpec as P

NV1 = 24
STEPS = 2


dv_step = 0.6
time_step = 0.25
diffusivity_ratio = 2.0 / 3.0
baseline_shear_coefficient = 3000.0
baseline_warmth = 3.0
shear_power_index = 0.81
free_density = 200.0
free_temp = 1.0
free_speed = 3.0
wall_density = 200.0
wall_temp = 1.5


def with_halo(cells, sides, width):
    for axis, dim in sides:
        count = lax.axis_size(axis)
        head = lax.slice_in_dim(cells, 0, width, axis=dim)
        tail = lax.slice_in_dim(cells, cells.shape[dim] - width, cells.shape[dim], axis=dim)
        cells = jnp.concatenate(
            [
                lax.ppermute(tail, axis, [(i, (i + 1) % count) for i in range(count)]),
                cells,
                lax.ppermute(head, axis, [((i + 1) % count, i) for i in range(count)]),
            ],
            axis=dim,
        )
    return cells


def velocity_grid(per_axis, first_index, length):
    velocity_index = first_index + jnp.arange(length, dtype=jnp.int32)
    index_x = velocity_index // (per_axis * per_axis)
    index_y = velocity_index // per_axis % per_axis
    index_z = velocity_index % per_axis
    centre_index = 0.5 * (per_axis - 1)
    grid_x = (index_x.astype(jnp.float32) - centre_index) * dv_step
    grid_y = (index_y.astype(jnp.float32) - centre_index) * dv_step
    grid_z = (index_z.astype(jnp.float32) - centre_index) * dv_step
    return (grid_x, grid_y, grid_z)


def gaussian_distribution(
    fluid_concentration,
    cell_kinetic_warmth,
    random_motion_first,
    random_motion_second,
    random_motion_third,
):
    magnitude_square_norm = (
        random_motion_first * random_motion_first
        + random_motion_second * random_motion_second
        + random_motion_third * random_motion_third
    )
    return (
        fluid_concentration
        / jnp.power(2.0 * jnp.pi * cell_kinetic_warmth, 1.5)
        * jnp.exp(-magnitude_square_norm / (2.0 * cell_kinetic_warmth))
    )


def beam_warming(centre, upwind_one, upwind_two, courant):
    return (
        centre
        - 0.5 * courant * (3.0 * centre - 4.0 * upwind_one + upwind_two)
        + 0.5 * courant * courant * (centre - 2.0 * upwind_one + upwind_two)
    )


def sweep_x(state_now, velocity_x, inflow_value, flag_rows):
    x_cells = state_now.shape[-1]
    right_ghost = state_now[..., x_cells - 1 :]
    left_ghost = jnp.where(flag_rows[..., None] > 0, inflow_value, state_now[..., :1])
    padded = jnp.concatenate([left_ghost, left_ghost, state_now, right_ghost, right_ghost], -1)
    courant = jnp.abs(velocity_x) * time_step
    forward = beam_warming(state_now, padded[..., 1 : x_cells + 1], padded[..., 0:x_cells], courant)
    backward = beam_warming(
        state_now, padded[..., 3 : x_cells + 3], padded[..., 4 : x_cells + 4], courant
    )
    return jnp.where(velocity_x > 0, forward, backward)


def sweep_y(padded, velocity_y):
    row_count = padded.shape[-2] - 4
    centre = padded[..., 2 : row_count + 2, :]
    courant = jnp.abs(velocity_y) * time_step
    forward = beam_warming(
        centre, padded[..., 1 : row_count + 1, :], padded[..., 0:row_count, :], courant
    )
    backward = beam_warming(
        centre, padded[..., 3 : row_count + 3, :], padded[..., 4 : row_count + 4, :], courant
    )
    return jnp.where(velocity_y > 0, forward, backward)


def drift_of(first_sums):
    fluid_concentration = first_sums[0]
    return (
        fluid_concentration,
        first_sums[1] / fluid_concentration,
        first_sums[2] / fluid_concentration,
        first_sums[3] / fluid_concentration,
    )


def second_terms(values, grid_x, grid_y, grid_z, drift_x, drift_y, drift_z):
    random_motion_first = grid_x - drift_x[None]
    random_motion_second = grid_y - drift_y[None]
    random_motion_third = grid_z - drift_z[None]
    magnitude_square_norm = (
        random_motion_first * random_motion_first
        + random_motion_second * random_motion_second
        + random_motion_third * random_motion_third
    )
    weighted = dv_step**3 * values * magnitude_square_norm
    return jnp.stack(
        [
            jnp.sum(weighted, 0) / 3.0,
            0.5 * jnp.sum(random_motion_first * weighted, 0),
            0.5 * jnp.sum(random_motion_second * weighted, 0),
            0.5 * jnp.sum(random_motion_third * weighted, 0),
        ]
    )


def relax(values, grid_x, grid_y, grid_z, fluid_concentration, drift_x, drift_y, drift_z, second):
    isotropic_stress = second[0]
    cell_kinetic_warmth = isotropic_stress / fluid_concentration
    random_motion_first = grid_x - drift_x[None]
    random_motion_second = grid_y - drift_y[None]
    random_motion_third = grid_z - drift_z[None]
    magnitude_square_norm = (
        random_motion_first * random_motion_first
        + random_motion_second * random_motion_second
        + random_motion_third * random_motion_third
    )
    target_distribution = gaussian_distribution(
        fluid_concentration[None],
        cell_kinetic_warmth[None],
        random_motion_first,
        random_motion_second,
        random_motion_third,
    )
    energy_current_projection = (
        random_motion_first * second[1][None]
        + random_motion_second * second[2][None]
        + random_motion_third * second[3][None]
    )
    skewness_adjustment = target_distribution * (
        1.0
        + (1.0 - diffusivity_ratio)
        * energy_current_projection
        / (5.0 * isotropic_stress * cell_kinetic_warmth)[None]
        * (magnitude_square_norm / cell_kinetic_warmth[None] - 5.0)
    )
    relaxation_rate = isotropic_stress / (
        baseline_shear_coefficient
        * jnp.power(cell_kinetic_warmth / baseline_warmth, shear_power_index)
    )
    damping = jnp.exp(-relaxation_rate * time_step)
    return skewness_adjustment + (values - skewness_adjustment) * damping[None]


def moment_table(grid_x, grid_y, grid_z):
    weights = jnp.full(grid_x.shape, dv_step**3, jnp.float32)
    return jnp.stack([weights, weights * grid_x, weights * grid_y, weights * grid_z])


def shards(distribution, body_mask, inflow_flags):
    vel_local = distribution.shape[0]
    row_count = distribution.shape[2]
    cell_count = distribution.shape[1] * row_count * distribution.shape[3]
    local_x, local_y, local_z = velocity_grid(NV1, lax.axis_index("vel") * vel_local, vel_local)
    inflow = gaussian_distribution(free_density, free_temp, local_x - free_speed, local_y, local_z)[
        :, None, None, None
    ]
    wall = gaussian_distribution(wall_density, wall_temp, local_x, local_y, local_z)[:, None]
    full_x, full_y, full_z = velocity_grid(NV1, 0, NV1**3)
    full_table = moment_table(full_x, full_y, full_z)
    speed_x = local_x[:, None, None, None]
    speed_y = local_y[:, None, None, None]
    row_start = lax.axis_index("gy") * row_count
    flags_own = lax.dynamic_slice_in_dim(inflow_flags, row_start, row_count, 1)
    solid = body_mask.reshape(1, cell_count) > 0
    state_now = distribution
    for step_index in range(STEPS):
        swept = sweep_x(state_now, speed_x, inflow, flags_own)
        swept = with_halo(swept, (("gy", 2),), 2)
        moved = sweep_y(swept, speed_y).reshape(vel_local, cell_count)
        gathered = lax.all_to_all(moved, "vel", split_axis=1, concat_axis=0, tiled=True)
        fluid_concentration, drift_x, drift_y, drift_z = drift_of(
            jnp.dot(full_table, gathered, precision=lax.Precision.HIGHEST)
        )
        cols_x, cols_y, cols_z = (full_x[:, None], full_y[:, None], full_z[:, None])
        second = second_terms(gathered, cols_x, cols_y, cols_z, drift_x, drift_y, drift_z)
        relaxed = relax(
            gathered, cols_x, cols_y, cols_z, fluid_concentration, drift_x, drift_y, drift_z, second
        )
        relaxed = lax.all_to_all(relaxed, "vel", split_axis=0, concat_axis=1, tiled=True)
        state_now = jnp.where(solid, wall, relaxed).reshape(distribution.shape)
    return state_now


def solution(mesh):
    placed = (P("vel", None, "gy", None), P(None, "gy", None), P())
    return jax.shard_map(
        shards, mesh=mesh, in_specs=placed, out_specs=P("vel", None, "gy", None), check_vma=False
    )
```

profile of v0, /device:TPU:24, one launch (start us, length us, event | category | flops | bytes accessed | tf_op | source)
XLA Modules:
  0.0 245.5 jit_solution(287960046469006245)
XLA Ops:
  0.1 1.9 copy.22
  2.0 0.1 dynamic-slice_compare_fusion
  2.1 0.1 broadcast_select_fusion.3
  2.1 1.2 copy-done
  3.3 6.3 %add_select_fusion.3 = f32[432,2,4,128]{0,3,2,1:T(8,128)S(1)} fusion(f32[432,2,4,128]{0,3,2,1:T(8,128)} %copy-done, f32[432,2,4,1]{0,3,2,1:T(1,128)S(1)} %get-tuple-element.24, f32[432,2,4,1]{0,3,2,1:T(1,128)S(1)} %get-tuple-element.23, f32[432]{0:T(512)S(1)} %get-tuple-element.39, f32[432]{0:T(512)S(1)} %abs_multiply_fusion.1, ...), kind=kLoop, calls=%fused_computation.89 | loop fusion | flops 12386304 | bytes 3570480 | tf_op jit(solution)/shard_map/jit(_where)/select_n | solution.py:88
  9.6 1.2 fusion.93
  10.8 2.5 %copy.29 = f32[432,2,2,128]{3,0,2,1:T(8,128)} copy(f32[432,2,2,128]{0,3,2,1:T(8,128)} %get-tuple-element.21) | data formatting | bytes 1769472 | tf_op jit(solution)/shard_map/slice | solution.py:27
  13.3 1.9 collective-permute-start
  15.2 1.2 copy.31
  16.5 3.9 %collective-permute-start.1 = (f32[432,2,2,128]{3,0,2,1:T(8,128)}, f32[432,2,2,128]{3,0,2,1:T(8,128)}, u32[]{:S(2)}, u32[]{:S(2)}) collective-permute-start(f32[432,2,2,128]{3,0,2,1:T(8,128)} %copy.31), channel_id=1, source_target_pairs={{1,0},{2,1},{3,2},{4,3},{5,4},{6,5},{7,6},{0,7},{9,8},{10,9},{11,1... | collective-permute-start | bytes 2654216 | tf_op jit(solution)/shard_map/ppermute | solution.py:32
  20.5 0.1 fusion.68
  20.6 18.5 %collective-permute-done = f32[432,2,2,128]{3,0,2,1:T(8,128)} collective-permute-done((f32[432,2,2,128]{3,0,2,1:T(8,128)}, f32[432,2,2,128]{3,0,2,1:T(8,128)}, u32[]{:S(2)}, u32[]{:S(2)}) %collective-permute-start) | collective-permute-done | bytes 884768 | tf_op jit(solution)/shard_map/ppermute | solution.py:30
  39.1 1.5 copy.30
  40.6 2.5 %copy.32 = f32[432,2,2,128]{0,3,2,1:T(8,128)} copy(f32[432,2,2,128]{3,0,2,1:T(8,128)} %collective-permute-done.1) | data formatting | bytes 1769472 | tf_op jit(solution)/shard_map/ppermute | solution.py:32
  43.1 4.0 %add_select_fusion.2 = f32[432,2,4,128]{0,3,2,1:T(8,128)} fusion(f32[432,2,4,128]{0,3,2,1:T(8,128)S(1)} %add_select_fusion.3, f32[432,2,2,128]{0,3,2,1:T(8,128)} %copy.32, f32[432,2,2,128]{0,3,2,1:T(8,128)S(1)} %copy.30, f32[432]{0:T(512)S(1)} %get-tuple-element.37, f32[432]{0:T(512)S(1)} %get-tuple-element.38, pred[432]{0:T(512)(128)(4,1)S(1)} %broadcast_compare_fusion.2), kind=kLoop, calls=%fused_computation.88 | loop fusion | flops 11501568 | bytes 5312304 | tf_op jit(solution)/shard_map/jit(_where)/select_n | solution.py:101
  47.1 7.4 %all-to-all-start = ((f32[432,32,32]{0,2,1:T(8,128)}), f32[432,32,32]{0,2,1:T(8,128)S(1)}, u32[]{:S(2)}, u32[]{:S(2)}) async-start(f32[432,32,32]{0,2,1:T(8,128)} %bitcast.75), calls=%async_computation | async-start | bytes 4194304 | tf_op jit(solution)/shard_map/all_to_all | solution.py:198
  54.5 0.1 fusion.53
  54.6 0.1 fusion.46
  54.7 0.5 fusion.62
  55.2 26.4 %all-to-all-done = f32[432,32,32]{0,2,1:T(8,128)S(1)} async-done(((f32[432,32,32]{0,2,1:T(8,128)}), f32[432,32,32]{0,2,1:T(8,128)S(1)}, u32[]{:S(2)}, u32[]{:S(2)}) %all-to-all-start) | async-done | bytes 1769504 | tf_op jit(solution)/shard_map/all_to_all | solution.py:198
  81.6 2.6 %copy.33 = f32[32,432,32]{1,0,2:T(8,128)} copy(f32[32,432,32]{1,2,0:T(8,128)S(1)} %bitcast.71) | data formatting | bytes 3538944 | tf_op jit(solution)/shard_map/all_to_all | solution.py:198
  84.1 3.5 %all_to_all.55 = f32[13824,32]{0,1:T(8,128)} reshape(f32[32,432,32]{1,0,2:T(8,128)} %copy.33) | data formatting | bytes 3538944 | tf_op jit(solution)/shard_map/all_to_all | solution.py:198
  87.6 3.0 %fusion.91 = f32[4,32]{1,0:T(4,128)S(1)} fusion(f32[13824,32]{0,1:T(8,128)} %all_to_all.55, f32[1,13824]{1,0:T(1,128)S(1)} %get-tuple-element.42, f32[1,13824]{1,0:T(1,128)S(1)} %get-tuple-element.41, f32[1,13824]{1,0:T(1,128)S(1)} %fusion.68, f32[4]{0:T(128)S(1)} %pad.28.clone), kind=kOutput, calls=%fused_computation.200 | convolution fusion | flops 21399552 | bytes 1935888 | tf_op jit(solution)/shard_map/dot_general | solution.py:200
  90.6 1.9 fusion.8
  92.6 3.1 %multiply_add_fusion.1 = f32[32,432,32]{1,2,0:T(8,128)} fusion(f32[32]{0:T(128)S(1)} %get-tuple-element.34, f32[32]{0:T(128)S(1)} %bitcast.78, f32[32]{0:T(128)S(1)} %get-tuple-element.33, f32[32]{0:T(128)S(1)} %broadcast_multiply_fusion.3, f32[32]{0:T(128)S(1)} %broadcast_multiply_fusion.4, f32[32]{0:T(128)S(1)} %broadcast_multiply_fusion.5, ...), kind=kLoop, calls=%fused_computation.87 | loop fusion | flops 11501568 | bytes 3706240 | tf_op jit(solution)/shard_map/add | solution.py:169
  95.7 7.1 %all-to-all-start.1 = ((f32[32,432,32]{1,2,0:T(8,128)}), f32[32,432,32]{1,2,0:T(8,128)S(1)}, u32[]{:S(2)}, u32[]{:S(2)}) async-start(f32[32,432,32]{1,2,0:T(8,128)} %multiply_add_fusion.1), calls=%async_computation.1 | async-start | bytes 4194304 | tf_op jit(solution)/shard_map/all_to_all | solution.py:207
  102.9 27.0 %all-to-all-done.1 = f32[32,432,32]{1,2,0:T(8,128)S(1)} async-done(((f32[32,432,32]{1,2,0:T(8,128)}), f32[32,432,32]{1,2,0:T(8,128)S(1)}, u32[]{:S(2)}, u32[]{:S(2)}) %all-to-all-start.1) | async-done | bytes 1769504 | tf_op jit(solution)/shard_map/all_to_all | solution.py:207
  129.9 0.2 broadcast_select_fusion.1
  130.1 0.1 broadcast_select_fusion.2
  130.2 2.6 %add_select_fusion.1 = f32[432,2,4,128]{0,3,2,1:T(8,128)S(1)} fusion(f32[432,2,4,128]{0,3,2,1:T(8,128)S(1)} %broadcast_select_fusion.1, f32[432,2,4,1]{0,3,2,1:T(1,128)S(1)} %get-tuple-element.20, f32[432,2,4,1]{0,3,2,1:T(1,128)S(1)} %get-tuple-element.19, f32[432]{0:T(512)S(1)} %get-tuple-element.39, f32[432]{0:T(512)S(1)} %abs_multiply_fusion.1, ...), kind=kLoop, calls=%fused_computation.86 | loop fusion | flops 12386304 | bytes 3570480 | tf_op jit(solution)/shard_map/jit(_where)/select_n | solution.py:88
  132.8 1.2 fusion.92
  134.0 2.5 %copy.34 = f32[432,2,2,128]{3,0,2,1:T(8,128)} copy(f32[432,2,2,128]{0,3,2,1:T(8,128)} %get-tuple-element.17) | data formatting | bytes 1769472 | tf_op jit(solution)/shard_map/slice | solution.py:27
  136.5 1.2 copy.36
  137.8 3.2 %collective-permute-start.3 = (f32[432,2,2,128]{3,0,2,1:T(8,128)}, f32[432,2,2,128]{3,0,2,1:T(8,128)}, u32[]{:S(2)}, u32[]{:S(2)}) collective-permute-start(f32[432,2,2,128]{3,0,2,1:T(8,128)} %copy.36), channel_id=1, source_target_pairs={{1,0},{2,1},{3,2},{4,3},{5,4},{6,5},{7,6},{0,7},{9,8},{10,9},{11,1... | collective-permute-start | bytes 2654216 | tf_op jit(solution)/shard_map/ppermute | solution.py:32
  141.0 17.6 %collective-permute-done.2 = f32[432,2,2,128]{3,0,2,1:T(8,128)} collective-permute-done((f32[432,2,2,128]{3,0,2,1:T(8,128)}, f32[432,2,2,128]{3,0,2,1:T(8,128)}, u32[]{:S(2)}, u32[]{:S(2)}) %collective-permute-start.2) | collective-permute-done | bytes 884768 | tf_op jit(solution)/shard_map/ppermute | solution.py:30
  158.6 1.5 copy.35
  160.1 0.0 collective-permute-done.3
  160.1 2.5 %copy.37 = f32[432,2,2,128]{0,3,2,1:T(8,128)} copy(f32[432,2,2,128]{3,0,2,1:T(8,128)} %collective-permute-done.3) | data formatting | bytes 1769472 | tf_op jit(solution)/shard_map/ppermute | solution.py:32
  162.6 3.0 %add_select_fusion = f32[432,2,4,128]{0,3,2,1:T(8,128)S(1)} fusion(f32[432,2,4,128]{0,3,2,1:T(8,128)S(1)} %add_select_fusion.1, f32[432,2,2,128]{0,3,2,1:T(8,128)} %copy.37, f32[432,2,2,128]{0,3,2,1:T(8,128)S(1)} %copy.35, f32[432]{0:T(512)S(1)} %get-tuple-element.37, f32[432]{0:T(512)S(1)} %get-tuple-element.38, pred[432]{0:T(512)(128)(4,1)S(1)} %broadcast_compare_fusion.2), kind=kLoop, calls=%fused_computation.85 | loop fusion | flops 11501568 | bytes 5312304 | tf_op jit(solution)/shard_map/jit(_where)/select_n | solution.py:101
  165.6 33.1 %all_to_all.70 = f32[432,32,32]{0,2,1:T(8,128)S(1)} all-to-all(f32[432,32,32]{0,2,1:T(8,128)S(1)} %bitcast.76), channel_id=1, replica_groups=mesh['vel'=32,'gy'=8] {'vel'}, dimensions={1} | all-to-all | bytes 3538944 | tf_op jit(solution)/shard_map/all_to_all | solution.py:198
  198.6 2.6 %copy.38 = f32[32,432,32]{1,0,2:T(8,128)} copy(f32[32,432,32]{1,2,0:T(8,128)S(1)} %bitcast.72) | data formatting | bytes 3538944 | tf_op jit(solution)/shard_map/all_to_all | solution.py:198
  201.2 3.5 %all_to_all.62 = f32[13824,32]{0,1:T(8,128)} reshape(f32[32,432,32]{1,0,2:T(8,128)} %copy.38) | data formatting | bytes 3538944 | tf_op jit(solution)/shard_map/all_to_all | solution.py:198
  204.7 3.0 %fusion.90 = f32[4,32]{1,0:T(4,128)S(1)} fusion(f32[13824,32]{0,1:T(8,128)} %all_to_all.62, f32[1,13824]{1,0:T(1,128)S(1)} %get-tuple-element.42, f32[1,13824]{1,0:T(1,128)S(1)} %get-tuple-element.41, f32[1,13824]{1,0:T(1,128)S(1)} %fusion.68, f32[4]{0:T(128)S(1)} %copy-done.3), kind=kOutput, calls=%fused_computation.199 | convolution fusion | flops 21399552 | bytes 1935888 | tf_op jit(solution)/shard_map/dot_general | solution.py:200
  207.7 1.9 fusion.27
  209.7 2.0 multiply_add_fusion
  211.7 31.9 %all_to_all.71 = f32[32,432,32]{1,2,0:T(8,128)S(1)} all-to-all(f32[32,432,32]{1,2,0:T(8,128)S(1)} %multiply_add_fusion), channel_id=1, replica_groups=mesh['vel'=32,'gy'=8] {'vel'}, dimensions={0} | all-to-all | bytes 3538944 | tf_op jit(solution)/shard_map/all_to_all | solution.py:207
  243.6 0.2 broadcast_select_fusion
  243.8 1.7 copy.39
  (31 shorter events, 0.3 us)
Async XLA Ops:
  0.0 2.0 copy-start.4
  2.0 1.3 copy-start
  13.3 25.8 %collective-permute-start = (f32[432,2,2,128]{3,0,2,1:T(8,128)}, f32[432,2,2,128]{3,0,2,1:T(8,128)}, u32[]{:S(2)}, u32[]{:S(2)}) collective-permute-start(f32[432,2,2,128]{3,0,2,1:T(8,128)} %copy.29), channel_id=1, source_target_pairs={{0,1},{1,2},{2,3},{3,4},{4,5},{5,6},{6,7},{7,0},{8,9},{9,10},{10,1... | collective-permute-start | bytes 2654216 | tf_op jit(solution)/shard_map/ppermute | solution.py:30
  16.5 24.2 %collective-permute-start.1 = (f32[432,2,2,128]{3,0,2,1:T(8,128)}, f32[432,2,2,128]{3,0,2,1:T(8,128)}, u32[]{:S(2)}, u32[]{:S(2)}) collective-permute-start(f32[432,2,2,128]{3,0,2,1:T(8,128)} %copy.31), channel_id=1, source_target_pairs={{1,0},{2,1},{3,2},{4,3},{5,4},{6,5},{7,6},{0,7},{9,8},{10,9},{11,1... | collective-permute-start | bytes 2654216 | tf_op jit(solution)/shard_map/ppermute | solution.py:32
  47.1 34.4 %all-to-all-start = ((f32[432,32,32]{0,2,1:T(8,128)}), f32[432,32,32]{0,2,1:T(8,128)S(1)}, u32[]{:S(2)}, u32[]{:S(2)}) async-start(f32[432,32,32]{0,2,1:T(8,128)} %bitcast.75), calls=%async_computation | async-start | bytes 4194304 | tf_op jit(solution)/shard_map/all_to_all | solution.py:198
  54.6 33.0 %copy-start.2 = (f32[4]{0:T(128)}, f32[4]{0:T(128)S(1)}, u32[]{:S(2)}) copy-start(f32[4]{0:T(128)S(1)} %pad.28.clone) | copy-start | bytes 52
  95.7 7.2 %copy-start.1 = (s32[2,4,128]{2,1,0:T(4,128)S(1)}, s32[2,4,128]{2,1,0:T(4,128)}, u32[]{:S(2)}) copy-start(s32[2,4,128]{2,1,0:T(4,128)} %param.4) | copy-start | bytes 12292
  95.7 34.2 %all-to-all-start.1 = ((f32[32,432,32]{1,2,0:T(8,128)}), f32[32,432,32]{1,2,0:T(8,128)S(1)}, u32[]{:S(2)}, u32[]{:S(2)}) async-start(f32[32,432,32]{1,2,0:T(8,128)} %multiply_add_fusion.1), calls=%async_computation.1 | async-start | bytes 4194304 | tf_op jit(solution)/shard_map/all_to_all | solution.py:207
  136.5 22.1 %collective-permute-start.2 = (f32[432,2,2,128]{3,0,2,1:T(8,128)}, f32[432,2,2,128]{3,0,2,1:T(8,128)}, u32[]{:S(2)}, u32[]{:S(2)}) collective-permute-start(f32[432,2,2,128]{3,0,2,1:T(8,128)} %copy.34), channel_id=1, source_target_pairs={{0,1},{1,2},{2,3},{3,4},{4,5},{5,6},{6,7},{7,0},{8,9},{9,10},{10,1... | collective-permute-start | bytes 2654216 | tf_op jit(solution)/shard_map/ppermute | solution.py:30
  137.8 22.3 %collective-permute-start.3 = (f32[432,2,2,128]{3,0,2,1:T(8,128)}, f32[432,2,2,128]{3,0,2,1:T(8,128)}, u32[]{:S(2)}, u32[]{:S(2)}) collective-permute-start(f32[432,2,2,128]{3,0,2,1:T(8,128)} %copy.36), channel_id=1, source_target_pairs={{1,0},{2,1},{3,2},{4,3},{5,4},{6,5},{7,6},{0,7},{9,8},{10,9},{11,1... | collective-permute-start | bytes 2654216 | tf_op jit(solution)/shard_map/ppermute | solution.py:32
  201.2 3.5 %copy-start.3 = (f32[4]{0:T(128)S(1)}, f32[4]{0:T(128)}, u32[]{:S(2)}) copy-start(f32[4]{0:T(128)} %copy-done.2) | copy-start | bytes 52
where the time goes:
time: 250 us; the launch traced here: 246 us
  waiting for transfers between devices  89.5 us (36%)
  blocking collectives  65 us (26%)
  local copies, waits for them, and re-layouts  34.8 us (14%)
  other arithmetic  26.4 us (11%)
  starting transfers between devices  23.6 us (9%)
  matrix products  6.04 us (2%)
    ppermute x2, waiting for transfers between devices, with_halo(): lax.ppermute(tail, axis, [(i, (i + 1) % count) for i in range(count)])  36.1 us
    all_to_all x1, blocking collectives, shards(): lax.all_to_all(moved, 'vel', split_axis=1, concat_axis=0, tiled=True)  33.1 us
    all_to_all x1, blocking collectives, shards(): lax.all_to_all(relaxed, 'vel', split_axis=0, concat_axis=1, tiled=True)  31.9 us
    all_to_all x1, waiting for transfers between devices, shards(): lax.all_to_all(relaxed, 'vel', split_axis=0, concat_axis=1, tiled=True)  27 us
    all_to_all x1, waiting for transfers between devices, shards(): lax.all_to_all(moved, 'vel', split_axis=1, concat_axis=0, tiled=True)  26.4 us
    all_to_all x4, local copies, waits for them, and re-layouts, shards(): lax.all_to_all(moved, 'vel', split_axis=1, concat_axis=0, tiled=True)  12.1 us
    select_n x2, other arithmetic, sweep_x(): return jnp.where(velocity_x > 0, forward, backward)  8.83 us
    slice x4, local copies, waits for them, and re-layouts, with_halo(): lax.slice_in_dim(cells, cells.shape[dim] - width, cells.shape[dim], axis=...  7.46 us
  transfers between devices with their start and end apart: 6, of which 4 were waited for; matrix products, arithmetic and copies ran while one was open for 3% of the time, Pallas kernels for 0%

commit v1 on v0

v1 whole, which is shorter than its diff:
```python
import math

import jax
import jax.numpy as jnp
from jax import lax
from jax.experimental import pallas as pl
from jax.experimental.pallas import tpu as pltpu
from jax.sharding import PartitionSpec as P

NV1 = 24
NB = 18
HALF = NV1 // 2
NMOM = 13
STEP = 0.6
DT = 0.25
WEIGHT = STEP**3
CENTRE = 0.5 * (NV1 - 1)
ZS = [(c - CENTRE) * STEP for c in range(NV1)]
INFLOW_Z = [math.exp(-0.5 * z * z) for z in ZS]
INFLOW_SUMS = [sum(z**k * g for z, g in zip(ZS, INFLOW_Z)) for k in range(4)]
INFLOW_SCALE = 200.0 / (2.0 * math.pi) ** 1.5
SHAPE = (8, 128)
F32 = jnp.float32


def iotas():
    rows = lax.rem(lax.broadcasted_iota(jnp.int32, SHAPE, 0), 4)
    lanes = lax.broadcasted_iota(jnp.int32, SHAPE, 1)
    return rows, lanes


def flag_tile(flags_ref, gy):
    subs = lax.broadcasted_iota(jnp.int32, SHAPE, 0)
    tile = jnp.zeros(SHAPE, jnp.int32)
    for plane in range(2):
        for row in range(4):
            tile = jnp.where(subs == plane * 4 + row, flags_ref[plane, gy * 4 + row], tile)
    return tile


def weights_of(speed):
    k = jnp.abs(speed) * DT
    return 1.0 - 1.5 * k + 0.5 * k * k, 2.0 * k - k * k, 0.5 * k * k - 0.5 * k


def block_speeds(vel, block):
    index = vel * NB + block
    a = lax.div(index, NV1)
    b = index - a * NV1
    return (a.astype(F32) - CENTRE) * STEP, (b.astype(F32) - CENTRE) * STEP, b


def inflow_block(speed_x, speed_y):
    drift = speed_x - 3.0
    return INFLOW_SCALE * jnp.exp(jnp.full(SHAPE, -0.5 * (drift * drift + speed_y * speed_y), F32))


def sweep(values, ghost, coef, shift, edge, inflow_edge):
    one = pltpu.roll(values, shift, 1)
    one = jnp.where(inflow_edge, ghost, jnp.where(edge, values, one))
    two = jnp.where(edge, one, pltpu.roll(one, shift, 1))
    return coef[0] * values + coef[1] * one + coef[2] * two


def side_masks(rows, up):
    far = jnp.where(up, 3, 0)
    near = jnp.where(up, 0, 3)
    first = rows == far
    last = rows == near
    low = rows < 2
    tail = low != up
    return first, tail, last, jnp.logical_not(tail)


def add_moments(sums_ref, base, z, speed_x, speed_y):
    sq = speed_x * speed_x + speed_y * speed_y
    x0 = speed_x * z[0]
    y0 = speed_y * z[0]
    terms = [
        z[0], x0, y0, z[1],
        speed_x * x0, speed_y * y0, z[2],
        speed_x * y0, speed_x * z[1], speed_y * z[1],
        sq * x0 + speed_x * z[2], sq * y0 + speed_y * z[2], sq * z[1] + z[3],
    ]
    for m, term in enumerate(terms):
        sums_ref[base + m] = sums_ref[base + m] + term


def block_moments(sums_ref, z, speed_x, speed_y, inflow, coef_x, shift_x, edge, inflow_edge, up, rows):
    first, tail, last, head = side_masks(rows, up)
    c0, c1, c2 = weights_of(speed_y)
    zero = jnp.zeros(SHAPE, F32)
    c1v = jnp.full(SHAPE, c1, F32)
    c2v = jnp.full(SHAPE, c2, F32)
    own1, cross1 = jnp.where(last, zero, c1v), jnp.where(last, c1v, zero)
    own2, cross2 = jnp.where(head, zero, c2v), jnp.where(head, c2v, zero)
    s1 = jnp.where(up, 1, 7)
    s2 = jnp.where(up, 2, 6)
    own, cross = [], []
    for k in range(4):
        swept = sweep(z[k], INFLOW_SUMS[k] * inflow, coef_x, shift_x, edge, inflow_edge)
        r1 = pltpu.roll(swept, s1, 0)
        r2 = pltpu.roll(swept, s2, 0)
        own.append(c0 * swept + own1 * r1 + own2 * r2)
        cross.append(cross1 * r1 + cross2 * r2)
    add_moments(sums_ref, 0, own, speed_x, speed_y)
    add_moments(sums_ref, NMOM, cross, speed_x, speed_y)


def swap_planes(sums_ref):
    for m in range(NMOM, 2 * NMOM):
        sums_ref[m] = pltpu.roll(sums_ref[m], 4, 0)


def z_sums(z, low, high, c):
    s = low + high
    d = high - low
    speed = ZS[NV1 - 1 - c]
    z0, z1, z2, z3 = z
    return [z0 + s, z1 + speed * d, z2 + speed**2 * s, z3 + speed**3 * d]


def pack(low, high, tail, s2b):
    return jnp.where(tail, pltpu.roll(low, 4, 0), pltpu.roll(high, s2b, 0))


def first_kernel(flags_ref, f_hbm, sums_ref, halo_ref, f_ref, sems):
    for j in range(NB):
        pltpu.make_async_copy(f_hbm.at[pl.ds(NV1 * j, NV1)], f_ref.at[pl.ds(NV1 * j, NV1)], sems.at[j]).start()
    vel, gy = lax.axis_index("vel"), lax.axis_index("gy")
    rows, lanes = iotas()
    right = vel >= 16
    shift_x = jnp.where(right, 1, 127)
    edge = lanes == jnp.where(right, 0, 127)
    own_flags = jnp.where(right, flag_tile(flags_ref, gy), 0)
    inflow_edge = jnp.logical_and(edge, own_flags > 0)
    for m in range(2 * NMOM):
        sums_ref[m] = jnp.zeros(SHAPE, F32)

    def body(j, carry):
        speed_x, speed_y, b = block_speeds(vel, j)
        up = b >= HALF
        first, tail, last, head = side_masks(rows, up)
        s2b = jnp.where(up, 6, 2)
        pltpu.make_async_copy(f_hbm.at[pl.ds(NV1 * j, NV1)], f_ref.at[pl.ds(NV1 * j, NV1)], sems.at[j]).wait()
        z = [jnp.zeros(SHAPE, F32)] * 4
        for c in range(HALF):
            low = f_ref[NV1 * j + c]
            high = f_ref[NV1 * j + (NV1 - 1 - c)]
            z = z_sums(z, low, high, c)
            halo_ref[HALF * j + c] = pack(low, high, tail, s2b)
        z = [WEIGHT * v for v in z]
        inflow = WEIGHT * inflow_block(speed_x, speed_y)
        block_moments(sums_ref, z, speed_x, speed_y, inflow, weights_of(speed_x), shift_x, edge, inflow_edge, up, rows)
        return carry

    lax.fori_loop(0, NB, body, 0)
    swap_planes(sums_ref)


def cell_values(mom, solid):
    n = mom[0]
    inv = 1.0 / n
    ux, uy, uz = mom[1] * inv, mom[2] * inv, mom[3] * inv
    xx, yy, zz, xy, xz, yz = mom[4:10]
    energy = xx + yy + zz
    usq = ux * ux + uy * uy + uz * uz
    p = (energy - n * usq) * (1.0 / 3.0)
    common = 2.0 * n * usq - energy
    qx = 0.5 * (mom[10] - 2.0 * (xx * ux + xy * uy + xz * uz) + common * ux)
    qy = 0.5 * (mom[11] - 2.0 * (xy * ux + yy * uy + yz * uz) + common * uy)
    qz = 0.5 * (mom[12] - 2.0 * (xz * ux + yz * uy + zz * uz) + common * uz)
    temp = p * inv
    rate = p / (3000.0 * jnp.exp(0.81 * jnp.log(temp * (1.0 / 3.0))))
    damp = jnp.exp(-DT * rate)
    skew = (1.0 / 15.0) / (p * temp)
    zero = jnp.zeros(SHAPE, F32)
    n = jnp.where(solid, 200.0, n)
    temp = jnp.where(solid, 1.5, temp)
    damp = jnp.where(solid, zero, damp)
    skew = jnp.where(solid, zero, skew)
    ux, uy, uz = (jnp.where(solid, zero, u) for u in (ux, uy, uz))
    wide = 2.0 * math.pi * temp
    scale = n / (wide * jnp.sqrt(wide)) * (1.0 - damp)
    return scale, ux, uy, uz, 1.0 / temp, skew * qx, skew * qy, skew * qz, damp


def step_kernel(last_step, flags_ref, mask_ref, mom_ref, f_hbm, halo_hbm, *refs):
    if last_step:
        out_hbm, f_ref, in_ref, o_ref, z_ref, sems, hsems, osems = refs
    else:
        out_hbm, sums_ref, halo_out, f_ref, in_ref, o_ref, z_ref, sems, hsems, osems = refs

    def f_copy(j):
        return pltpu.make_async_copy(f_hbm.at[pl.ds(NV1 * j, NV1)], f_ref.at[pl.ds(NV1 * j, NV1)], sems.at[j])

    def h_copy(j):
        return pltpu.make_async_copy(halo_hbm.at[pl.ds(HALF * j, HALF)], in_ref.at[pl.ds(HALF * j, HALF)], hsems.at[j])

    def o_copy(j):
        return pltpu.make_async_copy(o_ref.at[pl.ds(NV1 * j, NV1)], out_hbm.at[pl.ds(NV1 * j, NV1)], osems.at[j])

    for j in range(NB):
        f_copy(j).start()
        h_copy(j).start()
    vel, gy = lax.axis_index("vel"), lax.axis_index("gy")
    rows, lanes = iotas()
    right = vel >= 16
    shift_x = jnp.where(right, 1, 127)
    edge = lanes == jnp.where(right, 0, 127)
    own_flags = jnp.where(right, flag_tile(flags_ref, gy), 0)
    low_flags = jnp.where(right, flag_tile(flags_ref, lax.rem(gy + 7, 8)), 0)
    high_flags = jnp.where(right, flag_tile(flags_ref, lax.rem(gy + 1, 8)), 0)
    inflow_edge = jnp.logical_and(edge, own_flags > 0)
    solid = mask_ref[...] > 0
    scale, ux, uy, uz, inv_t, qx, qy, qz, damp = cell_values([mom_ref[m] for m in range(NMOM)], solid)
    half_inv = -0.5 * inv_t
    for c in range(NV1):
        cz = ZS[c] - uz
        sq = cz * cz
        z_ref[c] = jnp.exp(sq * half_inv)
        z_ref[NV1 + c] = cz * qz
        z_ref[2 * NV1 + c] = sq * inv_t
    if not last_step:
        for m in range(2 * NMOM):
            sums_ref[m] = jnp.zeros(SHAPE, F32)

    def body(j, carry):
        speed_x, speed_y, b = block_speeds(vel, j)
        up = b >= HALF
        first, tail, last, head = side_masks(rows, up)
        s1 = jnp.where(up, 1, 7)
        s2 = jnp.where(up, 2, 6)
        s1b = jnp.where(up, 7, 1)
        s2b = jnp.where(up, 6, 2)
        flags = jnp.where(up, low_flags, high_flags)
        halo_flags = jnp.where(tail, pltpu.roll(flags, 4, 0), pltpu.roll(flags, s2b, 0))
        halo_edge = jnp.logical_and(edge, halo_flags > 0)
        coef_x = weights_of(speed_x)
        y0, y1, y2 = weights_of(speed_y)
        d0, d1, d2 = damp * y0, damp * y1, damp * y2
        cx, cy = speed_x - ux, speed_y - uy
        sq = cx * cx + cy * cy
        e_xy = scale * jnp.exp(sq * half_inv)
        q_xy = cx * qx + cy * qy
        s_xy = sq * inv_t - 5.0
        inflow = inflow_block(speed_x, speed_y)
        f_copy(j).wait()
        h_copy(j).wait()

        def relax(c, swept, one, two):
            target = e_xy * z_ref[c]
            shape = (q_xy + z_ref[NV1 + c]) * (s_xy + z_ref[2 * NV1 + c])
            return d0 * swept + d1 * one + d2 * two + (target + target * shape)

        z = [jnp.zeros(SHAPE, F32)] * 4
        for c in range(HALF):
            h = NV1 - 1 - c
            ghost = INFLOW_Z[c] * inflow
            low = sweep(f_ref[NV1 * j + c], ghost, coef_x, shift_x, edge, inflow_edge)
            high = sweep(f_ref[NV1 * j + h], ghost, coef_x, shift_x, edge, inflow_edge)
            halo = sweep(in_ref[HALF * j + c], ghost, coef_x, shift_x, edge, halo_edge)
            low1 = pltpu.roll(jnp.where(first, halo, low), s1, 0)
            low2 = pltpu.roll(jnp.where(tail, halo, low), s2, 0)
            high1 = jnp.where(last, pltpu.roll(halo, s1b, 0), pltpu.roll(high, s1, 0))
            high2 = jnp.where(head, halo, pltpu.roll(high, s2, 0))
            low = relax(c, low, low1, low2)
            high = relax(h, high, high1, high2)
            o_ref[NV1 * j + c] = low
            o_ref[NV1 * j + h] = high
            if not last_step:
                z = z_sums(z, low, high, c)
                halo_out[HALF * j + c] = pack(low, high, tail, s2b)
        o_copy(j).start()
        if not last_step:
            z = [WEIGHT * v for v in z]
            block_moments(
                sums_ref, z, speed_x, speed_y, WEIGHT * inflow, coef_x, shift_x, edge, inflow_edge, up, rows
            )
        return carry

    lax.fori_loop(0, NB, body, 0)
    if not last_step:
        swap_planes(sums_ref)
    for j in range(NB):
        o_copy(j).wait()


def any_spec():
    return pl.BlockSpec(memory_space=pl.ANY)


def smem_spec():
    return pl.BlockSpec(memory_space=pltpu.SMEM)


def vmem_spec():
    return pl.BlockSpec(memory_space=pltpu.VMEM)


SUMS = jax.ShapeDtypeStruct((2 * NMOM, 8, 128), F32)
HALO = jax.ShapeDtypeStruct((NB * HALF, 8, 128), F32)
STATE = jax.ShapeDtypeStruct((NB * NV1, 8, 128), F32)
DMAS = pltpu.SemaphoreType.DMA((NB,))


def first_call(flags, f):
    return pl.pallas_call(
        first_kernel,
        out_shape=(SUMS, HALO),
        in_specs=[smem_spec(), any_spec()],
        out_specs=(vmem_spec(), vmem_spec()),
        scratch_shapes=[pltpu.VMEM(STATE.shape, F32), DMAS],
        name="first",
    )(flags, f)


def step_call(last_step, flags, mask, mom, f, halo):
    def kernel(*refs):
        step_kernel(last_step, *refs)

    scratch = [
        pltpu.VMEM(STATE.shape, F32),
        pltpu.VMEM(HALO.shape, F32),
        pltpu.VMEM(STATE.shape, F32),
        pltpu.VMEM((3 * NV1, 8, 128), F32),
        DMAS,
        DMAS,
        DMAS,
    ]
    return pl.pallas_call(
        kernel,
        out_shape=(STATE,) if last_step else (STATE, SUMS, HALO),
        in_specs=[smem_spec(), vmem_spec(), vmem_spec(), any_spec(), any_spec()],
        out_specs=(any_spec(),) if last_step else (any_spec(), vmem_spec(), vmem_spec()),
        scratch_shapes=scratch,
        name="last" if last_step else "middle",
    )(flags, mask, mom, f, halo)


def upwind(vel, group):
    return 1 if (NB * vel + 6 * group) % NV1 >= HALF else -1


def bulk_halo(halo):
    parts = []
    for group in range(3):
        pairs = [
            (v * 8 + g, v * 8 + (g + upwind(v, group)) % 8) for v in range(32) for g in range(8)
        ]
        parts.append(lax.ppermute(halo[72 * group : 72 * group + 72], ("vel", "gy"), pairs))
    return jnp.concatenate(parts)


def exchange(values, dy, dx, dc):
    pairs = []
    for v in range(32):
        y, x, c = v // 8, v // 2 % 4, v % 2
        pairs.append((v, (y ^ dy) * 8 + (x ^ dx) * 2 + (c ^ dc)))
    return lax.ppermute(values, "vel", pairs)


def total_moments(sums):
    own, cross = sums[:NMOM], sums[NMOM:]
    up = lax.ppermute(cross, "gy", [(g, (g + 1) % 8) for g in range(8)])
    down = lax.ppermute(cross, "gy", [((g + 1) % 8, g) for g in range(8)])
    rows = lax.broadcasted_iota(jnp.int32, (1, 8, 1), 1) % 4
    mom = own + jnp.where(rows < 2, up, down)
    for dy, dx, dc in ((0, 0, 1), (0, 1, 0), (0, 3, 0), (1, 0, 0), (3, 0, 0)):
        mom = mom + exchange(mom, dy, dx, dc)
    return mom


def shards(distribution, body_mask, inflow_flags):
    f = distribution.reshape(NB * NV1, 8, 128)
    mask = body_mask.reshape(8, 128)
    sums, halo = first_call(inflow_flags, f)
    mom = total_moments(sums)
    halo = bulk_halo(halo)
    f, sums, halo = step_call(False, inflow_flags, mask, mom, f, halo)
    mom = total_moments(sums)
    halo = bulk_halo(halo)
    (f,) = step_call(True, inflow_flags, mask, mom, f, halo)
    return f.reshape(distribution.shape)


def solution(mesh):
    placed = (P("vel", None, "gy", None), P(None, "gy", None), P())
    return jax.shard_map(
        shards, mesh=mesh, in_specs=placed, out_specs=P("vel", None, "gy", None), check_vma=False
    )
```

time: 250 us -> 90 us (0.36); the launches traced: 246 us -> 89.7 us
  blocking collectives: 65 us -> 0 us
  waiting for transfers between devices: 89.5 us -> 34.6 us
  local copies, waits for them, and re-layouts: 34.8 us -> 4.16 us
  Pallas kernels: 0 us -> 23.5 us
  other arithmetic: 26.4 us -> 3.44 us
  matrix products: 6.04 us -> 0 us
    all_to_all x2 -> x0, blocking collectives: 65 us -> none  [the longest x1 33.1 us: shards(): lax.all_to_all(moved, 'vel', split_axis=1, concat_axis=0, tiled=True)]
    all_to_all x2 -> x0, waiting for transfers between devices: 53.4 us -> none  [the longest x1 27 us: shards(): lax.all_to_all(relaxed, 'vel', split_axis=0, concat_axis=1, tiled=True)]
    pallas_call x0 -> x3, Pallas kernels: none -> 23.5 us  [the longest x2 17.5 us: step_call(): pl.pallas_call(kernel, out_shape=(STATE,) if last_step else (STATE, SUMS,...]
    select_n x8 -> x0, other arithmetic: 16.4 us -> none  [the longest x2 8.83 us: sweep_x(): return jnp.where(velocity_x > 0, forward, backward)]
    ppermute x4 -> x20, starting transfers between devices: 9.1 us -> 23.7 us  [the longest x6 11.1 us: bulk_halo(): lax.ppermute(halo[72 * group:72 * group + 72], ('vel', 'gy'), pairs)]
    all_to_all x2 -> x0, starting transfers between devices: 14.5 us -> none  [the longest x1 7.36 us: shards(): lax.all_to_all(moved, 'vel', split_axis=1, concat_axis=0, tiled=True)]
    all_to_all x4 -> x0, local copies, waits for them, and re-layouts: 12.1 us -> none  [shards(): lax.all_to_all(moved, 'vel', split_axis=1, concat_axis=0, tiled=True)]
    ppermute x4 -> x0, local copies, waits for them, and re-layouts: 7.94 us -> none  [the longest x2 4.95 us: with_halo(): lax.ppermute(head, axis, [((i + 1) % count, i) for i in range(count)])]
  transfers between devices with their start and end apart: 6 -> 20, of which waited for: 4 -> 10; matrix products, arithmetic and copies ran while one was open for 3% -> 5% of each run, Pallas kernels for 0% -> 0%
where the time goes in v1:
time: 90 us; the launch traced here: 89.7 us
  waiting for transfers between devices  34.6 us (38%)
  starting transfers between devices  23.7 us (26%)
  Pallas kernels  23.5 us (26%)
  local copies, waits for them, and re-layouts  4.16 us (5%)
  other arithmetic  3.44 us (4%)
    ppermute x10, waiting for transfers between devices, exchange(): return lax.ppermute(values, 'vel', pairs)  34.6 us
    pallas_call x2, Pallas kernels, step_call(): pl.pallas_call(kernel, out_shape=(STATE,) if last_step else (STATE, SUMS,...  17.5 us
    ppermute x6, starting transfers between devices, bulk_halo(): lax.ppermute(halo[72 * group:72 * group + 72], ('vel', 'gy'), pairs)  11.1 us
    pallas_call x1, Pallas kernels, first_call(): pl.pallas_call(first_kernel, out_shape=(SUMS, HALO), in_specs=[smem_spec(...  5.93 us
    ppermute x2, starting transfers between devices, total_moments(): down = lax.ppermute(cross, 'gy', [((g + 1) % 8, g) for g in range(8)])  5.86 us
    ppermute x10, starting transfers between devices, exchange(): return lax.ppermute(values, 'vel', pairs)  4.71 us
    slice x2, local copies, waits for them, and re-layouts, bulk_halo(): halo[72 * group:72 * group + 72]  2.39 us
    ppermute x2, starting transfers between devices, total_moments(): up = lax.ppermute(cross, 'gy', [(g, (g + 1) % 8) for g in range(8)])  2.02 us
  transfers between devices with their start and end apart: 20, of which 10 were waited for; matrix products, arithmetic and copies ran while one was open for 5% of the time, Pallas kernels for 0%

profile of v1, /device:TPU:24, one launch (start us, length us, event | category | flops | bytes accessed | tf_op | source)
XLA Modules:
  0.0 89.7 jit_solution(11375728016064622510)
XLA Ops:
  0.0 5.9 %first.1 = (f32[26,8,128]{2,1,0:T(8,128)}, f32[216,8,128]{2,1,0:T(8,128)}) custom-call(s32[2,32]{1,0:T(2,128)} %refs_0_.3, f32[432,8,128]{2,1,0:T(8,128)} %bitcast.3), custom_call_target="tpu_custom_call" | custom-call | tf_op jit(solution)/shard_map/first/pallas_call | solution.py:308
  5.9 0.9 slice.31
  6.8 5.9 %collective-permute-start.1 = (f32[13,8,128]{2,1,0:T(8,128)S(1)}, f32[13,8,128]{2,1,0:T(8,128)S(1)}, u32[]{:S(2)}, u32[]{:S(2)}) collective-permute-start(f32[13,8,128]{2,1,0:T(8,128)S(1)} %slice.31), channel_id=1, source_target_pairs={{1,0},{2,1},{3,2},{4,3},{5,4},{6,5},{7,6},{0,7},{9,8},{10,9},{11,1... | collective-permute-start | bytes 159752 | tf_op jit(solution)/shard_map/ppermute | solution.py:366
  12.7 1.2 %fusion.2 = (f32[72,8,128]{2,1,0:T(8,128)S(1)}, f32[72,8,128]{2,1,0:T(8,128)S(1)}, f32[72,8,128]{2,1,0:T(8,128)S(1)}) fusion(f32[216,8,128]{2,1,0:T(8,128)} %get-tuple-element.11), kind=kLoop, calls=%fused_computation.7 | loop fusion | bytes 1769472 | tf_op jit(solution)/shard_map/slice | solution.py:351
  13.9 3.3 %collective-permute-start.7 = (f32[72,8,128]{2,1,0:T(8,128)S(1)}, f32[72,8,128]{2,1,0:T(8,128)S(1)}, u32[]{:S(2)}, u32[]{:S(2)}) collective-permute-start(f32[72,8,128]{2,1,0:T(8,128)S(1)} %get-tuple-element.18), channel_id=1, source_target_pairs={{0,7},{1,0},{2,1},{3,2},{4,3},{5,4},{6,5},{7,6},{8,9},{9,10},{10,1... | collective-permute-start | bytes 884744 | tf_op jit(solution)/shard_map/ppermute | solution.py:351
  17.2 0.0 collective-permute-start.9
  17.2 3.2 %collective-permute-start.8 = (f32[72,8,128]{2,1,0:T(8,128)S(1)}, f32[72,8,128]{2,1,0:T(8,128)S(1)}, u32[]{:S(2)}, u32[]{:S(2)}) collective-permute-start(f32[72,8,128]{2,1,0:T(8,128)S(1)} %get-tuple-element.20), channel_id=1, source_target_pairs={{0,7},{1,0},{2,1},{3,2},{4,3},{5,4},{6,5},{7,6},{8,15},{9,8},{10,9... | collective-permute-start | bytes 884744 | tf_op jit(solution)/shard_map/ppermute | solution.py:351
  20.4 0.0 collective-permute-done.1
  20.5 0.1 select_add_fusion.1
  20.5 0.0 collective-permute-start.2
  20.6 1.2 %collective-permute-done.2 = f32[13,8,128]{2,1,0:T(8,128)S(1)} collective-permute-done((f32[13,8,128]{2,1,0:T(8,128)S(1)}, f32[13,8,128]{2,1,0:T(8,128)S(1)}, u32[]{:S(2)}, u32[]{:S(2)}) %collective-permute-start.2) | collective-permute-done | bytes 53280 | tf_op jit(solution)/shard_map/ppermute | solution.py:360
  21.8 0.1 collective-permute-start.3
  21.9 4.1 %collective-permute-done.3 = f32[13,8,128]{2,1,0:T(8,128)S(1)} collective-permute-done((f32[13,8,128]{2,1,0:T(8,128)S(1)}, f32[13,8,128]{2,1,0:T(8,128)S(1)}, u32[]{:S(2)}, u32[]{:S(2)}) %collective-permute-start.3) | collective-permute-done | bytes 53280 | tf_op jit(solution)/shard_map/ppermute | solution.py:360
  26.0 1.7 %collective-permute-start.4 = (f32[13,8,128]{2,1,0:T(8,128)S(1)}, f32[13,8,128]{2,1,0:T(8,128)S(1)}, u32[]{:S(2)}, u32[]{:S(2)}) collective-permute-start(f32[13,8,128]{2,1,0:T(8,128)S(1)} %add.54), channel_id=1, source_target_pairs={{0,48},{8,56},{16,32},{24,40},{32,16},{40,24},{48,0},{56,8},{64,11... | collective-permute-start | bytes 159752 | tf_op jit(solution)/shard_map/ppermute | solution.py:360
  27.7 3.8 %collective-permute-done.4 = f32[13,8,128]{2,1,0:T(8,128)S(1)} collective-permute-done((f32[13,8,128]{2,1,0:T(8,128)S(1)}, f32[13,8,128]{2,1,0:T(8,128)S(1)}, u32[]{:S(2)}, u32[]{:S(2)}) %collective-permute-start.4) | collective-permute-done | bytes 53280 | tf_op jit(solution)/shard_map/ppermute | solution.py:360
  31.5 0.8 collective-permute-start.5
  32.3 3.4 %collective-permute-done.5 = f32[13,8,128]{2,1,0:T(8,128)S(1)} collective-permute-done((f32[13,8,128]{2,1,0:T(8,128)S(1)}, f32[13,8,128]{2,1,0:T(8,128)S(1)}, u32[]{:S(2)}, u32[]{:S(2)}) %collective-permute-start.5) | collective-permute-done | bytes 53280 | tf_op jit(solution)/shard_map/ppermute | solution.py:360
  35.7 0.3 collective-permute-start.6
  36.0 0.0 collective-permute-done.9
  36.0 0.0 collective-permute-done.8
  36.0 1.0 %pad_maximum_fusion.refs_4_ = f32[216,8,128]{2,1,0:T(8,128)} fusion(f32[72,8,128]{2,1,0:T(8,128)S(1)} %collective-permute-done.9, f32[72,8,128]{2,1,0:T(8,128)S(1)} %collective-permute-done.8, f32[72,8,128]{2,1,0:T(8,128)S(1)} %collective-permute-done.7), kind=kLoop, calls=%fused_computation | loop fusion | flops 442368 | bytes 1769472 | tf_op jit(solution)/shard_map/concatenate | solution.py:352
  37.0 4.1 %collective-permute-done.6 = f32[13,8,128]{2,1,0:T(8,128)S(1)} collective-permute-done((f32[13,8,128]{2,1,0:T(8,128)S(1)}, f32[13,8,128]{2,1,0:T(8,128)S(1)}, u32[]{:S(2)}, u32[]{:S(2)}) %collective-permute-start.6) | collective-permute-done | bytes 53280 | tf_op jit(solution)/shard_map/ppermute | solution.py:360
  41.2 0.6 add.57.refs_2_
  41.8 10.7 %middle.1 = (f32[432,8,128]{2,1,0:T(8,128)}, f32[26,8,128]{2,1,0:T(8,128)}, f32[216,8,128]{2,1,0:T(8,128)}) custom-call(s32[2,32]{1,0:T(2,128)} %refs_0_.3, s32[8,128]{1,0:T(8,128)} %bitcast.5, f32[13,8,128]{2,1,0:T(8,128)} %add.57.refs_2_, f32[432,8,128]{2,1,0:T(8,128)} %bitcast.4, f32[216,8,128]{2,1,0:T(8,128)} %pad_maximum_fusion.refs_4_), custom_call_target="tpu_custom_call" | custom-call | tf_op jit(solution)/shard_map/middle/pallas_call | solution.py:331
  52.5 0.9 slice.36
  53.4 0.0 collective-permute-start.11
  53.4 2.0 %collective-permute-start.10 = (f32[13,8,128]{2,1,0:T(8,128)S(1)}, f32[13,8,128]{2,1,0:T(8,128)S(1)}, u32[]{:S(2)}, u32[]{:S(2)}) collective-permute-start(f32[13,8,128]{2,1,0:T(8,128)S(1)} %slice.36), channel_id=1, source_target_pairs={{0,1},{1,2},{2,3},{3,4},{4,5},{5,6},{6,7},{7,0},{8,9},{9,10},{10,1... | collective-permute-start | bytes 159752 | tf_op jit(solution)/shard_map/ppermute | solution.py:365
  55.4 1.2 %fusion.1 = (f32[72,8,128]{2,1,0:T(8,128)S(1)}, f32[72,8,128]{2,1,0:T(8,128)S(1)}, f32[72,8,128]{2,1,0:T(8,128)S(1)}) fusion(f32[216,8,128]{2,1,0:T(8,128)} %get-tuple-element.14), kind=kLoop, calls=%fused_computation.6 | loop fusion | bytes 1769472 | tf_op jit(solution)/shard_map/slice | solution.py:351
  56.6 1.3 %collective-permute-start.17 = (f32[72,8,128]{2,1,0:T(8,128)S(1)}, f32[72,8,128]{2,1,0:T(8,128)S(1)}, u32[]{:S(2)}, u32[]{:S(2)}) collective-permute-start(f32[72,8,128]{2,1,0:T(8,128)S(1)} %get-tuple-element.15), channel_id=1, source_target_pairs={{0,7},{1,0},{2,1},{3,2},{4,3},{5,4},{6,5},{7,6},{8,9},{9,10},{10,1... | collective-permute-start | bytes 884744 | tf_op jit(solution)/shard_map/ppermute | solution.py:351
  57.9 0.8 collective-permute-start.19
  58.7 2.4 %collective-permute-start.18 = (f32[72,8,128]{2,1,0:T(8,128)S(1)}, f32[72,8,128]{2,1,0:T(8,128)S(1)}, u32[]{:S(2)}, u32[]{:S(2)}) collective-permute-start(f32[72,8,128]{2,1,0:T(8,128)S(1)} %get-tuple-element.17), channel_id=1, source_target_pairs={{0,7},{1,0},{2,1},{3,2},{4,3},{5,4},{6,5},{7,6},{8,15},{9,8},{10,9... | collective-permute-start | bytes 884744 | tf_op jit(solution)/shard_map/ppermute | solution.py:351
  61.2 0.1 select_add_fusion
  61.2 0.0 collective-permute-start.12
  61.3 1.2 %collective-permute-done.12 = f32[13,8,128]{2,1,0:T(8,128)S(1)} collective-permute-done((f32[13,8,128]{2,1,0:T(8,128)S(1)}, f32[13,8,128]{2,1,0:T(8,128)S(1)}, u32[]{:S(2)}, u32[]{:S(2)}) %collective-permute-start.12) | collective-permute-done | bytes 53280 | tf_op jit(solution)/shard_map/ppermute | solution.py:360
  62.5 0.3 collective-permute-start.13
  62.8 4.1 %collective-permute-done.13 = f32[13,8,128]{2,1,0:T(8,128)S(1)} collective-permute-done((f32[13,8,128]{2,1,0:T(8,128)S(1)}, f32[13,8,128]{2,1,0:T(8,128)S(1)}, u32[]{:S(2)}, u32[]{:S(2)}) %collective-permute-start.13) | collective-permute-done | bytes 53280 | tf_op jit(solution)/shard_map/ppermute | solution.py:360
  66.9 1.1 %collective-permute-start.14 = (f32[13,8,128]{2,1,0:T(8,128)S(1)}, f32[13,8,128]{2,1,0:T(8,128)S(1)}, u32[]{:S(2)}, u32[]{:S(2)}) collective-permute-start(f32[13,8,128]{2,1,0:T(8,128)S(1)} %add.60), channel_id=1, source_target_pairs={{0,48},{8,56},{16,32},{24,40},{32,16},{40,24},{48,0},{56,8},{64,11... | collective-permute-start | bytes 159752 | tf_op jit(solution)/shard_map/ppermute | solution.py:360
  68.0 4.4 %collective-permute-done.14 = f32[13,8,128]{2,1,0:T(8,128)S(1)} collective-permute-done((f32[13,8,128]{2,1,0:T(8,128)S(1)}, f32[13,8,128]{2,1,0:T(8,128)S(1)}, u32[]{:S(2)}, u32[]{:S(2)}) %collective-permute-start.14) | collective-permute-done | bytes 53280 | tf_op jit(solution)/shard_map/ppermute | solution.py:360
  72.4 0.1 collective-permute-start.15
  72.5 4.1 %collective-permute-done.15 = f32[13,8,128]{2,1,0:T(8,128)S(1)} collective-permute-done((f32[13,8,128]{2,1,0:T(8,128)S(1)}, f32[13,8,128]{2,1,0:T(8,128)S(1)}, u32[]{:S(2)}, u32[]{:S(2)}) %collective-permute-start.15) | collective-permute-done | bytes 53280 | tf_op jit(solution)/shard_map/ppermute | solution.py:360
  76.6 0.3 collective-permute-start.16
  76.9 0.0 collective-permute-done.17
  76.9 0.0 collective-permute-done.19
  76.9 0.0 collective-permute-done.18
  76.9 1.0 %pad_maximum_fusion.1.refs_4_ = f32[216,8,128]{2,1,0:T(8,128)} fusion(f32[72,8,128]{2,1,0:T(8,128)S(1)} %collective-permute-done.19, f32[72,8,128]{2,1,0:T(8,128)S(1)} %collective-permute-done.18, f32[72,8,128]{2,1,0:T(8,128)S(1)} %collective-permute-done.17), kind=kLoop, calls=%fused_computation.1 | loop fusion | flops 442368 | bytes 1769472 | tf_op jit(solution)/shard_map/concatenate | solution.py:352
  77.9 4.1 %collective-permute-done.16 = f32[13,8,128]{2,1,0:T(8,128)S(1)} collective-permute-done((f32[13,8,128]{2,1,0:T(8,128)S(1)}, f32[13,8,128]{2,1,0:T(8,128)S(1)}, u32[]{:S(2)}, u32[]{:S(2)}) %collective-permute-start.16) | collective-permute-done | bytes 53280 | tf_op jit(solution)/shard_map/ppermute | solution.py:360
  82.0 0.6 add.63.refs_2_
  82.7 6.8 %last.1 = f32[432,8,128]{2,1,0:T(8,128)} custom-call(s32[2,32]{1,0:T(2,128)} %refs_0_.3, s32[8,128]{1,0:T(8,128)} %bitcast.6, f32[13,8,128]{2,1,0:T(8,128)} %add.63.refs_2_, f32[432,8,128]{2,1,0:T(8,128)} %get-tuple-element.13.refs_3_, f32[216,8,128]{2,1,0:T(8,128)} %pad_maximum_fusion.1.refs_4_), custom_call_target="tpu_custom_call" | custom-call | tf_op jit(solution)/shard_map/last/pallas_call | solution.py:331
  (18 shorter events, 0.1 us)
Async XLA Ops:
  5.9 14.5 %copy-start.1 = (f32[26,8,128]{2,1,0:T(8,128)S(1)}, f32[26,8,128]{2,1,0:T(8,128)}, u32[]{:S(2)}) copy-start(f32[26,8,128]{2,1,0:T(8,128)} %get-tuple-element.10) | copy-start | bytes 319492
  6.8 13.6 %collective-permute-start.1 = (f32[13,8,128]{2,1,0:T(8,128)S(1)}, f32[13,8,128]{2,1,0:T(8,128)S(1)}, u32[]{:S(2)}, u32[]{:S(2)}) collective-permute-start(f32[13,8,128]{2,1,0:T(8,128)S(1)} %slice.31), channel_id=1, source_target_pairs={{1,0},{2,1},{3,2},{4,3},{5,4},{6,5},{7,6},{0,7},{9,8},{10,9},{11,1... | collective-permute-start | bytes 159752 | tf_op jit(solution)/shard_map/ppermute | solution.py:366
  12.7 7.8 %collective-permute-start = (f32[13,8,128]{2,1,0:T(8,128)S(1)}, f32[13,8,128]{2,1,0:T(8,128)S(1)}, u32[]{:S(2)}, u32[]{:S(2)}) collective-permute-start(f32[13,8,128]{2,1,0:T(8,128)S(1)} %slice.31), channel_id=1, source_target_pairs={{0,1},{1,2},{2,3},{3,4},{4,5},{5,6},{6,7},{7,0},{8,9},{9,10},{10,1... | collective-permute-start | bytes 159752 | tf_op jit(solution)/shard_map/ppermute | solution.py:365
  13.9 22.1 %collective-permute-start.7 = (f32[72,8,128]{2,1,0:T(8,128)S(1)}, f32[72,8,128]{2,1,0:T(8,128)S(1)}, u32[]{:S(2)}, u32[]{:S(2)}) collective-permute-start(f32[72,8,128]{2,1,0:T(8,128)S(1)} %get-tuple-element.18), channel_id=1, source_target_pairs={{0,7},{1,0},{2,1},{3,2},{4,3},{5,4},{6,5},{7,6},{8,9},{9,10},{10,1... | collective-permute-start | bytes 884744 | tf_op jit(solution)/shard_map/ppermute | solution.py:351
  17.2 18.8 %collective-permute-start.9 = (f32[72,8,128]{2,1,0:T(8,128)S(1)}, f32[72,8,128]{2,1,0:T(8,128)S(1)}, u32[]{:S(2)}, u32[]{:S(2)}) collective-permute-start(f32[72,8,128]{2,1,0:T(8,128)S(1)} %get-tuple-element.19), channel_id=1, source_target_pairs={{0,1},{1,2},{2,3},{3,4},{4,5},{5,6},{6,7},{7,0},{8,15},{9,8},{10,9... | collective-permute-start | bytes 884744 | tf_op jit(solution)/shard_map/ppermute | solution.py:351
  17.2 18.8 %collective-permute-start.8 = (f32[72,8,128]{2,1,0:T(8,128)S(1)}, f32[72,8,128]{2,1,0:T(8,128)S(1)}, u32[]{:S(2)}, u32[]{:S(2)}) collective-permute-start(f32[72,8,128]{2,1,0:T(8,128)S(1)} %get-tuple-element.20), channel_id=1, source_target_pairs={{0,7},{1,0},{2,1},{3,2},{4,3},{5,4},{6,5},{7,6},{8,15},{9,8},{10,9... | collective-permute-start | bytes 884744 | tf_op jit(solution)/shard_map/ppermute | solution.py:351
  20.5 1.3 %collective-permute-start.2 = (f32[13,8,128]{2,1,0:T(8,128)S(1)}, f32[13,8,128]{2,1,0:T(8,128)S(1)}, u32[]{:S(2)}, u32[]{:S(2)}) collective-permute-start(f32[13,8,128]{2,1,0:T(8,128)S(1)} %select_add_fusion.1), channel_id=1, source_target_pairs={{0,8},{8,0},{16,24},{24,16},{32,40},{40,32},{48,56},{56,48},{64,72... | collective-permute-start | bytes 159752 | tf_op jit(solution)/shard_map/ppermute | solution.py:360
  21.8 4.2 %collective-permute-start.3 = (f32[13,8,128]{2,1,0:T(8,128)S(1)}, f32[13,8,128]{2,1,0:T(8,128)S(1)}, u32[]{:S(2)}, u32[]{:S(2)}) collective-permute-start(f32[13,8,128]{2,1,0:T(8,128)S(1)} %add.53), channel_id=1, source_target_pairs={{0,16},{8,24},{16,0},{24,8},{32,48},{40,56},{48,32},{56,40},{64,80... | collective-permute-start | bytes 159752 | tf_op jit(solution)/shard_map/ppermute | solution.py:360
  26.0 5.4 %collective-permute-start.4 = (f32[13,8,128]{2,1,0:T(8,128)S(1)}, f32[13,8,128]{2,1,0:T(8,128)S(1)}, u32[]{:S(2)}, u32[]{:S(2)}) collective-permute-start(f32[13,8,128]{2,1,0:T(8,128)S(1)} %add.54), channel_id=1, source_target_pairs={{0,48},{8,56},{16,32},{24,40},{32,16},{40,24},{48,0},{56,8},{64,11... | collective-permute-start | bytes 159752 | tf_op jit(solution)/shard_map/ppermute | solution.py:360
  31.5 4.2 %collective-permute-start.5 = (f32[13,8,128]{2,1,0:T(8,128)S(1)}, f32[13,8,128]{2,1,0:T(8,128)S(1)}, u32[]{:S(2)}, u32[]{:S(2)}) collective-permute-start(f32[13,8,128]{2,1,0:T(8,128)S(1)} %add.55), channel_id=1, source_target_pairs={{0,64},{8,72},{16,80},{24,88},{32,96},{40,104},{48,112},{56,120},{... | collective-permute-start | bytes 159752 | tf_op jit(solution)/shard_map/ppermute | solution.py:360
  35.7 5.4 %collective-permute-start.6 = (f32[13,8,128]{2,1,0:T(8,128)S(1)}, f32[13,8,128]{2,1,0:T(8,128)S(1)}, u32[]{:S(2)}, u32[]{:S(2)}) collective-permute-start(f32[13,8,128]{2,1,0:T(8,128)S(1)} %add.56), channel_id=1, source_target_pairs={{0,192},{8,200},{16,208},{24,216},{32,224},{40,232},{48,240},{56,2... | collective-permute-start | bytes 159752 | tf_op jit(solution)/shard_map/ppermute | solution.py:360
  52.5 8.7 %copy-start = (f32[26,8,128]{2,1,0:T(8,128)S(1)}, f32[26,8,128]{2,1,0:T(8,128)}, u32[]{:S(2)}) copy-start(f32[26,8,128]{2,1,0:T(8,128)} %get-tuple-element.12) | copy-start | bytes 319492
  53.4 7.8 %collective-permute-start.11 = (f32[13,8,128]{2,1,0:T(8,128)S(1)}, f32[13,8,128]{2,1,0:T(8,128)S(1)}, u32[]{:S(2)}, u32[]{:S(2)}) collective-permute-start(f32[13,8,128]{2,1,0:T(8,128)S(1)} %slice.36), channel_id=1, source_target_pairs={{1,0},{2,1},{3,2},{4,3},{5,4},{6,5},{7,6},{0,7},{9,8},{10,9},{11,1... | collective-permute-start | bytes 159752 | tf_op jit(solution)/shard_map/ppermute | solution.py:366
  53.4 7.8 %collective-permute-start.10 = (f32[13,8,128]{2,1,0:T(8,128)S(1)}, f32[13,8,128]{2,1,0:T(8,128)S(1)}, u32[]{:S(2)}, u32[]{:S(2)}) collective-permute-start(f32[13,8,128]{2,1,0:T(8,128)S(1)} %slice.36), channel_id=1, source_target_pairs={{0,1},{1,2},{2,3},{3,4},{4,5},{5,6},{6,7},{7,0},{8,9},{9,10},{10,1... | collective-permute-start | bytes 159752 | tf_op jit(solution)/shard_map/ppermute | solution.py:365
  56.6 20.3 %collective-permute-start.17 = (f32[72,8,128]{2,1,0:T(8,128)S(1)}, f32[72,8,128]{2,1,0:T(8,128)S(1)}, u32[]{:S(2)}, u32[]{:S(2)}) collective-permute-start(f32[72,8,128]{2,1,0:T(8,128)S(1)} %get-tuple-element.15), channel_id=1, source_target_pairs={{0,7},{1,0},{2,1},{3,2},{4,3},{5,4},{6,5},{7,6},{8,9},{9,10},{10,1... | collective-permute-start | bytes 884744 | tf_op jit(solution)/shard_map/ppermute | solution.py:351
  57.9 19.0 %collective-permute-start.19 = (f32[72,8,128]{2,1,0:T(8,128)S(1)}, f32[72,8,128]{2,1,0:T(8,128)S(1)}, u32[]{:S(2)}, u32[]{:S(2)}) collective-permute-start(f32[72,8,128]{2,1,0:T(8,128)S(1)} %get-tuple-element.16), channel_id=1, source_target_pairs={{0,1},{1,2},{2,3},{3,4},{4,5},{5,6},{6,7},{7,0},{8,15},{9,8},{10,9... | collective-permute-start | bytes 884744 | tf_op jit(solution)/shard_map/ppermute | solution.py:351
  58.7 18.2 %collective-permute-start.18 = (f32[72,8,128]{2,1,0:T(8,128)S(1)}, f32[72,8,128]{2,1,0:T(8,128)S(1)}, u32[]{:S(2)}, u32[]{:S(2)}) collective-permute-start(f32[72,8,128]{2,1,0:T(8,128)S(1)} %get-tuple-element.17), channel_id=1, source_target_pairs={{0,7},{1,0},{2,1},{3,2},{4,3},{5,4},{6,5},{7,6},{8,15},{9,8},{10,9... | collective-permute-start | bytes 884744 | tf_op jit(solution)/shard_map/ppermute | solution.py:351
  61.2 1.3 %collective-permute-start.12 = (f32[13,8,128]{2,1,0:T(8,128)S(1)}, f32[13,8,128]{2,1,0:T(8,128)S(1)}, u32[]{:S(2)}, u32[]{:S(2)}) collective-permute-start(f32[13,8,128]{2,1,0:T(8,128)S(1)} %select_add_fusion), channel_id=1, source_target_pairs={{0,8},{8,0},{16,24},{24,16},{32,40},{40,32},{48,56},{56,48},{64,72... | collective-permute-start | bytes 159752 | tf_op jit(solution)/shard_map/ppermute | solution.py:360
  62.5 4.4 %collective-permute-start.13 = (f32[13,8,128]{2,1,0:T(8,128)S(1)}, f32[13,8,128]{2,1,0:T(8,128)S(1)}, u32[]{:S(2)}, u32[]{:S(2)}) collective-permute-start(f32[13,8,128]{2,1,0:T(8,128)S(1)} %add.59), channel_id=1, source_target_pairs={{0,16},{8,24},{16,0},{24,8},{32,48},{40,56},{48,32},{56,40},{64,80... | collective-permute-start | bytes 159752 | tf_op jit(solution)/shard_map/ppermute | solution.py:360
  66.9 5.4 %collective-permute-start.14 = (f32[13,8,128]{2,1,0:T(8,128)S(1)}, f32[13,8,128]{2,1,0:T(8,128)S(1)}, u32[]{:S(2)}, u32[]{:S(2)}) collective-permute-start(f32[13,8,128]{2,1,0:T(8,128)S(1)} %add.60), channel_id=1, source_target_pairs={{0,48},{8,56},{16,32},{24,40},{32,16},{40,24},{48,0},{56,8},{64,11... | collective-permute-start | bytes 159752 | tf_op jit(solution)/shard_map/ppermute | solution.py:360
  72.4 4.2 %collective-permute-start.15 = (f32[13,8,128]{2,1,0:T(8,128)S(1)}, f32[13,8,128]{2,1,0:T(8,128)S(1)}, u32[]{:S(2)}, u32[]{:S(2)}) collective-permute-start(f32[13,8,128]{2,1,0:T(8,128)S(1)} %add.61), channel_id=1, source_target_pairs={{0,64},{8,72},{16,80},{24,88},{32,96},{40,104},{48,112},{56,120},{... | collective-permute-start | bytes 159752 | tf_op jit(solution)/shard_map/ppermute | solution.py:360
  76.6 5.4 %collective-permute-start.16 = (f32[13,8,128]{2,1,0:T(8,128)S(1)}, f32[13,8,128]{2,1,0:T(8,128)S(1)}, u32[]{:S(2)}, u32[]{:S(2)}) collective-permute-start(f32[13,8,128]{2,1,0:T(8,128)S(1)} %add.62), channel_id=1, source_target_pairs={{0,192},{8,200},{16,208},{24,216},{32,224},{40,232},{48,240},{56,2... | collective-permute-start | bytes 159752 | tf_op jit(solution)/shard_map/ppermute | solution.py:360

commit v2 on v1

v2 whole, which is shorter than its diff:
```python
import math

import jax
import jax.numpy as jnp
from jax import lax
from jax.experimental import pallas as pl
from jax.experimental.pallas import tpu as pltpu
from jax.sharding import PartitionSpec as P

NV1 = 24
NB = 18
HALF = NV1 // 2
NGROUP = 3
PER = NB // NGROUP
SLOT = PER * HALF
NMOM = 13
NPACK = 7
ORDERS = ((0, 0), (1, 0), (2, 0), (3, 0), (0, 1), (1, 1), (2, 1), (0, 2), (1, 2), (0, 3))
NORD = len(ORDERS)
STEP = 0.6
DT = 0.25
WEIGHT = STEP**3
CENTRE = 0.5 * (NV1 - 1)
ZS = [(c - CENTRE) * STEP for c in range(NV1)]
INFLOW_Z = [math.exp(-0.5 * z * z) for z in ZS]
INFLOW_SUMS = [sum(z**k * g for z, g in zip(ZS, INFLOW_Z)) for k in range(4)]
INFLOW_SCALE = 200.0 / (2.0 * math.pi) ** 1.5
SHAPE = (8, 128)
F32 = jnp.float32


def iotas():
    subs = lax.broadcasted_iota(jnp.int32, SHAPE, 0)
    lanes = lax.broadcasted_iota(jnp.int32, SHAPE, 1)
    return subs, jnp.bitwise_and(subs, 3), lanes


def flag_tile(flags_ref, subs, gy):
    tile = jnp.zeros(SHAPE, jnp.int32)
    for plane in range(2):
        for row in range(4):
            tile = jnp.where(subs == plane * 4 + row, flags_ref[plane, gy * 4 + row], tile)
    return tile > 0


def weights_of(speed):
    k = jnp.abs(speed) * DT
    return 1.0 - 1.5 * k + 0.5 * k * k, 2.0 * k - k * k, 0.5 * k * k - 0.5 * k


def speeds(vel, block):
    index = vel * NB + block
    a = lax.div(index, NV1)
    b = index - a * NV1
    return (a.astype(F32) - CENTRE) * STEP, (b.astype(F32) - CENTRE) * STEP


def group_state(vel, group):
    first = lax.rem(3 * vel, 4)

    def up_of(g):
        return lax.rem(first + g, 4) >= 2

    up = up_of(group)
    slot = jnp.where(jnp.logical_and(group > 0, up_of(0) == up), 1, 0)
    slot = slot + jnp.where(jnp.logical_and(group > 1, up_of(1) == up), 1, 0)
    a_slot = lax.div(vel * NB + PER * group, NV1) - lax.div(vel * NB, NV1)
    return up, slot, a_slot


def over_blocks(vel, body):
    for right in (True, False):

        @pl.when((vel >= 16) == right)
        def _(right=right):
            def group_loop(group, carry):
                up, slot, a_slot = group_state(vel, group)
                for up_now in (True, False):

                    @pl.when(up == up_now)
                    def _(up_now=up_now):
                        def block_loop(k, c):
                            body(PER * group + k, slot * SLOT + HALF * k, a_slot, right, up_now)
                            return c

                        lax.fori_loop(0, PER, block_loop, 0)

                return carry

            lax.fori_loop(0, NGROUP, group_loop, 0)


def inflow_block(speed_x, speed_y):
    drift = speed_x - 3.0
    return INFLOW_SCALE * jnp.exp(jnp.full(SHAPE, -0.5 * (drift * drift + speed_y * speed_y), F32))


def x_weights(speed_x, lanes, right, inflow_rows):
    c0, c1, c2 = weights_of(speed_x)
    zero = jnp.zeros(SHAPE, F32)
    v0, v1, v2 = (jnp.full(SHAPE, c, F32) for c in (c0, c1, c2))
    if right:
        edge, next_edge, inner = lanes == 0, lanes == 1, lanes >= 2
        held = jnp.logical_not(inflow_rows)
        a0 = jnp.where(jnp.logical_and(edge, held), 1.0, v0)
        a1 = jnp.where(edge, zero, jnp.where(jnp.logical_and(next_edge, held), v1 + v2, v1))
        a2 = jnp.where(inner, v2, zero)
        ghost = jnp.where(inflow_rows, jnp.where(edge, v1 + v2, jnp.where(next_edge, v2, zero)), zero)
        return a0, a1, a2, ghost
    edge, next_edge, inner = lanes == 127, lanes == 126, lanes < 126
    a0 = jnp.where(edge, 1.0, v0)
    a1 = jnp.where(edge, zero, jnp.where(next_edge, v1 + v2, v1))
    a2 = jnp.where(inner, v2, zero)
    return a0, a1, a2, None


def sweep_x(values, weights, right, ghost):
    one = pltpu.roll(values, 1 if right else 127, 1)
    two = pltpu.roll(values, 2 if right else 126, 1)
    swept = weights[0] * values + weights[1] * one + weights[2] * two
    return swept if ghost is None else swept + ghost


def z_sums(z, low, high, c):
    s = low + high
    d = high - low
    speed = ZS[NV1 - 1 - c]
    z0, z1, z2, z3 = z
    return [z0 + s, z1 + speed * d, z2 + speed**2 * s, z3 + speed**3 * d]


def pack_halo(low, high, rows, up):
    if up:
        return jnp.where(rows >= 2, pltpu.roll(low, 4, 0), pltpu.roll(high, 6, 0))
    return jnp.where(rows < 2, pltpu.roll(low, 4, 0), pltpu.roll(high, 2, 0))


def block_moments(acc_ref, a_slot, z, speed_x, speed_y, lanes, rows, right, up, inflow_rows):
    weights = x_weights(speed_x, lanes, right, inflow_rows)
    c0, c1, c2 = weights_of(speed_y)
    zero = jnp.zeros(SHAPE, F32)
    v1, v2 = jnp.full(SHAPE, c1, F32), jnp.full(SHAPE, c2, F32)
    last = rows == (0 if up else 3)
    head = rows < 2 if up else rows >= 2
    own1, cross1 = jnp.where(last, zero, v1), jnp.where(last, v1, zero)
    own2, cross2 = jnp.where(head, zero, v2), jnp.where(head, v2, zero)
    own, cross = [], []
    base = weights[3] * inflow_block(speed_x, speed_y) if right else None
    for k in range(4):
        ghost = INFLOW_SUMS[k] * base if right and k % 2 == 0 else None
        swept = sweep_x(z[k], weights, right, ghost)
        r1 = pltpu.roll(swept, 1 if up else 7, 0)
        r2 = pltpu.roll(swept, 2 if up else 6, 0)
        own.append(c0 * swept + own1 * r1 + own2 * r2)
        cross.append(cross1 * r1 + cross2 * r2)
    for side, values in enumerate((own, cross)):
        powers = {}
        for m, (j, k) in enumerate(ORDERS):
            powers[j, k] = values[k] if j == 0 else speed_y * powers[j - 1, k]
            at = a_slot * (2 * NORD) + side * NORD + m
            acc_ref[at] = acc_ref[at] + powers[j, k]


def clear_moments(acc_ref):
    for m in range(4 * NORD):
        acc_ref[m] = jnp.zeros(SHAPE, F32)


def finish_moments(acc_ref, keep_ref, send_ref, vel, rows):
    first_a = lax.div(vel * NB, NV1).astype(F32)
    odd = lax.rem(vel, 2) == 1
    low = rows < 2
    for side in range(2):
        total = None
        for a_slot in range(2):
            x = (first_a + (a_slot - CENTRE)) * STEP
            o = {jk: WEIGHT * acc_ref[a_slot * 2 * NORD + side * NORD + m] for m, jk in enumerate(ORDERS)}
            xo = x * o[0, 0]
            xx = x * xo
            terms = [
                o[0, 0], xo, o[1, 0], o[0, 1],
                xx, o[2, 0], o[0, 2],
                x * o[1, 0], x * o[0, 1], o[1, 1],
                x * xx + x * (o[2, 0] + o[0, 2]),
                x * x * o[1, 0] + (o[3, 0] + o[1, 2]),
                x * x * o[0, 1] + (o[2, 1] + o[0, 3]),
            ]
            total = terms if total is None else [p + q for p, q in zip(total, terms)]
        if side:
            total = [pltpu.roll(v, 4, 0) for v in total]
        for k in range(NPACK):
            one = total[k]
            two = total[k + NPACK] if k + NPACK < NMOM else one
            upper = jnp.where(low, one, pltpu.roll(two, 2, 0))
            lower = jnp.where(low, pltpu.roll(two, 6, 0), one)
            keep_ref[side * NPACK + k] = jnp.where(odd, lower, upper)
            send_ref[side * NPACK + k] = jnp.where(odd, upper, lower)


def first_kernel(flags_ref, f_hbm, f_ref, keep_ref, send_ref, up_ref, down_ref, acc_ref, sems):
    def f_copy(j):
        return pltpu.make_async_copy(f_hbm.at[pl.ds(NV1 * j, NV1)], f_ref.at[pl.ds(NV1 * j, NV1)], sems.at[j])

    for j in range(NB):
        f_copy(j).start()
    vel, gy = lax.axis_index("vel"), lax.axis_index("gy")
    subs, rows, lanes = iotas()
    inflow_rows = flag_tile(flags_ref, subs, gy)
    clear_moments(acc_ref)

    def body(j, at, a_slot, right, up):
        speed_x, speed_y = speeds(vel, j)
        out_ref = up_ref if up else down_ref
        f_copy(j).wait()
        z = [jnp.zeros(SHAPE, F32)] * 4
        for c in range(HALF):
            low = f_ref[NV1 * j + c]
            high = f_ref[NV1 * j + (NV1 - 1 - c)]
            z = z_sums(z, low, high, c)
            out_ref[at + c] = pack_halo(low, high, rows, up)
        block_moments(acc_ref, a_slot, z, speed_x, speed_y, lanes, rows, right, up, inflow_rows)

    over_blocks(vel, body)
    finish_moments(acc_ref, keep_ref, send_ref, vel, rows)


def move_kernel(flags_ref, f_ref, up_ref, down_ref, moved_ref):
    vel, gy = lax.axis_index("vel"), lax.axis_index("gy")
    subs, rows, lanes = iotas()
    own_rows = flag_tile(flags_ref, subs, gy)
    low_rows = flag_tile(flags_ref, subs, lax.rem(gy + 7, 8)).astype(F32)
    high_rows = flag_tile(flags_ref, subs, lax.rem(gy + 1, 8)).astype(F32)
    halo_rows = [pack_halo(r, r, rows, up) > 0.5 for r, up in ((high_rows, False), (low_rows, True))]

    def body(j, at, a_slot, right, up):
        speed_x, speed_y = speeds(vel, j)
        in_ref = up_ref if up else down_ref
        own = x_weights(speed_x, lanes, right, own_rows)
        out = x_weights(speed_x, lanes, right, halo_rows[up]) if right else own
        inflow = inflow_block(speed_x, speed_y) if right else None
        c0, c1, c2 = weights_of(speed_y)
        last = rows == (0 if up else 3)
        first = rows == (3 if up else 0)
        head = rows < 2 if up else rows >= 2
        s1, s2 = (1, 2) if up else (7, 6)
        own_base = own[3] * inflow if right else None
        out_base = out[3] * inflow if right else None
        for c in range(HALF):
            h = NV1 - 1 - c
            ghost = INFLOW_Z[c] * own_base if right else None
            low = sweep_x(f_ref[NV1 * j + c], own, right, ghost)
            high = sweep_x(f_ref[NV1 * j + h], own, right, ghost)
            halo = sweep_x(in_ref[at + c], out, right, INFLOW_Z[c] * out_base if right else None)
            low1 = pltpu.roll(jnp.where(first, halo, low), s1, 0)
            low2 = pltpu.roll(jnp.where(head, low, halo), s2, 0)
            high1 = jnp.where(last, pltpu.roll(halo, 8 - s1, 0), pltpu.roll(high, s1, 0))
            high2 = jnp.where(head, halo, pltpu.roll(high, s2, 0))
            moved_ref[NV1 * j + c] = c0 * low + c1 * low1 + c2 * low2
            moved_ref[NV1 * j + h] = c0 * high + c1 * high1 + c2 * high2

    over_blocks(vel, body)


def unpack_moments(own_ref, other_ref, vel, rows):
    odd = lax.rem(vel, 2) == 1
    low = rows < 2
    one, two = [], []
    for k in range(NPACK):
        a, b = own_ref[k], other_ref[k]
        upper, lower = jnp.where(odd, b, a), jnp.where(odd, a, b)
        one.append(jnp.where(low, upper, lower))
        two.append(jnp.where(low, pltpu.roll(upper, 6, 0), pltpu.roll(lower, 2, 0)))
    return (one + two)[:NMOM]


def cell_values(mom, solid):
    n = mom[0]
    inv = 1.0 / n
    ux, uy, uz = mom[1] * inv, mom[2] * inv, mom[3] * inv
    xx, yy, zz, xy, xz, yz = mom[4:10]
    energy = xx + yy + zz
    usq = ux * ux + uy * uy + uz * uz
    p = (energy - n * usq) * (1.0 / 3.0)
    common = 2.0 * n * usq - energy
    qx = 0.5 * (mom[10] - 2.0 * (xx * ux + xy * uy + xz * uz) + common * ux)
    qy = 0.5 * (mom[11] - 2.0 * (xy * ux + yy * uy + yz * uz) + common * uy)
    qz = 0.5 * (mom[12] - 2.0 * (xz * ux + yz * uy + zz * uz) + common * uz)
    temp = p * inv
    rate = p / (3000.0 * jnp.exp(0.81 * jnp.log(temp * (1.0 / 3.0))))
    damp = jnp.exp(-DT * rate)
    skew = (1.0 / 15.0) / (p * temp)
    zero = jnp.zeros(SHAPE, F32)
    n = jnp.where(solid, 200.0, n)
    temp = jnp.where(solid, 1.5, temp)
    damp = jnp.where(solid, zero, damp)
    skew = jnp.where(solid, zero, skew)
    ux, uy, uz = (jnp.where(solid, zero, u) for u in (ux, uy, uz))
    wide = 2.0 * math.pi * temp
    scale = n / (wide * jnp.sqrt(wide)) * (1.0 - damp)
    return scale, ux, uy, uz, 1.0 / temp, skew * qx, skew * qy, skew * qz, damp


def relax_kernel(last_step, flags_ref, mask_ref, own_ref, other_ref, moved_ref, *refs):
    if last_step:
        out_hbm, o_ref, z_ref, sems = refs
    else:
        o_ref, keep_ref, send_ref, up_ref, down_ref, acc_ref, z_ref = refs

    def o_copy(j):
        return pltpu.make_async_copy(o_ref.at[pl.ds(NV1 * j, NV1)], out_hbm.at[pl.ds(NV1 * j, NV1)], sems.at[j])

    vel, gy = lax.axis_index("vel"), lax.axis_index("gy")
    subs, rows, lanes = iotas()
    solid = mask_ref[...] > 0
    mom = unpack_moments(own_ref, other_ref, vel, rows)
    scale, ux, uy, uz, inv_t, qx, qy, qz, damp = cell_values(mom, solid)
    half_inv = -0.5 * inv_t
    for c in range(NV1):
        cz = ZS[c] - uz
        sq = cz * cz
        z_ref[c] = jnp.exp(sq * half_inv)
        z_ref[NV1 + c] = cz * qz
        z_ref[2 * NV1 + c] = sq * inv_t
    if not last_step:
        inflow_rows = flag_tile(flags_ref, subs, gy)
        clear_moments(acc_ref)

    def body(j, at, a_slot, right, up):
        speed_x, speed_y = speeds(vel, j)
        cx, cy = speed_x - ux, speed_y - uy
        sq = cx * cx + cy * cy
        e_xy = scale * jnp.exp(sq * half_inv)
        q_xy = cx * qx + cy * qy
        s_xy = sq * inv_t - 5.0

        def relax(c):
            shape = (q_xy + z_ref[NV1 + c]) * (s_xy + z_ref[2 * NV1 + c]) + 1.0
            return damp * moved_ref[NV1 * j + c] + (e_xy * z_ref[c]) * shape

        z = [jnp.zeros(SHAPE, F32)] * 4
        for c in range(HALF):
            h = NV1 - 1 - c
            low, high = relax(c), relax(h)
            o_ref[NV1 * j + c] = low
            o_ref[NV1 * j + h] = high
            if not last_step:
                z = z_sums(z, low, high, c)
                (up_ref if up else down_ref)[at + c] = pack_halo(low, high, rows, up)
        if last_step:
            o_copy(j).start()
        else:
            block_moments(acc_ref, a_slot, z, speed_x, speed_y, lanes, rows, right, up, inflow_rows)

    if last_step:
        lax.fori_loop(0, NB, lambda j, c: (body(j, 0, 0, True, True), c)[1], 0)
        for j in range(NB):
            o_copy(j).wait()
    else:
        over_blocks(vel, body)
        finish_moments(acc_ref, keep_ref, send_ref, vel, rows)


HBM = pl.BlockSpec(memory_space=pltpu.HBM)
SMEM = pl.BlockSpec(memory_space=pltpu.SMEM)
VMEM = pl.BlockSpec(memory_space=pltpu.VMEM)
SUMS = pltpu.VMEM((2 * NPACK, 8, 128), F32)
HALO = pltpu.VMEM((2 * SLOT, 8, 128), F32)
STATE = pltpu.VMEM((NB * NV1, 8, 128), F32)
ACC = pltpu.VMEM((4 * NORD, 8, 128), F32)
TABLE = pltpu.VMEM((3 * NV1, 8, 128), F32)
PARAMS = pltpu.CompilerParams(vmem_limit_bytes=12 << 20)
DMAS = pltpu.SemaphoreType.DMA((NB,))


def in_vmem(x):
    return pltpu.with_memory_space_constraint(x, pltpu.VMEM)


def first_call(flags, f):
    return pl.pallas_call(
        first_kernel,
        out_shape=(STATE, SUMS, SUMS, HALO, HALO),
        in_specs=[SMEM, HBM],
        out_specs=(VMEM,) * 5,
        scratch_shapes=[ACC, DMAS],
        compiler_params=PARAMS,
        name="first",
    )(flags, pltpu.with_memory_space_constraint(f, pltpu.HBM))


def move_call(flags, f, up, down):
    return pl.pallas_call(
        move_kernel,
        out_shape=STATE,
        in_specs=[SMEM, VMEM, VMEM, VMEM],
        out_specs=VMEM,
        compiler_params=PARAMS,
        name="move",
    )(flags, in_vmem(f), in_vmem(up), in_vmem(down))


def relax_call(last_step, flags, mask, own, other, moved):
    def kernel(*refs):
        relax_kernel(last_step, *refs)

    if last_step:
        out_shape = (jax.ShapeDtypeStruct(STATE.shape, F32),)
        out_specs, scratch, name = (HBM,), [STATE, TABLE, DMAS], "last"
    else:
        out_shape, out_specs = (STATE, SUMS, SUMS, HALO, HALO), (VMEM,) * 5
        scratch, name = [ACC, TABLE], "middle"
    return pl.pallas_call(
        kernel,
        out_shape=out_shape,
        in_specs=[SMEM, VMEM, VMEM, VMEM, VMEM],
        out_specs=out_specs,
        scratch_shapes=scratch,
        compiler_params=PARAMS,
        name=name,
    )(flags, mask, in_vmem(own), in_vmem(other), in_vmem(moved))


def shift(values, toward):
    pairs = [(v * 8 + g, v * 8 + (g + toward(v)) % 8) for v in range(32) for g in range(8)]
    return lax.ppermute(values, ("vel", "gy"), pairs)


def exchange(values, flip):
    return lax.ppermute(values, "vel", [(v, v ^ flip) for v in range(32)])


def tie(value, *others):
    return lax.optimization_barrier((value,) + others)[0]


def communicate(flags, f, keep, send, up, down):
    both = keep + exchange(send, 1)
    cross = shift(both[NPACK:], lambda v: 1 if v % 2 == 0 else -1)
    up = shift(tie(up, both), lambda v: 1)
    mom = both[:NPACK] + cross
    mom = mom + exchange(mom, 2)
    down = shift(tie(down, cross), lambda v: -1)
    mom = mom + exchange(mom, 6)
    mom = mom + exchange(mom, 8)
    moved = move_call(flags, f, tie(up, mom), tie(down, mom))
    mom = mom + exchange(mom, 24)
    return mom, exchange(mom, 1), moved


def shards(distribution, body_mask, inflow_flags):
    mask = body_mask.reshape(8, 128)
    parts = first_call(inflow_flags, distribution.reshape(NB * NV1, 8, 128))
    own, other, moved = communicate(inflow_flags, *parts)
    parts = relax_call(False, inflow_flags, mask, own, other, moved)
    own, other, moved = communicate(inflow_flags, *parts)
    (out,) = relax_call(True, inflow_flags, mask, own, other, moved)
    return out.reshape(distribution.shape)


def solution(mesh):
    placed = (P("vel", None, "gy", None), P(None, "gy", None), P())
    return jax.shard_map(
        shards, mesh=mesh, in_specs=placed, out_specs=P("vel", None, "gy", None), check_vma=False
    )
```

time: 90 us -> 72.6 us (0.81); the launches traced: 89.7 us -> 71.2 us
  starting transfers between devices: 23.7 us -> 15.6 us
  Pallas kernels: 23.5 us -> 16.2 us
  waiting for transfers between devices: 34.6 us -> 38.5 us
  local copies, waits for them, and re-layouts: 4.16 us -> 0.7 us
  other arithmetic: 3.44 us -> 0.07 us
    ppermute x20 -> x18, starting transfers between devices: 23.7 us -> 15.6 us  [the longest x12 9.17 us: exchange(): return lax.ppermute(values, 'vel', [(v, v ^ flip) for v in range(32)])]
    pallas_call x3 -> x5, Pallas kernels: 23.5 us -> 16.2 us  [the longest x2 7.02 us: move_call(): pl.pallas_call(move_kernel, out_shape=STATE, in_specs=[SMEM, VMEM, VMEM,...]
    slice x4 -> x2, local copies, waits for them, and re-layouts: 4.15 us -> 0.01 us  [communicate(): cross = shift(both[NPACK:], lambda v: 1 if v % 2 == 0 else -1)]
    ppermute x20 -> x18, waiting for transfers between devices: 34.6 us -> 38.5 us  [the longest x12 29.5 us: exchange(): return lax.ppermute(values, 'vel', [(v, v ^ flip) for v in range(32)])]
    concatenate x2 -> x0, other arithmetic: 1.95 us -> none  [bulk_halo(): return jnp.concatenate(parts)]
    add x12, other arithmetic: 1.48 us -> 0.07 us  [the longest x2 0.02 us: communicate(): both = keep + exchange(send, 1)]
  transfers between devices with their start and end apart: 20 -> 18, of which waited for: 10 -> 12; matrix products, arithmetic and copies ran while one was open for 5% -> 0% of each run, Pallas kernels for 0% -> 10%
where the time goes in v2:
time: 72.6 us; the launch traced here: 71.2 us
  waiting for transfers between devices  38.5 us (53%)
  Pallas kernels  16.2 us (22%)
  starting transfers between devices  15.6 us (21%)
    ppermute x12, waiting for transfers between devices, exchange(): return lax.ppermute(values, 'vel', [(v, v ^ flip) for v in range(32)])  29.5 us
    ppermute x12, starting transfers between devices, exchange(): return lax.ppermute(values, 'vel', [(v, v ^ flip) for v in range(32)])  9.17 us
    ppermute x6, waiting for transfers between devices, shift(): return lax.ppermute(values, ('vel', 'gy'), pairs)  9.04 us
    pallas_call x2, Pallas kernels, move_call(): pl.pallas_call(move_kernel, out_shape=STATE, in_specs=[SMEM, VMEM, VMEM,...  7.02 us
    ppermute x6, starting transfers between devices, shift(): return lax.ppermute(values, ('vel', 'gy'), pairs)  6.41 us
    pallas_call x2, Pallas kernels, relax_call(): pl.pallas_call(kernel, out_shape=out_shape, in_specs=[SMEM, VMEM, VMEM, V...  5.49 us
    pallas_call x1, Pallas kernels, first_call(): pl.pallas_call(first_kernel, out_shape=(STATE, SUMS, SUMS, HALO, HALO), i...  3.66 us
  transfers between devices with their start and end apart: 18, of which 12 were waited for; matrix products, arithmetic and copies ran while one was open for 0% of the time, Pallas kernels for 10%

profile of v2, /device:TPU:24, one launch (start us, length us, event | category | flops | bytes accessed | tf_op | source)
XLA Modules:
  0.0 71.2 jit_solution(7359807242284173395)
XLA Ops:
  0.0 0.0 copy-start
  0.0 0.7 copy-done
  0.7 3.7 %first.1 = (f32[432,8,128]{2,1,0:T(8,128)S(1)}, f32[14,8,128]{2,1,0:T(8,128)S(1)}, f32[14,8,128]{2,1,0:T(8,128)S(1)}, f32[144,8,128]{2,1,0:T(8,128)S(1)}, f32[144,8,128]{2,1,0:T(8,128)S(1)}) custom-call(s32[2,32]{1,0:T(2,128)S(1)} %copy-done, f32[432,8,128]{2,1,0:T(8,128)} %bitcast.5), custom_call_target="tpu_custom_call" | custom-call | tf_op jit(solution)/shard_map/first/pallas_call | solution.py:380
  4.3 0.1 collective-permute-start
  4.4 1.2 %collective-permute-done = f32[14,8,128]{2,1,0:T(8,128)S(1)} collective-permute-done((f32[14,8,128]{2,1,0:T(8,128)S(1)}, f32[14,8,128]{2,1,0:T(8,128)S(1)}, u32[]{:S(2)}, u32[]{:S(2)}) %collective-permute-start) | collective-permute-done | bytes 57376 | tf_op jit(solution)/shard_map/ppermute | solution.py:429
  5.7 2.0 %collective-permute-start.1 = (f32[7,8,128]{2,1,0:T(8,128)S(1)}, f32[7,8,128]{2,1,0:T(8,128)S(1)}, u32[]{:S(2)}, u32[]{:S(2)}) collective-permute-start(f32[7,8,128]{2,1,0:T(8,128)S(1)} %slice.17), channel_id=1, source_target_pairs={{0,1},{1,2},{2,3},{3,4},{4,5},{5,6},{6,7},{7,0},{8,15},{9,8},{10,9... | collective-permute-start | bytes 86024 | tf_op jit(solution)/shard_map/ppermute | solution.py:425
  7.7 1.9 %collective-permute-start.7 = (f32[144,8,128]{2,1,0:T(8,128)S(1)}, f32[144,8,128]{2,1,0:T(8,128)S(1)}, u32[]{:S(2)}, u32[]{:S(2)}) collective-permute-start(f32[144,8,128]{2,1,0:T(8,128)S(1)} %get-tuple-element.27), channel_id=1, source_target_pairs={{0,1},{1,2},{2,3},{3,4},{4,5},{5,6},{6,7},{7,0},{8,9},{9,10},{10,1... | collective-permute-start | bytes 1769480 | tf_op jit(solution)/shard_map/ppermute | solution.py:425
  9.6 3.9 %collective-permute-done.1 = f32[7,8,128]{2,1,0:T(8,128)S(1)} collective-permute-done((f32[7,8,128]{2,1,0:T(8,128)S(1)}, f32[7,8,128]{2,1,0:T(8,128)S(1)}, u32[]{:S(2)}, u32[]{:S(2)}) %collective-permute-start.1) | collective-permute-done | bytes 28704 | tf_op jit(solution)/shard_map/ppermute | solution.py:425
  13.5 2.3 %collective-permute-start.8 = (f32[144,8,128]{2,1,0:T(8,128)S(1)}, f32[144,8,128]{2,1,0:T(8,128)S(1)}, u32[]{:S(2)}, u32[]{:S(2)}) collective-permute-start(f32[144,8,128]{2,1,0:T(8,128)S(1)} %get-tuple-element.30), channel_id=1, source_target_pairs={{0,7},{1,0},{2,1},{3,2},{4,3},{5,4},{6,5},{7,6},{8,15},{9,8},{10,9... | collective-permute-start | bytes 1769480 | tf_op jit(solution)/shard_map/ppermute | solution.py:425
  15.8 1.5 %collective-permute-start.2 = (f32[7,8,128]{2,1,0:T(8,128)S(1)}, f32[7,8,128]{2,1,0:T(8,128)S(1)}, u32[]{:S(2)}, u32[]{:S(2)}) collective-permute-start(f32[7,8,128]{2,1,0:T(8,128)S(1)} %slice_add_fusion.1), channel_id=1, source_target_pairs={{0,16},{8,24},{16,0},{24,8},{32,48},{40,56},{48,32},{56,40},{64,80... | collective-permute-start | bytes 86024 | tf_op jit(solution)/shard_map/ppermute | solution.py:429
  17.3 2.4 %collective-permute-done.2 = f32[7,8,128]{2,1,0:T(8,128)S(1)} collective-permute-done((f32[7,8,128]{2,1,0:T(8,128)S(1)}, f32[7,8,128]{2,1,0:T(8,128)S(1)}, u32[]{:S(2)}, u32[]{:S(2)}) %collective-permute-start.2) | collective-permute-done | bytes 28704 | tf_op jit(solution)/shard_map/ppermute | solution.py:429
  19.7 2.8 %collective-permute-start.3 = (f32[7,8,128]{2,1,0:T(8,128)S(1)}, f32[7,8,128]{2,1,0:T(8,128)S(1)}, u32[]{:S(2)}, u32[]{:S(2)}) collective-permute-start(f32[7,8,128]{2,1,0:T(8,128)S(1)} %add.38), channel_id=1, source_target_pairs={{0,48},{8,56},{16,32},{24,40},{32,16},{40,24},{48,0},{56,8},{64,11... | collective-permute-start | bytes 86024 | tf_op jit(solution)/shard_map/ppermute | solution.py:429
  22.5 2.3 %collective-permute-done.3 = f32[7,8,128]{2,1,0:T(8,128)S(1)} collective-permute-done((f32[7,8,128]{2,1,0:T(8,128)S(1)}, f32[7,8,128]{2,1,0:T(8,128)S(1)}, u32[]{:S(2)}, u32[]{:S(2)}) %collective-permute-start.3) | collective-permute-done | bytes 28704 | tf_op jit(solution)/shard_map/ppermute | solution.py:429
  24.8 0.7 %collective-permute-start.4 = (f32[7,8,128]{2,1,0:T(8,128)S(1)}, f32[7,8,128]{2,1,0:T(8,128)S(1)}, u32[]{:S(2)}, u32[]{:S(2)}) collective-permute-start(f32[7,8,128]{2,1,0:T(8,128)S(1)} %add.39), channel_id=1, source_target_pairs={{0,64},{8,72},{16,80},{24,88},{32,96},{40,104},{48,112},{56,120},{... | collective-permute-start | bytes 86024 | tf_op jit(solution)/shard_map/ppermute | solution.py:429
  25.5 3.1 %collective-permute-done.4 = f32[7,8,128]{2,1,0:T(8,128)S(1)} collective-permute-done((f32[7,8,128]{2,1,0:T(8,128)S(1)}, f32[7,8,128]{2,1,0:T(8,128)S(1)}, u32[]{:S(2)}, u32[]{:S(2)}) %collective-permute-start.4) | collective-permute-done | bytes 28704 | tf_op jit(solution)/shard_map/ppermute | solution.py:429
  28.7 0.2 collective-permute-start.5
  28.9 4.9 %collective-permute-done.5 = f32[7,8,128]{2,1,0:T(8,128)S(1)} collective-permute-done((f32[7,8,128]{2,1,0:T(8,128)S(1)}, f32[7,8,128]{2,1,0:T(8,128)S(1)}, u32[]{:S(2)}, u32[]{:S(2)}) %collective-permute-start.5) | collective-permute-done | bytes 28704 | tf_op jit(solution)/shard_map/ppermute | solution.py:429
  33.7 0.0 collective-permute-start.6
  33.8 0.0 collective-permute-done.7.up_ref
  33.8 0.0 collective-permute-done.8.down_ref
  33.8 0.0 copy-start.1
  33.8 3.5 %move.2.refs_4_ = f32[432,8,128]{2,1,0:T(8,128)S(1)} custom-call(s32[2,32]{1,0:T(2,128)S(1)} %copy-done, f32[432,8,128]{2,1,0:T(8,128)S(1)} %get-tuple-element.25.f_ref, f32[144,8,128]{2,1,0:T(8,128)S(1)} %collective-permute-done.7.up_ref, f32[144,8,128]{2,1,0:T(8,128)S(1)} %collective-permute-done.8.down_ref), custom_call_target="tpu_custom_call" | custom-call | tf_op jit(solution)/shard_map/move/pallas_call | solution.py:392
  37.3 0.0 collective-permute-done.6.refs_3_
  37.3 0.0 copy-done.1
  37.3 3.3 %middle.1 = (f32[432,8,128]{2,1,0:T(8,128)S(1)}, f32[14,8,128]{2,1,0:T(8,128)S(1)}, f32[14,8,128]{2,1,0:T(8,128)S(1)}, f32[144,8,128]{2,1,0:T(8,128)S(1)}, f32[144,8,128]{2,1,0:T(8,128)S(1)}) custom-call(s32[2,32]{1,0:T(2,128)S(1)} %copy-done, s32[8,128]{1,0:T(8,128)S(1)} %bitcast.3, f32[7,8,128]{2,1,0:T(8,128)S(1)} %add.41.refs_2_, ...), custom_call_target="tpu_custom_call" | custom-call | tf_op jit(solution)/shard_map/middle/pallas_call | solution.py:412
  40.6 0.6 collective-permute-start.9
  41.2 0.9 %collective-permute-done.9 = f32[14,8,128]{2,1,0:T(8,128)S(1)} collective-permute-done((f32[14,8,128]{2,1,0:T(8,128)S(1)}, f32[14,8,128]{2,1,0:T(8,128)S(1)}, u32[]{:S(2)}, u32[]{:S(2)}) %collective-permute-start.9) | collective-permute-done | bytes 57376 | tf_op jit(solution)/shard_map/ppermute | solution.py:429
  42.1 0.1 collective-permute-start.10
  42.2 0.1 collective-permute-start.16
  42.3 5.2 %collective-permute-done.10 = f32[7,8,128]{2,1,0:T(8,128)S(1)} collective-permute-done((f32[7,8,128]{2,1,0:T(8,128)S(1)}, f32[7,8,128]{2,1,0:T(8,128)S(1)}, u32[]{:S(2)}, u32[]{:S(2)}) %collective-permute-start.10) | collective-permute-done | bytes 28704 | tf_op jit(solution)/shard_map/ppermute | solution.py:425
  47.4 0.0 collective-permute-start.17
  47.4 0.4 collective-permute-start.11
  47.8 3.6 %collective-permute-done.11 = f32[7,8,128]{2,1,0:T(8,128)S(1)} collective-permute-done((f32[7,8,128]{2,1,0:T(8,128)S(1)}, f32[7,8,128]{2,1,0:T(8,128)S(1)}, u32[]{:S(2)}, u32[]{:S(2)}) %collective-permute-start.11) | collective-permute-done | bytes 28704 | tf_op jit(solution)/shard_map/ppermute | solution.py:429
  51.4 2.8 %collective-permute-start.12 = (f32[7,8,128]{2,1,0:T(8,128)S(1)}, f32[7,8,128]{2,1,0:T(8,128)S(1)}, u32[]{:S(2)}, u32[]{:S(2)}) collective-permute-start(f32[7,8,128]{2,1,0:T(8,128)S(1)} %add.44), channel_id=1, source_target_pairs={{0,48},{8,56},{16,32},{24,40},{32,16},{40,24},{48,0},{56,8},{64,11... | collective-permute-start | bytes 86024 | tf_op jit(solution)/shard_map/ppermute | solution.py:429
  54.2 2.3 %collective-permute-done.12 = f32[7,8,128]{2,1,0:T(8,128)S(1)} collective-permute-done((f32[7,8,128]{2,1,0:T(8,128)S(1)}, f32[7,8,128]{2,1,0:T(8,128)S(1)}, u32[]{:S(2)}, u32[]{:S(2)}) %collective-permute-start.12) | collective-permute-done | bytes 28704 | tf_op jit(solution)/shard_map/ppermute | solution.py:429
  56.5 0.0 collective-permute-start.13
  56.5 3.9 %collective-permute-done.13 = f32[7,8,128]{2,1,0:T(8,128)S(1)} collective-permute-done((f32[7,8,128]{2,1,0:T(8,128)S(1)}, f32[7,8,128]{2,1,0:T(8,128)S(1)}, u32[]{:S(2)}, u32[]{:S(2)}) %collective-permute-start.13) | collective-permute-done | bytes 28704 | tf_op jit(solution)/shard_map/ppermute | solution.py:429
  60.4 0.1 collective-permute-start.14
  60.5 5.0 %collective-permute-done.14 = f32[7,8,128]{2,1,0:T(8,128)S(1)} collective-permute-done((f32[7,8,128]{2,1,0:T(8,128)S(1)}, f32[7,8,128]{2,1,0:T(8,128)S(1)}, u32[]{:S(2)}, u32[]{:S(2)}) %collective-permute-start.14) | collective-permute-done | bytes 28704 | tf_op jit(solution)/shard_map/ppermute | solution.py:429
  65.5 0.0 collective-permute-start.15
  65.5 0.0 collective-permute-done.16.up_ref
  65.5 0.0 collective-permute-done.17.down_ref
  65.5 3.5 %move.3.refs_4_ = f32[432,8,128]{2,1,0:T(8,128)S(1)} custom-call(s32[2,32]{1,0:T(2,128)S(1)} %copy-done, f32[432,8,128]{2,1,0:T(8,128)S(1)} %get-tuple-element.34.f_ref, f32[144,8,128]{2,1,0:T(8,128)S(1)} %collective-permute-done.16.up_ref, f32[144,8,128]{2,1,0:T(8,128)S(1)} %collective-permute-done.17.down_ref), custom_call_target="tpu_custom_call" | custom-call | tf_op jit(solution)/shard_map/move/pallas_call | solution.py:392
  69.0 0.0 collective-permute-done.15.refs_3_
  69.0 2.2 %last.1 = f32[432,8,128]{2,1,0:T(8,128)} custom-call(s32[2,32]{1,0:T(2,128)S(1)} %copy-done, s32[8,128]{1,0:T(8,128)S(1)} %bitcast.4, f32[7,8,128]{2,1,0:T(8,128)S(1)} %add.47.refs_2_, f32[7,8,128]{2,1,0:T(8,128)S(1)} %collective-permute-done.15.refs_3_, f32[432,8,128]{2,1,0:T(8,128)S(1)} %move.3.refs_4_), custom_call_target="tpu_custom_call" | custom-call | tf_op jit(solution)/shard_map/last/pallas_call | solution.py:412
  (14 shorter events, 0.1 us)
Async XLA Ops:
  0.0 0.7 copy-start
  4.3 1.3 %collective-permute-start = (f32[14,8,128]{2,1,0:T(8,128)S(1)}, f32[14,8,128]{2,1,0:T(8,128)S(1)}, u32[]{:S(2)}, u32[]{:S(2)}) collective-permute-start(f32[14,8,128]{2,1,0:T(8,128)S(1)} %get-tuple-element.24), channel_id=1, source_target_pairs={{0,8},{8,0},{16,24},{24,16},{32,40},{40,32},{48,56},{56,48},{64,72... | collective-permute-start | bytes 172040 | tf_op jit(solution)/shard_map/ppermute | solution.py:429
  5.7 7.8 %collective-permute-start.1 = (f32[7,8,128]{2,1,0:T(8,128)S(1)}, f32[7,8,128]{2,1,0:T(8,128)S(1)}, u32[]{:S(2)}, u32[]{:S(2)}) collective-permute-start(f32[7,8,128]{2,1,0:T(8,128)S(1)} %slice.17), channel_id=1, source_target_pairs={{0,1},{1,2},{2,3},{3,4},{4,5},{5,6},{6,7},{7,0},{8,15},{9,8},{10,9... | collective-permute-start | bytes 86024 | tf_op jit(solution)/shard_map/ppermute | solution.py:425
  7.7 26.1 %collective-permute-start.7 = (f32[144,8,128]{2,1,0:T(8,128)S(1)}, f32[144,8,128]{2,1,0:T(8,128)S(1)}, u32[]{:S(2)}, u32[]{:S(2)}) collective-permute-start(f32[144,8,128]{2,1,0:T(8,128)S(1)} %get-tuple-element.27), channel_id=1, source_target_pairs={{0,1},{1,2},{2,3},{3,4},{4,5},{5,6},{6,7},{7,0},{8,9},{9,10},{10,1... | collective-permute-start | bytes 1769480 | tf_op jit(solution)/shard_map/ppermute | solution.py:425
  13.5 20.3 %collective-permute-start.8 = (f32[144,8,128]{2,1,0:T(8,128)S(1)}, f32[144,8,128]{2,1,0:T(8,128)S(1)}, u32[]{:S(2)}, u32[]{:S(2)}) collective-permute-start(f32[144,8,128]{2,1,0:T(8,128)S(1)} %get-tuple-element.30), channel_id=1, source_target_pairs={{0,7},{1,0},{2,1},{3,2},{4,3},{5,4},{6,5},{7,6},{8,15},{9,8},{10,9... | collective-permute-start | bytes 1769480 | tf_op jit(solution)/shard_map/ppermute | solution.py:425
  15.8 3.9 %collective-permute-start.2 = (f32[7,8,128]{2,1,0:T(8,128)S(1)}, f32[7,8,128]{2,1,0:T(8,128)S(1)}, u32[]{:S(2)}, u32[]{:S(2)}) collective-permute-start(f32[7,8,128]{2,1,0:T(8,128)S(1)} %slice_add_fusion.1), channel_id=1, source_target_pairs={{0,16},{8,24},{16,0},{24,8},{32,48},{40,56},{48,32},{56,40},{64,80... | collective-permute-start | bytes 86024 | tf_op jit(solution)/shard_map/ppermute | solution.py:429
  19.7 5.1 %collective-permute-start.3 = (f32[7,8,128]{2,1,0:T(8,128)S(1)}, f32[7,8,128]{2,1,0:T(8,128)S(1)}, u32[]{:S(2)}, u32[]{:S(2)}) collective-permute-start(f32[7,8,128]{2,1,0:T(8,128)S(1)} %add.38), channel_id=1, source_target_pairs={{0,48},{8,56},{16,32},{24,40},{32,16},{40,24},{48,0},{56,8},{64,11... | collective-permute-start | bytes 86024 | tf_op jit(solution)/shard_map/ppermute | solution.py:429
  24.8 3.9 %collective-permute-start.4 = (f32[7,8,128]{2,1,0:T(8,128)S(1)}, f32[7,8,128]{2,1,0:T(8,128)S(1)}, u32[]{:S(2)}, u32[]{:S(2)}) collective-permute-start(f32[7,8,128]{2,1,0:T(8,128)S(1)} %add.39), channel_id=1, source_target_pairs={{0,64},{8,72},{16,80},{24,88},{32,96},{40,104},{48,112},{56,120},{... | collective-permute-start | bytes 86024 | tf_op jit(solution)/shard_map/ppermute | solution.py:429
  28.7 5.1 %collective-permute-start.5 = (f32[7,8,128]{2,1,0:T(8,128)S(1)}, f32[7,8,128]{2,1,0:T(8,128)S(1)}, u32[]{:S(2)}, u32[]{:S(2)}) collective-permute-start(f32[7,8,128]{2,1,0:T(8,128)S(1)} %add.40), channel_id=1, source_target_pairs={{0,192},{8,200},{16,208},{24,216},{32,224},{40,232},{48,240},{56,2... | collective-permute-start | bytes 86024 | tf_op jit(solution)/shard_map/ppermute | solution.py:429
  33.7 3.6 %collective-permute-start.6 = (f32[7,8,128]{2,1,0:T(8,128)S(1)}, f32[7,8,128]{2,1,0:T(8,128)S(1)}, u32[]{:S(2)}, u32[]{:S(2)}) collective-permute-start(f32[7,8,128]{2,1,0:T(8,128)S(1)} %add.41.refs_2_), channel_id=1, source_target_pairs={{0,8},{8,0},{16,24},{24,16},{32,40},{40,32},{48,56},{56,48},{64,72... | collective-permute-start | bytes 86024 | tf_op jit(solution)/shard_map/ppermute | solution.py:429
  33.8 3.5 %copy-start.1 = (s32[2,4,128]{2,1,0:T(4,128)S(1)}, s32[2,4,128]{2,1,0:T(4,128)}, u32[]{:S(2)}) copy-start(s32[2,4,128]{2,1,0:T(4,128)} %param.4) | copy-start | bytes 12292
  40.6 1.5 %collective-permute-start.9 = (f32[14,8,128]{2,1,0:T(8,128)S(1)}, f32[14,8,128]{2,1,0:T(8,128)S(1)}, u32[]{:S(2)}, u32[]{:S(2)}) collective-permute-start(f32[14,8,128]{2,1,0:T(8,128)S(1)} %get-tuple-element.33), channel_id=1, source_target_pairs={{0,8},{8,0},{16,24},{24,16},{32,40},{40,32},{48,56},{56,48},{64,72... | collective-permute-start | bytes 172040 | tf_op jit(solution)/shard_map/ppermute | solution.py:429
  42.1 5.3 %collective-permute-start.10 = (f32[7,8,128]{2,1,0:T(8,128)S(1)}, f32[7,8,128]{2,1,0:T(8,128)S(1)}, u32[]{:S(2)}, u32[]{:S(2)}) collective-permute-start(f32[7,8,128]{2,1,0:T(8,128)S(1)} %slice.19), channel_id=1, source_target_pairs={{0,1},{1,2},{2,3},{3,4},{4,5},{5,6},{6,7},{7,0},{8,15},{9,8},{10,9... | collective-permute-start | bytes 86024 | tf_op jit(solution)/shard_map/ppermute | solution.py:425
  42.2 23.3 %collective-permute-start.16 = (f32[144,8,128]{2,1,0:T(8,128)S(1)}, f32[144,8,128]{2,1,0:T(8,128)S(1)}, u32[]{:S(2)}, u32[]{:S(2)}) collective-permute-start(f32[144,8,128]{2,1,0:T(8,128)S(1)} %get-tuple-element.36), channel_id=1, source_target_pairs={{0,1},{1,2},{2,3},{3,4},{4,5},{5,6},{6,7},{7,0},{8,9},{9,10},{10,1... | collective-permute-start | bytes 1769480 | tf_op jit(solution)/shard_map/ppermute | solution.py:425
  47.4 18.1 %collective-permute-start.17 = (f32[144,8,128]{2,1,0:T(8,128)S(1)}, f32[144,8,128]{2,1,0:T(8,128)S(1)}, u32[]{:S(2)}, u32[]{:S(2)}) collective-permute-start(f32[144,8,128]{2,1,0:T(8,128)S(1)} %get-tuple-element.39), channel_id=1, source_target_pairs={{0,7},{1,0},{2,1},{3,2},{4,3},{5,4},{6,5},{7,6},{8,15},{9,8},{10,9... | collective-permute-start | bytes 1769480 | tf_op jit(solution)/shard_map/ppermute | solution.py:425
  47.4 4.0 %collective-permute-start.11 = (f32[7,8,128]{2,1,0:T(8,128)S(1)}, f32[7,8,128]{2,1,0:T(8,128)S(1)}, u32[]{:S(2)}, u32[]{:S(2)}) collective-permute-start(f32[7,8,128]{2,1,0:T(8,128)S(1)} %slice_add_fusion), channel_id=1, source_target_pairs={{0,16},{8,24},{16,0},{24,8},{32,48},{40,56},{48,32},{56,40},{64,80... | collective-permute-start | bytes 86024 | tf_op jit(solution)/shard_map/ppermute | solution.py:429
  51.4 5.1 %collective-permute-start.12 = (f32[7,8,128]{2,1,0:T(8,128)S(1)}, f32[7,8,128]{2,1,0:T(8,128)S(1)}, u32[]{:S(2)}, u32[]{:S(2)}) collective-permute-start(f32[7,8,128]{2,1,0:T(8,128)S(1)} %add.44), channel_id=1, source_target_pairs={{0,48},{8,56},{16,32},{24,40},{32,16},{40,24},{48,0},{56,8},{64,11... | collective-permute-start | bytes 86024 | tf_op jit(solution)/shard_map/ppermute | solution.py:429
  56.5 3.9 %collective-permute-start.13 = (f32[7,8,128]{2,1,0:T(8,128)S(1)}, f32[7,8,128]{2,1,0:T(8,128)S(1)}, u32[]{:S(2)}, u32[]{:S(2)}) collective-permute-start(f32[7,8,128]{2,1,0:T(8,128)S(1)} %add.45), channel_id=1, source_target_pairs={{0,64},{8,72},{16,80},{24,88},{32,96},{40,104},{48,112},{56,120},{... | collective-permute-start | bytes 86024 | tf_op jit(solution)/shard_map/ppermute | solution.py:429
  60.4 5.1 %collective-permute-start.14 = (f32[7,8,128]{2,1,0:T(8,128)S(1)}, f32[7,8,128]{2,1,0:T(8,128)S(1)}, u32[]{:S(2)}, u32[]{:S(2)}) collective-permute-start(f32[7,8,128]{2,1,0:T(8,128)S(1)} %add.46), channel_id=1, source_target_pairs={{0,192},{8,200},{16,208},{24,216},{32,224},{40,232},{48,240},{56,2... | collective-permute-start | bytes 86024 | tf_op jit(solution)/shard_map/ppermute | solution.py:429
  65.5 3.6 %collective-permute-start.15 = (f32[7,8,128]{2,1,0:T(8,128)S(1)}, f32[7,8,128]{2,1,0:T(8,128)S(1)}, u32[]{:S(2)}, u32[]{:S(2)}) collective-permute-start(f32[7,8,128]{2,1,0:T(8,128)S(1)} %add.47.refs_2_), channel_id=1, source_target_pairs={{0,8},{8,0},{16,24},{24,16},{32,40},{40,32},{48,56},{56,48},{64,72... | collective-permute-start | bytes 86024 | tf_op jit(solution)/shard_map/ppermute | solution.py:429

commit v3 on v2

--- a/solution.py
+++ b/solution.py
@@ -6,6 +6,7 @@
 from jax.experimental import pallas as pl
 from jax.experimental.pallas import tpu as pltpu
 from jax.sharding import PartitionSpec as P
+
 
 NV1 = 24
 NB = 18
@@ -385,7 +386,7 @@
         scratch_shapes=[ACC, DMAS],
         compiler_params=PARAMS,
         name="first",
-    )(flags, pltpu.with_memory_space_constraint(f, pltpu.HBM))
+    )(pltpu.with_memory_space_constraint(flags, pltpu.HBM), pltpu.with_memory_space_constraint(f, pltpu.HBM))
 
 
 def move_call(flags, f, up, down):
@@ -405,10 +406,10 @@
 
     if last_step:
         out_shape = (jax.ShapeDtypeStruct(STATE.shape, F32),)
-        out_specs, scratch, name = (HBM,), [STATE, TABLE, DMAS], "last"
+        out_specs, scratch = (HBM,), [STATE, TABLE, DMAS]
     else:
         out_shape, out_specs = (STATE, SUMS, SUMS, HALO, HALO), (VMEM,) * 5
-        scratch, name = [ACC, TABLE], "middle"
+        scratch = [ACC, TABLE]
     return pl.pallas_call(
         kernel,
         out_shape=out_shape,
@@ -416,35 +417,37 @@
         out_specs=out_specs,
         scratch_shapes=scratch,
         compiler_params=PARAMS,
-        name=name,
     )(flags, mask, in_vmem(own), in_vmem(other), in_vmem(moved))
 
 
-def shift(values, toward):
-    pairs = [(v * 8 + g, v * 8 + (g + toward(v)) % 8) for v in range(32) for g in range(8)]
+def permute(values, flip, z_shift=None):
+    step = z_shift or (lambda v: 0)
+    pairs = [(v * 8 + g, (v ^ flip) * 8 + (g + step(v)) % 8) for v in range(32) for g in range(8)]
     return lax.ppermute(values, ("vel", "gy"), pairs)
-
-
-def exchange(values, flip):
-    return lax.ppermute(values, "vel", [(v, v ^ flip) for v in range(32)])
 
 
 def tie(value, *others):
     return lax.optimization_barrier((value,) + others)[0]
 
 
+def by_core(v):
+    return 1 if v % 2 == 0 else -1
+
+
 def communicate(flags, f, keep, send, up, down):
-    both = keep + exchange(send, 1)
-    cross = shift(both[NPACK:], lambda v: 1 if v % 2 == 0 else -1)
-    up = shift(tie(up, both), lambda v: 1)
-    mom = both[:NPACK] + cross
-    mom = mom + exchange(mom, 2)
-    down = shift(tie(down, cross), lambda v: -1)
-    mom = mom + exchange(mom, 6)
-    mom = mom + exchange(mom, 8)
+    both = keep + permute(send, 1)
+    mom, cross = both[:NPACK], both[NPACK:]
+    near = permute(mom, 2)
+    side = permute(cross, 0, by_core)
+    diagonal = permute(cross, 2, by_core)
+    up = permute(tie(up, both), 0, lambda v: 1)
+    down = permute(tie(down, both), 0, lambda v: -1)
+    mom = (mom + near) + (side + diagonal)
+    mom = mom + permute(mom, 6)
+    first, second, third = (permute(mom, k) for k in (16, 8, 24))
     moved = move_call(flags, f, tie(up, mom), tie(down, mom))
-    mom = mom + exchange(mom, 24)
-    return mom, exchange(mom, 1), moved
+    mom = (mom + second) + (first + third)
+    return mom, permute(mom, 1), moved
 
 
 def shards(distribution, body_mask, inflow_flags):

time: 72.6 us -> 85 us (1.17)
  the two profiles are of different devices: /device:TPU:24 before, /device:TPU:1 now
where the time goes in v3:
time: 85 us; the launch traced here: 84.9 us
  starting transfers between devices  35.5 us (42%)
  waiting for transfers between devices  32.8 us (39%)
  Pallas kernels  16.3 us (19%)
    ppermute x22, starting transfers between devices, permute(): return lax.ppermute(values, ('vel', 'gy'), pairs)  35.5 us
    ppermute x22, waiting for transfers between devices, permute(): return lax.ppermute(values, ('vel', 'gy'), pairs)  32.8 us
    pallas_call x2, Pallas kernels, move_call(): pl.pallas_call(move_kernel, out_shape=STATE, in_specs=[SMEM, VMEM, VMEM,...  6.83 us
    pallas_call x2, Pallas kernels, relax_call(): pl.pallas_call(kernel, out_shape=out_shape, in_specs=[SMEM, VMEM, VMEM, V...  5.49 us
    pallas_call x1, Pallas kernels, first_call(): pl.pallas_call(first_kernel, out_shape=(STATE, SUMS, SUMS, HALO, HALO), i...  3.94 us
  transfers between devices with their start and end apart: 22, of which 13 were waited for; matrix products, arithmetic and copies ran while one was open for 0% of the time, Pallas kernels for 8%

profile of v3, /device:TPU:1, one launch (start us, length us, event | category | flops | bytes accessed | tf_op | source)
XLA Modules:
  0.0 84.9 jit_solution(18336834562904904120)
XLA Ops:
  0.0 3.9 %first.1 = (f32[432,8,128]{2,1,0:T(8,128)S(1)}, f32[14,8,128]{2,1,0:T(8,128)S(1)}, f32[14,8,128]{2,1,0:T(8,128)S(1)}, f32[144,8,128]{2,1,0:T(8,128)S(1)}, f32[144,8,128]{2,1,0:T(8,128)S(1)}) custom-call(s32[2,32]{1,0:T(2,128)} %refs_0_.3, f32[432,8,128]{2,1,0:T(8,128)} %bitcast.5), custom_call_target="tpu_custom_call" | custom-call | tf_op jit(solution)/shard_map/first/pallas_call | solution.py:381
  3.9 3.3 %collective-permute-start = (f32[14,8,128]{2,1,0:T(8,128)S(1)}, f32[14,8,128]{2,1,0:T(8,128)S(1)}, u32[]{:S(2)}, u32[]{:S(2)}) collective-permute-start(f32[14,8,128]{2,1,0:T(8,128)S(1)} %get-tuple-element.24), channel_id=1, source_target_pairs={{0,8},{1,9},{2,10},{3,11},{4,12},{5,13},{6,14},{7,15},{8,0},{9,1},... | collective-permute-start | bytes 172040 | tf_op jit(solution)/shard_map/ppermute | solution.py:426
  7.2 0.9 %collective-permute-done = f32[14,8,128]{2,1,0:T(8,128)S(1)} collective-permute-done((f32[14,8,128]{2,1,0:T(8,128)S(1)}, f32[14,8,128]{2,1,0:T(8,128)S(1)}, u32[]{:S(2)}, u32[]{:S(2)}) %collective-permute-start) | collective-permute-done | bytes 57376 | tf_op jit(solution)/shard_map/ppermute | solution.py:426
  8.1 0.0 collective-permute-start.9
  8.2 3.9 %collective-permute-start.10 = (f32[144,8,128]{2,1,0:T(8,128)S(1)}, f32[144,8,128]{2,1,0:T(8,128)S(1)}, u32[]{:S(2)}, u32[]{:S(2)}) collective-permute-start(f32[144,8,128]{2,1,0:T(8,128)S(1)} %get-tuple-element.30), channel_id=1, source_target_pairs={{0,7},{1,0},{2,1},{3,2},{4,3},{5,4},{6,5},{7,6},{8,15},{9,8},{10,9... | collective-permute-start | bytes 1769480 | tf_op jit(solution)/shard_map/ppermute | solution.py:426
  12.1 1.2 %collective-permute-start.1 = (f32[7,8,128]{2,1,0:T(8,128)S(1)}, f32[7,8,128]{2,1,0:T(8,128)S(1)}, u32[]{:S(2)}, u32[]{:S(2)}) collective-permute-start(f32[7,8,128]{2,1,0:T(8,128)S(1)} %get-tuple-element.43), channel_id=1, source_target_pairs={{0,16},{1,17},{2,18},{3,19},{4,20},{5,21},{6,22},{7,23},{8,24},{9,... | collective-permute-start | bytes 86024 | tf_op jit(solution)/shard_map/ppermute | solution.py:426
  13.3 1.3 %collective-permute-start.3 = (f32[7,8,128]{2,1,0:T(8,128)S(1)}, f32[7,8,128]{2,1,0:T(8,128)S(1)}, u32[]{:S(2)}, u32[]{:S(2)}) collective-permute-start(f32[7,8,128]{2,1,0:T(8,128)S(1)} %get-tuple-element.44), channel_id=1, source_target_pairs={{0,17},{1,18},{2,19},{3,20},{4,21},{5,22},{6,23},{7,16},{8,31},{9,... | collective-permute-start | bytes 86024 | tf_op jit(solution)/shard_map/ppermute | solution.py:426
  14.7 0.7 collective-permute-start.2
  15.4 0.0 collective-permute-done.1
  15.4 9.6 %collective-permute-done.3 = f32[7,8,128]{2,1,0:T(8,128)S(1)} collective-permute-done((f32[7,8,128]{2,1,0:T(8,128)S(1)}, f32[7,8,128]{2,1,0:T(8,128)S(1)}, u32[]{:S(2)}, u32[]{:S(2)}) %collective-permute-start.3) | collective-permute-done | bytes 28704 | tf_op jit(solution)/shard_map/ppermute | solution.py:426
  25.0 0.6 collective-permute-done.2
  25.7 2.6 %collective-permute-start.4 = (f32[7,8,128]{2,1,0:T(8,128)S(1)}, f32[7,8,128]{2,1,0:T(8,128)S(1)}, u32[]{:S(2)}, u32[]{:S(2)}) collective-permute-start(f32[7,8,128]{2,1,0:T(8,128)S(1)} %add_add_fusion.3), channel_id=1, source_target_pairs={{0,48},{1,49},{2,50},{3,51},{4,52},{5,53},{6,54},{7,55},{8,56},{9,... | collective-permute-start | bytes 86024 | tf_op jit(solution)/shard_map/ppermute | solution.py:426
  28.2 1.4 %collective-permute-done.4 = f32[7,8,128]{2,1,0:T(8,128)S(1)} collective-permute-done((f32[7,8,128]{2,1,0:T(8,128)S(1)}, f32[7,8,128]{2,1,0:T(8,128)S(1)}, u32[]{:S(2)}, u32[]{:S(2)}) %collective-permute-start.4) | collective-permute-done | bytes 28704 | tf_op jit(solution)/shard_map/ppermute | solution.py:426
  29.7 2.7 %collective-permute-start.7 = (f32[7,8,128]{2,1,0:T(8,128)S(1)}, f32[7,8,128]{2,1,0:T(8,128)S(1)}, u32[]{:S(2)}, u32[]{:S(2)}) collective-permute-start(f32[7,8,128]{2,1,0:T(8,128)S(1)} %add.52), channel_id=1, source_target_pairs={{0,192},{1,193},{2,194},{3,195},{4,196},{5,197},{6,198},{7,199},{8... | collective-permute-start | bytes 86024 | tf_op jit(solution)/shard_map/ppermute | solution.py:426
  32.4 0.4 collective-permute-start.6
  32.8 0.3 collective-permute-start.5
  33.1 0.6 collective-permute-done.7
  33.7 3.0 %collective-permute-done.6 = f32[7,8,128]{2,1,0:T(8,128)S(1)} collective-permute-done((f32[7,8,128]{2,1,0:T(8,128)S(1)}, f32[7,8,128]{2,1,0:T(8,128)S(1)}, u32[]{:S(2)}, u32[]{:S(2)}) %collective-permute-start.6) | collective-permute-done | bytes 28704 | tf_op jit(solution)/shard_map/ppermute | solution.py:426
  36.6 0.0 collective-permute-done.5
  36.6 4.6 %collective-permute-start.8 = (f32[7,8,128]{2,1,0:T(8,128)S(1)}, f32[7,8,128]{2,1,0:T(8,128)S(1)}, u32[]{:S(2)}, u32[]{:S(2)}) collective-permute-start(f32[7,8,128]{2,1,0:T(8,128)S(1)} %add_add_fusion.2.refs_2_), channel_id=1, source_target_pairs={{0,8},{1,9},{2,10},{3,11},{4,12},{5,13},{6,14},{7,15},{8,0},{9,1},... | collective-permute-start | bytes 86024 | tf_op jit(solution)/shard_map/ppermute | solution.py:426
  41.2 0.0 collective-permute-done.9.up_ref
  41.2 0.0 collective-permute-done.10.down_ref
  41.2 0.0 copy-start.1
  41.3 3.4 %move.2.refs_4_ = f32[432,8,128]{2,1,0:T(8,128)S(1)} custom-call(s32[2,32]{1,0:T(2,128)S(1)} %copy-done, f32[432,8,128]{2,1,0:T(8,128)S(1)} %get-tuple-element.25.f_ref, f32[144,8,128]{2,1,0:T(8,128)S(1)} %collective-permute-done.9.up_ref, f32[144,8,128]{2,1,0:T(8,128)S(1)} %collective-permute-done.10.down_ref), custom_call_target="tpu_custom_call" | custom-call | tf_op jit(solution)/shard_map/move/pallas_call | solution.py:393
  44.7 0.0 collective-permute-done.8.refs_3_
  44.7 3.3 %shard_map.37 = (f32[432,8,128]{2,1,0:T(8,128)S(1)}, f32[14,8,128]{2,1,0:T(8,128)S(1)}, f32[14,8,128]{2,1,0:T(8,128)S(1)}, f32[144,8,128]{2,1,0:T(8,128)S(1)}, f32[144,8,128]{2,1,0:T(8,128)S(1)}) custom-call(s32[2,32]{1,0:T(2,128)S(1)} %copy-done, s32[8,128]{1,0:T(8,128)S(1)} %bitcast.3, f32[7,8,128]{2,1,0:T(8,128)S(1)} %add_add_fusion.2.refs_2_, ...), custom_call_target="tpu_custom_call" | custom-call | tf_op jit(solution)/shard_map/pallas_call | solution.py:413
  48.0 0.1 collective-permute-start.11
  48.1 1.2 %collective-permute-done.11 = f32[14,8,128]{2,1,0:T(8,128)S(1)} collective-permute-done((f32[14,8,128]{2,1,0:T(8,128)S(1)}, f32[14,8,128]{2,1,0:T(8,128)S(1)}, u32[]{:S(2)}, u32[]{:S(2)}) %collective-permute-start.11) | collective-permute-done | bytes 57376 | tf_op jit(solution)/shard_map/ppermute | solution.py:426
  49.3 0.1 collective-permute-start.20
  49.4 2.7 %collective-permute-start.21 = (f32[144,8,128]{2,1,0:T(8,128)S(1)}, f32[144,8,128]{2,1,0:T(8,128)S(1)}, u32[]{:S(2)}, u32[]{:S(2)}) collective-permute-start(f32[144,8,128]{2,1,0:T(8,128)S(1)} %get-tuple-element.39), channel_id=1, source_target_pairs={{0,7},{1,0},{2,1},{3,2},{4,3},{5,4},{6,5},{7,6},{8,15},{9,8},{10,9... | collective-permute-start | bytes 1769480 | tf_op jit(solution)/shard_map/ppermute | solution.py:426
  52.1 0.0 collective-permute-start.12
  52.1 1.4 %collective-permute-start.14 = (f32[7,8,128]{2,1,0:T(8,128)S(1)}, f32[7,8,128]{2,1,0:T(8,128)S(1)}, u32[]{:S(2)}, u32[]{:S(2)}) collective-permute-start(f32[7,8,128]{2,1,0:T(8,128)S(1)} %get-tuple-element.42), channel_id=1, source_target_pairs={{0,17},{1,18},{2,19},{3,20},{4,21},{5,22},{6,23},{7,16},{8,31},{9,... | collective-permute-start | bytes 86024 | tf_op jit(solution)/shard_map/ppermute | solution.py:426
  53.5 0.8 collective-permute-start.13
  54.4 0.7 collective-permute-done.12
  55.1 9.9 %collective-permute-done.14 = f32[7,8,128]{2,1,0:T(8,128)S(1)} collective-permute-done((f32[7,8,128]{2,1,0:T(8,128)S(1)}, f32[7,8,128]{2,1,0:T(8,128)S(1)}, u32[]{:S(2)}, u32[]{:S(2)}) %collective-permute-start.14) | collective-permute-done | bytes 28704 | tf_op jit(solution)/shard_map/ppermute | solution.py:426
  65.0 0.6 collective-permute-done.13
  65.6 1.9 %collective-permute-start.15 = (f32[7,8,128]{2,1,0:T(8,128)S(1)}, f32[7,8,128]{2,1,0:T(8,128)S(1)}, u32[]{:S(2)}, u32[]{:S(2)}) collective-permute-start(f32[7,8,128]{2,1,0:T(8,128)S(1)} %add_add_fusion.1), channel_id=1, source_target_pairs={{0,48},{1,49},{2,50},{3,51},{4,52},{5,53},{6,54},{7,55},{8,56},{9,... | collective-permute-start | bytes 86024 | tf_op jit(solution)/shard_map/ppermute | solution.py:426
  67.6 2.1 %collective-permute-done.15 = f32[7,8,128]{2,1,0:T(8,128)S(1)} collective-permute-done((f32[7,8,128]{2,1,0:T(8,128)S(1)}, f32[7,8,128]{2,1,0:T(8,128)S(1)}, u32[]{:S(2)}, u32[]{:S(2)}) %collective-permute-start.15) | collective-permute-done | bytes 28704 | tf_op jit(solution)/shard_map/ppermute | solution.py:426
  69.6 1.1 %collective-permute-start.18 = (f32[7,8,128]{2,1,0:T(8,128)S(1)}, f32[7,8,128]{2,1,0:T(8,128)S(1)}, u32[]{:S(2)}, u32[]{:S(2)}) collective-permute-start(f32[7,8,128]{2,1,0:T(8,128)S(1)} %add.60), channel_id=1, source_target_pairs={{0,192},{1,193},{2,194},{3,195},{4,196},{5,197},{6,198},{7,199},{8... | collective-permute-start | bytes 86024 | tf_op jit(solution)/shard_map/ppermute | solution.py:426
  70.8 0.8 collective-permute-start.17
  71.6 1.3 %collective-permute-start.16 = (f32[7,8,128]{2,1,0:T(8,128)S(1)}, f32[7,8,128]{2,1,0:T(8,128)S(1)}, u32[]{:S(2)}, u32[]{:S(2)}) collective-permute-start(f32[7,8,128]{2,1,0:T(8,128)S(1)} %add.60), channel_id=1, source_target_pairs={{0,64},{1,65},{2,66},{3,67},{4,68},{5,69},{6,70},{7,71},{8,72},{9,... | collective-permute-start | bytes 86024 | tf_op jit(solution)/shard_map/ppermute | solution.py:426
  72.9 0.7 collective-permute-done.18
  73.6 1.4 %collective-permute-done.17 = f32[7,8,128]{2,1,0:T(8,128)S(1)} collective-permute-done((f32[7,8,128]{2,1,0:T(8,128)S(1)}, f32[7,8,128]{2,1,0:T(8,128)S(1)}, u32[]{:S(2)}, u32[]{:S(2)}) %collective-permute-start.17) | collective-permute-done | bytes 28704 | tf_op jit(solution)/shard_map/ppermute | solution.py:426
  75.0 0.0 collective-permute-done.16
  75.0 4.0 %collective-permute-start.19 = (f32[7,8,128]{2,1,0:T(8,128)S(1)}, f32[7,8,128]{2,1,0:T(8,128)S(1)}, u32[]{:S(2)}, u32[]{:S(2)}) collective-permute-start(f32[7,8,128]{2,1,0:T(8,128)S(1)} %add_add_fusion.refs_2_), channel_id=1, source_target_pairs={{0,8},{1,9},{2,10},{3,11},{4,12},{5,13},{6,14},{7,15},{8,0},{9,1},... | collective-permute-start | bytes 86024 | tf_op jit(solution)/shard_map/ppermute | solution.py:426
  79.1 3.4 %move.3.refs_4_ = f32[432,8,128]{2,1,0:T(8,128)S(1)} custom-call(s32[2,32]{1,0:T(2,128)S(1)} %copy-done, f32[432,8,128]{2,1,0:T(8,128)S(1)} %get-tuple-element.34.f_ref, f32[144,8,128]{2,1,0:T(8,128)S(1)} %collective-permute-done.20.up_ref, f32[144,8,128]{2,1,0:T(8,128)S(1)} %collective-permute-done.21.down_ref), custom_call_target="tpu_custom_call" | custom-call | tf_op jit(solution)/shard_map/move/pallas_call | solution.py:393
  82.5 0.0 collective-permute-done.19.refs_3_
  82.5 2.2 %shard_map.38 = f32[432,8,128]{2,1,0:T(8,128)} custom-call(s32[2,32]{1,0:T(2,128)S(1)} %copy-done, s32[8,128]{1,0:T(8,128)S(1)} %bitcast.4, f32[7,8,128]{2,1,0:T(8,128)S(1)} %add_add_fusion.refs_2_, f32[7,8,128]{2,1,0:T(8,128)S(1)} %collective-permute-done.19.refs_3_, f32[432,8,128]{2,1,0:T(8,128)S(1)} %move.3.refs_4_), custom_call_target="tpu_custom_call" | custom-call | tf_op jit(solution)/shard_map/pallas_call | solution.py:413
  (15 shorter events, 0.1 us)
Async XLA Ops:
  0.0 41.2 %copy-start = (s32[2,32]{1,0:T(2,128)S(1)}, s32[2,32]{1,0:T(2,128)}, u32[]{:S(2)}) copy-start(s32[2,32]{1,0:T(2,128)} %refs_0_.3) | copy-start | bytes 772
  3.9 4.2 %collective-permute-start = (f32[14,8,128]{2,1,0:T(8,128)S(1)}, f32[14,8,128]{2,1,0:T(8,128)S(1)}, u32[]{:S(2)}, u32[]{:S(2)}) collective-permute-start(f32[14,8,128]{2,1,0:T(8,128)S(1)} %get-tuple-element.24), channel_id=1, source_target_pairs={{0,8},{1,9},{2,10},{3,11},{4,12},{5,13},{6,14},{7,15},{8,0},{9,1},... | collective-permute-start | bytes 172040 | tf_op jit(solution)/shard_map/ppermute | solution.py:426
  8.1 33.1 %collective-permute-start.9 = (f32[144,8,128]{2,1,0:T(8,128)S(1)}, f32[144,8,128]{2,1,0:T(8,128)S(1)}, u32[]{:S(2)}, u32[]{:S(2)}) collective-permute-start(f32[144,8,128]{2,1,0:T(8,128)S(1)} %get-tuple-element.27), channel_id=1, source_target_pairs={{0,1},{1,2},{2,3},{3,4},{4,5},{5,6},{6,7},{7,0},{8,9},{9,10},{10,1... | collective-permute-start | bytes 1769480 | tf_op jit(solution)/shard_map/ppermute | solution.py:426
  8.2 33.1 %collective-permute-start.10 = (f32[144,8,128]{2,1,0:T(8,128)S(1)}, f32[144,8,128]{2,1,0:T(8,128)S(1)}, u32[]{:S(2)}, u32[]{:S(2)}) collective-permute-start(f32[144,8,128]{2,1,0:T(8,128)S(1)} %get-tuple-element.30), channel_id=1, source_target_pairs={{0,7},{1,0},{2,1},{3,2},{4,3},{5,4},{6,5},{7,6},{8,15},{9,8},{10,9... | collective-permute-start | bytes 1769480 | tf_op jit(solution)/shard_map/ppermute | solution.py:426
  12.1 3.3 %collective-permute-start.1 = (f32[7,8,128]{2,1,0:T(8,128)S(1)}, f32[7,8,128]{2,1,0:T(8,128)S(1)}, u32[]{:S(2)}, u32[]{:S(2)}) collective-permute-start(f32[7,8,128]{2,1,0:T(8,128)S(1)} %get-tuple-element.43), channel_id=1, source_target_pairs={{0,16},{1,17},{2,18},{3,19},{4,20},{5,21},{6,22},{7,23},{8,24},{9,... | collective-permute-start | bytes 86024 | tf_op jit(solution)/shard_map/ppermute | solution.py:426
  13.3 11.7 %collective-permute-start.3 = (f32[7,8,128]{2,1,0:T(8,128)S(1)}, f32[7,8,128]{2,1,0:T(8,128)S(1)}, u32[]{:S(2)}, u32[]{:S(2)}) collective-permute-start(f32[7,8,128]{2,1,0:T(8,128)S(1)} %get-tuple-element.44), channel_id=1, source_target_pairs={{0,17},{1,18},{2,19},{3,20},{4,21},{5,22},{6,23},{7,16},{8,31},{9,... | collective-permute-start | bytes 86024 | tf_op jit(solution)/shard_map/ppermute | solution.py:426
  14.7 11.0 %collective-permute-start.2 = (f32[7,8,128]{2,1,0:T(8,128)S(1)}, f32[7,8,128]{2,1,0:T(8,128)S(1)}, u32[]{:S(2)}, u32[]{:S(2)}) collective-permute-start(f32[7,8,128]{2,1,0:T(8,128)S(1)} %get-tuple-element.44), channel_id=1, source_target_pairs={{0,1},{1,2},{2,3},{3,4},{4,5},{5,6},{6,7},{7,0},{8,15},{9,8},{10,9... | collective-permute-start | bytes 86024 | tf_op jit(solution)/shard_map/ppermute | solution.py:426
  25.7 4.0 %collective-permute-start.4 = (f32[7,8,128]{2,1,0:T(8,128)S(1)}, f32[7,8,128]{2,1,0:T(8,128)S(1)}, u32[]{:S(2)}, u32[]{:S(2)}) collective-permute-start(f32[7,8,128]{2,1,0:T(8,128)S(1)} %add_add_fusion.3), channel_id=1, source_target_pairs={{0,48},{1,49},{2,50},{3,51},{4,52},{5,53},{6,54},{7,55},{8,56},{9,... | collective-permute-start | bytes 86024 | tf_op jit(solution)/shard_map/ppermute | solution.py:426
  29.7 4.0 %collective-permute-start.7 = (f32[7,8,128]{2,1,0:T(8,128)S(1)}, f32[7,8,128]{2,1,0:T(8,128)S(1)}, u32[]{:S(2)}, u32[]{:S(2)}) collective-permute-start(f32[7,8,128]{2,1,0:T(8,128)S(1)} %add.52), channel_id=1, source_target_pairs={{0,192},{1,193},{2,194},{3,195},{4,196},{5,197},{6,198},{7,199},{8... | collective-permute-start | bytes 86024 | tf_op jit(solution)/shard_map/ppermute | solution.py:426
  32.4 4.2 %collective-permute-start.6 = (f32[7,8,128]{2,1,0:T(8,128)S(1)}, f32[7,8,128]{2,1,0:T(8,128)S(1)}, u32[]{:S(2)}, u32[]{:S(2)}) collective-permute-start(f32[7,8,128]{2,1,0:T(8,128)S(1)} %add.52), channel_id=1, source_target_pairs={{0,128},{1,129},{2,130},{3,131},{4,132},{5,133},{6,134},{7,135},{8... | collective-permute-start | bytes 86024 | tf_op jit(solution)/shard_map/ppermute | solution.py:426
  32.8 3.9 %collective-permute-start.5 = (f32[7,8,128]{2,1,0:T(8,128)S(1)}, f32[7,8,128]{2,1,0:T(8,128)S(1)}, u32[]{:S(2)}, u32[]{:S(2)}) collective-permute-start(f32[7,8,128]{2,1,0:T(8,128)S(1)} %add.52), channel_id=1, source_target_pairs={{0,64},{1,65},{2,66},{3,67},{4,68},{5,69},{6,70},{7,71},{8,72},{9,... | collective-permute-start | bytes 86024 | tf_op jit(solution)/shard_map/ppermute | solution.py:426
  36.6 8.0 %collective-permute-start.8 = (f32[7,8,128]{2,1,0:T(8,128)S(1)}, f32[7,8,128]{2,1,0:T(8,128)S(1)}, u32[]{:S(2)}, u32[]{:S(2)}) collective-permute-start(f32[7,8,128]{2,1,0:T(8,128)S(1)} %add_add_fusion.2.refs_2_), channel_id=1, source_target_pairs={{0,8},{1,9},{2,10},{3,11},{4,12},{5,13},{6,14},{7,15},{8,0},{9,1},... | collective-permute-start | bytes 86024 | tf_op jit(solution)/shard_map/ppermute | solution.py:426
  41.2 3.5 %copy-start.1 = (s32[2,4,128]{2,1,0:T(4,128)S(1)}, s32[2,4,128]{2,1,0:T(4,128)}, u32[]{:S(2)}) copy-start(s32[2,4,128]{2,1,0:T(4,128)} %param.4) | copy-start | bytes 12292
  48.0 1.3 %collective-permute-start.11 = (f32[14,8,128]{2,1,0:T(8,128)S(1)}, f32[14,8,128]{2,1,0:T(8,128)S(1)}, u32[]{:S(2)}, u32[]{:S(2)}) collective-permute-start(f32[14,8,128]{2,1,0:T(8,128)S(1)} %get-tuple-element.33), channel_id=1, source_target_pairs={{0,8},{1,9},{2,10},{3,11},{4,12},{5,13},{6,14},{7,15},{8,0},{9,1},... | collective-permute-start | bytes 172040 | tf_op jit(solution)/shard_map/ppermute | solution.py:426
  49.3 29.7 %collective-permute-start.20 = (f32[144,8,128]{2,1,0:T(8,128)S(1)}, f32[144,8,128]{2,1,0:T(8,128)S(1)}, u32[]{:S(2)}, u32[]{:S(2)}) collective-permute-start(f32[144,8,128]{2,1,0:T(8,128)S(1)} %get-tuple-element.36), channel_id=1, source_target_pairs={{0,1},{1,2},{2,3},{3,4},{4,5},{5,6},{6,7},{7,0},{8,9},{9,10},{10,1... | collective-permute-start | bytes 1769480 | tf_op jit(solution)/shard_map/ppermute | solution.py:426
  49.4 29.6 %collective-permute-start.21 = (f32[144,8,128]{2,1,0:T(8,128)S(1)}, f32[144,8,128]{2,1,0:T(8,128)S(1)}, u32[]{:S(2)}, u32[]{:S(2)}) collective-permute-start(f32[144,8,128]{2,1,0:T(8,128)S(1)} %get-tuple-element.39), channel_id=1, source_target_pairs={{0,7},{1,0},{2,1},{3,2},{4,3},{5,4},{6,5},{7,6},{8,15},{9,8},{10,9... | collective-permute-start | bytes 1769480 | tf_op jit(solution)/shard_map/ppermute | solution.py:426
  52.1 3.0 %collective-permute-start.12 = (f32[7,8,128]{2,1,0:T(8,128)S(1)}, f32[7,8,128]{2,1,0:T(8,128)S(1)}, u32[]{:S(2)}, u32[]{:S(2)}) collective-permute-start(f32[7,8,128]{2,1,0:T(8,128)S(1)} %get-tuple-element.41), channel_id=1, source_target_pairs={{0,16},{1,17},{2,18},{3,19},{4,20},{5,21},{6,22},{7,23},{8,24},{9,... | collective-permute-start | bytes 86024 | tf_op jit(solution)/shard_map/ppermute | solution.py:426
  52.1 12.9 %collective-permute-start.14 = (f32[7,8,128]{2,1,0:T(8,128)S(1)}, f32[7,8,128]{2,1,0:T(8,128)S(1)}, u32[]{:S(2)}, u32[]{:S(2)}) collective-permute-start(f32[7,8,128]{2,1,0:T(8,128)S(1)} %get-tuple-element.42), channel_id=1, source_target_pairs={{0,17},{1,18},{2,19},{3,20},{4,21},{5,22},{6,23},{7,16},{8,31},{9,... | collective-permute-start | bytes 86024 | tf_op jit(solution)/shard_map/ppermute | solution.py:426
  53.5 12.1 %collective-permute-start.13 = (f32[7,8,128]{2,1,0:T(8,128)S(1)}, f32[7,8,128]{2,1,0:T(8,128)S(1)}, u32[]{:S(2)}, u32[]{:S(2)}) collective-permute-start(f32[7,8,128]{2,1,0:T(8,128)S(1)} %get-tuple-element.42), channel_id=1, source_target_pairs={{0,1},{1,2},{2,3},{3,4},{4,5},{5,6},{6,7},{7,0},{8,15},{9,8},{10,9... | collective-permute-start | bytes 86024 | tf_op jit(solution)/shard_map/ppermute | solution.py:426
  65.6 4.0 %collective-permute-start.15 = (f32[7,8,128]{2,1,0:T(8,128)S(1)}, f32[7,8,128]{2,1,0:T(8,128)S(1)}, u32[]{:S(2)}, u32[]{:S(2)}) collective-permute-start(f32[7,8,128]{2,1,0:T(8,128)S(1)} %add_add_fusion.1), channel_id=1, source_target_pairs={{0,48},{1,49},{2,50},{3,51},{4,52},{5,53},{6,54},{7,55},{8,56},{9,... | collective-permute-start | bytes 86024 | tf_op jit(solution)/shard_map/ppermute | solution.py:426
  69.6 3.9 %collective-permute-start.18 = (f32[7,8,128]{2,1,0:T(8,128)S(1)}, f32[7,8,128]{2,1,0:T(8,128)S(1)}, u32[]{:S(2)}, u32[]{:S(2)}) collective-permute-start(f32[7,8,128]{2,1,0:T(8,128)S(1)} %add.60), channel_id=1, source_target_pairs={{0,192},{1,193},{2,194},{3,195},{4,196},{5,197},{6,198},{7,199},{8... | collective-permute-start | bytes 86024 | tf_op jit(solution)/shard_map/ppermute | solution.py:426
  70.8 4.2 %collective-permute-start.17 = (f32[7,8,128]{2,1,0:T(8,128)S(1)}, f32[7,8,128]{2,1,0:T(8,128)S(1)}, u32[]{:S(2)}, u32[]{:S(2)}) collective-permute-start(f32[7,8,128]{2,1,0:T(8,128)S(1)} %add.60), channel_id=1, source_target_pairs={{0,128},{1,129},{2,130},{3,131},{4,132},{5,133},{6,134},{7,135},{8... | collective-permute-start | bytes 86024 | tf_op jit(solution)/shard_map/ppermute | solution.py:426
  71.6 3.4 %collective-permute-start.16 = (f32[7,8,128]{2,1,0:T(8,128)S(1)}, f32[7,8,128]{2,1,0:T(8,128)S(1)}, u32[]{:S(2)}, u32[]{:S(2)}) collective-permute-start(f32[7,8,128]{2,1,0:T(8,128)S(1)} %add.60), channel_id=1, source_target_pairs={{0,64},{1,65},{2,66},{3,67},{4,68},{5,69},{6,70},{7,71},{8,72},{9,... | collective-permute-start | bytes 86024 | tf_op jit(solution)/shard_map/ppermute | solution.py:426
  75.0 7.5 %collective-permute-start.19 = (f32[7,8,128]{2,1,0:T(8,128)S(1)}, f32[7,8,128]{2,1,0:T(8,128)S(1)}, u32[]{:S(2)}, u32[]{:S(2)}) collective-permute-start(f32[7,8,128]{2,1,0:T(8,128)S(1)} %add_add_fusion.refs_2_), channel_id=1, source_target_pairs={{0,8},{1,9},{2,10},{3,11},{4,12},{5,13},{6,14},{7,15},{8,0},{9,1},... | collective-permute-start | bytes 86024 | tf_op jit(solution)/shard_map/ppermute | solution.py:426

commit v4 on v3

--- a/solution.py
+++ b/solution.py
@@ -37,11 +37,12 @@
 
 
 def flag_tile(flags_ref, subs, gy):
-    tile = jnp.zeros(SHAPE, jnp.int32)
+    tile = jnp.zeros(SHAPE, F32)
     for plane in range(2):
         for row in range(4):
-            tile = jnp.where(subs == plane * 4 + row, flags_ref[plane, gy * 4 + row], tile)
-    return tile > 0
+            value = flags_ref[plane, gy * 4 + row].astype(F32)
+            tile = jnp.where(subs == plane * 4 + row, value, tile)
+    return tile
 
 
 def weights_of(speed):
@@ -69,26 +70,34 @@
     return up, slot, a_slot
 
 
-def over_blocks(vel, body):
+def over_blocks(vel, body, ways=(True, False), by_right=True, finish=None):
+    def groups(right):
+        def group_loop(group, carry):
+            up, slot, a_slot = group_state(vel, group)
+            for up_now in ways:
+
+                @pl.when(up == up_now)
+                def _(up_now=up_now):
+                    def block_loop(k, c):
+                        body(PER * group + k, slot * SLOT + HALF * k, a_slot, right, up_now)
+                        return c
+
+                    lax.fori_loop(0, PER, block_loop, 0)
+                    if finish is not None:
+                        finish(group, a_slot, right, up_now)
+
+            return carry
+
+        lax.fori_loop(0, NGROUP, group_loop, 0)
+
+    if not by_right:
+        groups(None)
+        return
     for right in (True, False):
 
         @pl.when((vel >= 16) == right)
         def _(right=right):
-            def group_loop(group, carry):
-                up, slot, a_slot = group_state(vel, group)
-                for up_now in (True, False):
-
-                    @pl.when(up == up_now)
-                    def _(up_now=up_now):
-                        def block_loop(k, c):
-                            body(PER * group + k, slot * SLOT + HALF * k, a_slot, right, up_now)
-                            return c
-
-                        lax.fori_loop(0, PER, block_loop, 0)
-
-                return carry
-
-            lax.fori_loop(0, NGROUP, group_loop, 0)
+            groups(right)
 
 
 def inflow_block(speed_x, speed_y):
@@ -136,30 +145,37 @@
     return jnp.where(rows < 2, pltpu.roll(low, 4, 0), pltpu.roll(high, 2, 0))
 
 
-def block_moments(acc_ref, a_slot, z, speed_x, speed_y, lanes, rows, right, up, inflow_rows):
-    weights = x_weights(speed_x, lanes, right, inflow_rows)
-    c0, c1, c2 = weights_of(speed_y)
-    zero = jnp.zeros(SHAPE, F32)
-    v1, v2 = jnp.full(SHAPE, c1, F32), jnp.full(SHAPE, c2, F32)
+def group_moments(acc_ref, z_ref, vel, group, a_slot, lanes, rows, right, up, inflow_rows):
     last = rows == (0 if up else 3)
     head = rows < 2 if up else rows >= 2
-    own1, cross1 = jnp.where(last, zero, v1), jnp.where(last, v1, zero)
-    own2, cross2 = jnp.where(head, zero, v2), jnp.where(head, v2, zero)
-    own, cross = [], []
-    base = weights[3] * inflow_block(speed_x, speed_y) if right else None
-    for k in range(4):
-        ghost = INFLOW_SUMS[k] * base if right and k % 2 == 0 else None
-        swept = sweep_x(z[k], weights, right, ghost)
-        r1 = pltpu.roll(swept, 1 if up else 7, 0)
-        r2 = pltpu.roll(swept, 2 if up else 6, 0)
-        own.append(c0 * swept + own1 * r1 + own2 * r2)
-        cross.append(cross1 * r1 + cross2 * r2)
-    for side, values in enumerate((own, cross)):
-        powers = {}
-        for m, (j, k) in enumerate(ORDERS):
-            powers[j, k] = values[k] if j == 0 else speed_y * powers[j - 1, k]
-            at = a_slot * (2 * NORD) + side * NORD + m
-            acc_ref[at] = acc_ref[at] + powers[j, k]
+    zero = jnp.zeros(SHAPE, F32)
+    weights = x_weights(speeds(vel, PER * group)[0], lanes, right, inflow_rows)
+    total = {}
+    for n in range(PER):
+        j = PER * group + n
+        speed_x, speed_y = speeds(vel, j)
+        c0, c1, c2 = weights_of(speed_y)
+        v1, v2 = jnp.full(SHAPE, c1, F32), jnp.full(SHAPE, c2, F32)
+        own1, cross1 = jnp.where(last, zero, v1), jnp.where(last, v1, zero)
+        own2, cross2 = jnp.where(head, zero, v2), jnp.where(head, v2, zero)
+        own, cross = [], []
+        base = weights[3] * inflow_block(speed_x, speed_y) if right else None
+        for k in range(4):
+            ghost = INFLOW_SUMS[k] * base if right and k % 2 == 0 else None
+            swept = sweep_x(z_ref[4 * j + k], weights, right, ghost)
+            r1 = pltpu.roll(swept, 1 if up else 7, 0)
+            r2 = pltpu.roll(swept, 2 if up else 6, 0)
+            own.append(c0 * swept + own1 * r1 + own2 * r2)
+            cross.append(cross1 * r1 + cross2 * r2)
+        for side, values in enumerate((own, cross)):
+            powers = {}
+            for m, (i, k) in enumerate(ORDERS):
+                powers[i, k] = values[k] if i == 0 else speed_y * powers[i - 1, k]
+                at = side * NORD + m
+                total[at] = total[at] + powers[i, k] if n else powers[i, k]
+    for at, value in total.items():
+        where = a_slot * (2 * NORD) + at
+        acc_ref[where] = acc_ref[where] + value
 
 
 def clear_moments(acc_ref):
@@ -198,19 +214,27 @@
             send_ref[side * NPACK + k] = jnp.where(odd, upper, lower)
 
 
-def first_kernel(flags_ref, f_hbm, f_ref, keep_ref, send_ref, up_ref, down_ref, acc_ref, sems):
+def first_kernel(
+    flags_hbm, f_hbm, f_ref, keep_ref, send_ref, up_ref, down_ref, tiles_ref, flags_ref, acc_ref, z_ref, sems, sem
+):
     def f_copy(j):
         return pltpu.make_async_copy(f_hbm.at[pl.ds(NV1 * j, NV1)], f_ref.at[pl.ds(NV1 * j, NV1)], sems.at[j])
 
+    flags_copy = pltpu.make_async_copy(flags_hbm, flags_ref, sem)
+    flags_copy.start()
     for j in range(NB):
         f_copy(j).start()
     vel, gy = lax.axis_index("vel"), lax.axis_index("gy")
     subs, rows, lanes = iotas()
-    inflow_rows = flag_tile(flags_ref, subs, gy)
     clear_moments(acc_ref)
+    flags_copy.wait()
+    tiles_ref[0] = flag_tile(flags_ref, subs, gy)
+    for at, turn, up in ((1, 7, True), (2, 1, False)):
+        flags = flag_tile(flags_ref, subs, lax.rem(gy + turn, 8))
+        tiles_ref[at] = pack_halo(flags, flags, rows, up)
+    inflow_rows = tiles_ref[0] > 0.5
 
     def body(j, at, a_slot, right, up):
-        speed_x, speed_y = speeds(vel, j)
         out_ref = up_ref if up else down_ref
         f_copy(j).wait()
         z = [jnp.zeros(SHAPE, F32)] * 4
@@ -219,47 +243,63 @@
             high = f_ref[NV1 * j + (NV1 - 1 - c)]
             z = z_sums(z, low, high, c)
             out_ref[at + c] = pack_halo(low, high, rows, up)
-        block_moments(acc_ref, a_slot, z, speed_x, speed_y, lanes, rows, right, up, inflow_rows)
-
-    over_blocks(vel, body)
+        for k in range(4):
+            z_ref[4 * j + k] = z[k]
+
+    def finish(group, a_slot, right, up):
+        group_moments(acc_ref, z_ref, vel, group, a_slot, lanes, rows, right, up, inflow_rows)
+
+    over_blocks(vel, body, finish=finish)
     finish_moments(acc_ref, keep_ref, send_ref, vel, rows)
 
 
-def move_kernel(flags_ref, f_ref, up_ref, down_ref, moved_ref):
-    vel, gy = lax.axis_index("vel"), lax.axis_index("gy")
-    subs, rows, lanes = iotas()
-    own_rows = flag_tile(flags_ref, subs, gy)
-    low_rows = flag_tile(flags_ref, subs, lax.rem(gy + 7, 8)).astype(F32)
-    high_rows = flag_tile(flags_ref, subs, lax.rem(gy + 1, 8)).astype(F32)
-    halo_rows = [pack_halo(r, r, rows, up) > 0.5 for r, up in ((high_rows, False), (low_rows, True))]
+def sweep_kernel(tiles_ref, f_ref, swept_ref):
+    vel = lax.axis_index("vel")
+    _, _, lanes = iotas()
+    inflow_rows = tiles_ref[0] > 0.5
+    for right in (True, False):
+
+        @pl.when((vel >= 16) == right)
+        def _(right=right):
+            def block_loop(j, carry):
+                speed_x, speed_y = speeds(vel, j)
+                weights = x_weights(speed_x, lanes, right, inflow_rows)
+                base = weights[3] * inflow_block(speed_x, speed_y) if right else None
+                for c in range(HALF):
+                    ghost = INFLOW_Z[c] * base if right else None
+                    for v in (c, NV1 - 1 - c):
+                        swept_ref[NV1 * j + v] = sweep_x(f_ref[NV1 * j + v], weights, right, ghost)
+                return carry
+
+            lax.fori_loop(0, NB, block_loop, 0)
+
+
+def move_kernel(up, tiles_ref, swept_ref, halo_ref, moved_ref):
+    vel = lax.axis_index("vel")
+    _, rows, lanes = iotas()
+    inflow_rows = tiles_ref[1 if up else 2] > 0.5
+    last = rows == (0 if up else 3)
+    first = rows == (3 if up else 0)
+    head = rows < 2 if up else rows >= 2
+    s1, s2 = (1, 2) if up else (7, 6)
 
     def body(j, at, a_slot, right, up):
         speed_x, speed_y = speeds(vel, j)
-        in_ref = up_ref if up else down_ref
-        own = x_weights(speed_x, lanes, right, own_rows)
-        out = x_weights(speed_x, lanes, right, halo_rows[up]) if right else own
-        inflow = inflow_block(speed_x, speed_y) if right else None
+        weights = x_weights(speed_x, lanes, right, inflow_rows)
+        base = weights[3] * inflow_block(speed_x, speed_y) if right else None
         c0, c1, c2 = weights_of(speed_y)
-        last = rows == (0 if up else 3)
-        first = rows == (3 if up else 0)
-        head = rows < 2 if up else rows >= 2
-        s1, s2 = (1, 2) if up else (7, 6)
-        own_base = own[3] * inflow if right else None
-        out_base = out[3] * inflow if right else None
         for c in range(HALF):
             h = NV1 - 1 - c
-            ghost = INFLOW_Z[c] * own_base if right else None
-            low = sweep_x(f_ref[NV1 * j + c], own, right, ghost)
-            high = sweep_x(f_ref[NV1 * j + h], own, right, ghost)
-            halo = sweep_x(in_ref[at + c], out, right, INFLOW_Z[c] * out_base if right else None)
+            low, high = swept_ref[NV1 * j + c], swept_ref[NV1 * j + h]
+            halo = sweep_x(halo_ref[at + c], weights, right, INFLOW_Z[c] * base if right else None)
             low1 = pltpu.roll(jnp.where(first, halo, low), s1, 0)
             low2 = pltpu.roll(jnp.where(head, low, halo), s2, 0)
             high1 = jnp.where(last, pltpu.roll(halo, 8 - s1, 0), pltpu.roll(high, s1, 0))
             high2 = jnp.where(head, halo, pltpu.roll(high, s2, 0))
-            moved_ref[NV1 * j + c] = c0 * low + c1 * low1 + c2 * low2
-            moved_ref[NV1 * j + h] = c0 * high + c1 * high1 + c2 * high2
-
-    over_blocks(vel, body)
+            moved_ref[2 * at + c] = c0 * low + c1 * low1 + c2 * low2
+            moved_ref[2 * at + h] = c0 * high + c1 * high1 + c2 * high2
+
+    over_blocks(vel, body, (up,))
 
 
 def unpack_moments(own_ref, other_ref, vel, rows):
@@ -301,17 +341,17 @@
     return scale, ux, uy, uz, 1.0 / temp, skew * qx, skew * qy, skew * qz, damp
 
 
-def relax_kernel(last_step, flags_ref, mask_ref, own_ref, other_ref, moved_ref, *refs):
+def relax_kernel(last_step, tiles_ref, mask_ref, own_ref, other_ref, up_moved_ref, down_moved_ref, *refs):
     if last_step:
         out_hbm, o_ref, z_ref, sems = refs
     else:
-        o_ref, keep_ref, send_ref, up_ref, down_ref, acc_ref, z_ref = refs
+        o_ref, keep_ref, send_ref, up_ref, down_ref, acc_ref, zs_ref, z_ref = refs
 
     def o_copy(j):
         return pltpu.make_async_copy(o_ref.at[pl.ds(NV1 * j, NV1)], out_hbm.at[pl.ds(NV1 * j, NV1)], sems.at[j])
 
-    vel, gy = lax.axis_index("vel"), lax.axis_index("gy")
-    subs, rows, lanes = iotas()
+    vel = lax.axis_index("vel")
+    _, rows, lanes = iotas()
     solid = mask_ref[...] > 0
     mom = unpack_moments(own_ref, other_ref, vel, rows)
     scale, ux, uy, uz, inv_t, qx, qy, qz, damp = cell_values(mom, solid)
@@ -323,7 +363,7 @@
         z_ref[NV1 + c] = cz * qz
         z_ref[2 * NV1 + c] = sq * inv_t
     if not last_step:
-        inflow_rows = flag_tile(flags_ref, subs, gy)
+        inflow_rows = tiles_ref[0] > 0.5
         clear_moments(acc_ref)
 
     def body(j, at, a_slot, right, up):
@@ -334,9 +374,11 @@
         q_xy = cx * qx + cy * qy
         s_xy = sq * inv_t - 5.0
 
+        moved_ref = up_moved_ref if up else down_moved_ref
+
         def relax(c):
             shape = (q_xy + z_ref[NV1 + c]) * (s_xy + z_ref[2 * NV1 + c]) + 1.0
-            return damp * moved_ref[NV1 * j + c] + (e_xy * z_ref[c]) * shape
+            return damp * moved_ref[2 * at + c] + (e_xy * z_ref[c]) * shape
 
         z = [jnp.zeros(SHAPE, F32)] * 4
         for c in range(HALF):
@@ -350,23 +392,29 @@
         if last_step:
             o_copy(j).start()
         else:
-            block_moments(acc_ref, a_slot, z, speed_x, speed_y, lanes, rows, right, up, inflow_rows)
+            for k in range(4):
+                zs_ref[4 * j + k] = z[k]
+
+    def finish(group, a_slot, right, up):
+        group_moments(acc_ref, zs_ref, vel, group, a_slot, lanes, rows, right, up, inflow_rows)
 
     if last_step:
-        lax.fori_loop(0, NB, lambda j, c: (body(j, 0, 0, True, True), c)[1], 0)
+        over_blocks(vel, body, by_right=False)
         for j in range(NB):
             o_copy(j).wait()
     else:
-        over_blocks(vel, body)
+        over_blocks(vel, body, finish=finish)
         finish_moments(acc_ref, keep_ref, send_ref, vel, rows)
 
 
 HBM = pl.BlockSpec(memory_space=pltpu.HBM)
-SMEM = pl.BlockSpec(memory_space=pltpu.SMEM)
 VMEM = pl.BlockSpec(memory_space=pltpu.VMEM)
 SUMS = pltpu.VMEM((2 * NPACK, 8, 128), F32)
 HALO = pltpu.VMEM((2 * SLOT, 8, 128), F32)
+MOVED = pltpu.VMEM((4 * SLOT, 8, 128), F32)
 STATE = pltpu.VMEM((NB * NV1, 8, 128), F32)
+TILES = pltpu.VMEM((3, 8, 128), F32)
+ZSUMS = pltpu.VMEM((4 * NB, 8, 128), F32)
 ACC = pltpu.VMEM((4 * NORD, 8, 128), F32)
 TABLE = pltpu.VMEM((3 * NV1, 8, 128), F32)
 PARAMS = pltpu.CompilerParams(vmem_limit_bytes=12 << 20)
@@ -380,27 +428,41 @@
 def first_call(flags, f):
     return pl.pallas_call(
         first_kernel,
-        out_shape=(STATE, SUMS, SUMS, HALO, HALO),
-        in_specs=[SMEM, HBM],
-        out_specs=(VMEM,) * 5,
-        scratch_shapes=[ACC, DMAS],
+        out_shape=(STATE, SUMS, SUMS, HALO, HALO, TILES),
+        in_specs=[HBM, HBM],
+        out_specs=(VMEM,) * 6,
+        scratch_shapes=[pltpu.SMEM((2, 32), jnp.int32), ACC, ZSUMS, DMAS, pltpu.SemaphoreType.DMA(())],
         compiler_params=PARAMS,
         name="first",
     )(pltpu.with_memory_space_constraint(flags, pltpu.HBM), pltpu.with_memory_space_constraint(f, pltpu.HBM))
 
 
-def move_call(flags, f, up, down):
+def sweep_call(tiles, f):
     return pl.pallas_call(
-        move_kernel,
+        sweep_kernel,
         out_shape=STATE,
-        in_specs=[SMEM, VMEM, VMEM, VMEM],
+        in_specs=[VMEM, VMEM],
         out_specs=VMEM,
         compiler_params=PARAMS,
-        name="move",
-    )(flags, in_vmem(f), in_vmem(up), in_vmem(down))
-
-
-def relax_call(last_step, flags, mask, own, other, moved):
+        name="sweep",
+    )(in_vmem(tiles), in_vmem(f))
+
+
+def move_call(up, tiles, swept, halo):
+    def kernel(*refs):
+        move_kernel(up, *refs)
+
+    return pl.pallas_call(
+        kernel,
+        out_shape=MOVED,
+        in_specs=[VMEM, VMEM, VMEM],
+        out_specs=VMEM,
+        compiler_params=PARAMS,
+        name="rise" if up else "fall",
+    )(in_vmem(tiles), in_vmem(swept), in_vmem(halo))
+
+
+def relax_call(last_step, tiles, mask, own, other, rise, fall):
     def kernel(*refs):
         relax_kernel(last_step, *refs)
 
@@ -409,15 +471,15 @@
         out_specs, scratch = (HBM,), [STATE, TABLE, DMAS]
     else:
         out_shape, out_specs = (STATE, SUMS, SUMS, HALO, HALO), (VMEM,) * 5
-        scratch = [ACC, TABLE]
+        scratch = [ACC, ZSUMS, TABLE]
     return pl.pallas_call(
         kernel,
         out_shape=out_shape,
-        in_specs=[SMEM, VMEM, VMEM, VMEM, VMEM],
+        in_specs=[VMEM] * 6,
         out_specs=out_specs,
         scratch_shapes=scratch,
         compiler_params=PARAMS,
-    )(flags, mask, in_vmem(own), in_vmem(other), in_vmem(moved))
+    )(in_vmem(tiles), mask, in_vmem(own), in_vmem(other), in_vmem(rise), in_vmem(fall))
 
 
 def permute(values, flip, z_shift=None):
@@ -434,7 +496,7 @@
     return 1 if v % 2 == 0 else -1
 
 
-def communicate(flags, f, keep, send, up, down):
+def communicate(tiles, f, keep, send, up, down):
     both = keep + permute(send, 1)
     mom, cross = both[:NPACK], both[NPACK:]
     near = permute(mom, 2)
@@ -443,20 +505,22 @@
     up = permute(tie(up, both), 0, lambda v: 1)
     down = permute(tie(down, both), 0, lambda v: -1)
     mom = (mom + near) + (side + diagonal)
+    swept = sweep_call(tiles, tie(f, mom))
     mom = mom + permute(mom, 6)
     first, second, third = (permute(mom, k) for k in (16, 8, 24))
-    moved = move_call(flags, f, tie(up, mom), tie(down, mom))
+    rise = move_call(True, tiles, swept, tie(up, mom))
     mom = (mom + second) + (first + third)
-    return mom, permute(mom, 1), moved
+    fall = move_call(False, tiles, swept, tie(down, mom))
+    return mom, permute(mom, 1), rise, fall
 
 
 def shards(distribution, body_mask, inflow_flags):
     mask = body_mask.reshape(8, 128)
-    parts = first_call(inflow_flags, distribution.reshape(NB * NV1, 8, 128))
-    own, other, moved = communicate(inflow_flags, *parts)
-    parts = relax_call(False, inflow_flags, mask, own, other, moved)
-    own, other, moved = communicate(inflow_flags, *parts)
-    (out,) = relax_call(True, inflow_flags, mask, own, other, moved)
+    *parts, tiles = first_call(inflow_flags, distribution.reshape(NB * NV1, 8, 128))
+    parts = communicate(tiles, *parts)
+    parts = relax_call(False, tiles, mask, *parts)
+    parts = communicate(tiles, *parts)
+    (out,) = relax_call(True, tiles, mask, *parts)
     return out.reshape(distribution.shape)
 
 

time: 85 us -> 83.4 us (0.981)
  Pallas kernels: 16.3 us -> 14.6 us
    pallas_call x5 -> x9, Pallas kernels: 16.3 us -> 14.6 us  [the longest x4 4.53 us: move_call(): pl.pallas_call(kernel, out_shape=MOVED, in_specs=[VMEM, VMEM, VMEM], out_...]
  transfers between devices with their start and end apart: 22 -> 22, of which waited for: 13 -> 13; matrix products, arithmetic and copies ran while one was open for 0% -> 0% of each run, Pallas kernels for 8% -> 11%
where the time goes in v4:
time: 83.4 us; the launch traced here: 83.3 us
  starting transfers between devices  35.5 us (43%)
  waiting for transfers between devices  32.8 us (39%)
  Pallas kernels  14.6 us (18%)
    ppermute x22, starting transfers between devices, permute(): return lax.ppermute(values, ('vel', 'gy'), pairs)  35.5 us
    ppermute x22, waiting for transfers between devices, permute(): return lax.ppermute(values, ('vel', 'gy'), pairs)  32.8 us
    pallas_call x4, Pallas kernels, move_call(): pl.pallas_call(kernel, out_shape=MOVED, in_specs=[VMEM, VMEM, VMEM], out_...  4.53 us
    pallas_call x2, Pallas kernels, sweep_call(): pl.pallas_call(sweep_kernel, out_shape=STATE, in_specs=[VMEM, VMEM], out_...  4.29 us
    pallas_call x2, Pallas kernels, relax_call(): pl.pallas_call(kernel, out_shape=out_shape, in_specs=[VMEM] * 6, out_spec...  3.51 us
    pallas_call x1, Pallas kernels, first_call(): pl.pallas_call(first_kernel, out_shape=(STATE, SUMS, SUMS, HALO, HALO, TI...  2.25 us
  transfers between devices with their start and end apart: 22, of which 13 were waited for; matrix products, arithmetic and copies ran while one was open for 0% of the time, Pallas kernels for 11%

profile of v4, /device:TPU:1, one launch (start us, length us, event | category | flops | bytes accessed | tf_op | source)
XLA Modules:
  0.0 83.3 jit_solution(839563421081978723)
XLA Ops:
  0.0 2.2 %first.1 = (f32[432,8,128]{2,1,0:T(8,128)S(1)}, f32[14,8,128]{2,1,0:T(8,128)S(1)}, f32[14,8,128]{2,1,0:T(8,128)S(1)}, f32[144,8,128]{2,1,0:T(8,128)S(1)}, f32[14...) custom-call(s32[2,32]{1,0:T(2,128)} %flags_hbm.1, f32[432,8,128]{2,1,0:T(8,128)} %bitcast.5), custom_call_target="tpu_custom_call" | custom-call | tf_op jit(solution)/shard_map/first/pallas_call | solution.py:429
  2.3 3.3 %collective-permute-start = (f32[14,8,128]{2,1,0:T(8,128)S(1)}, f32[14,8,128]{2,1,0:T(8,128)S(1)}, u32[]{:S(2)}, u32[]{:S(2)}) collective-permute-start(f32[14,8,128]{2,1,0:T(8,128)S(1)} %get-tuple-element.28), channel_id=1, source_target_pairs={{0,8},{1,9},{2,10},{3,11},{4,12},{5,13},{6,14},{7,15},{8,0},{9,1},... | collective-permute-start | bytes 172040 | tf_op jit(solution)/shard_map/ppermute | solution.py:488
  5.5 0.9 %collective-permute-done = f32[14,8,128]{2,1,0:T(8,128)S(1)} collective-permute-done((f32[14,8,128]{2,1,0:T(8,128)S(1)}, f32[14,8,128]{2,1,0:T(8,128)S(1)}, u32[]{:S(2)}, u32[]{:S(2)}) %collective-permute-start) | collective-permute-done | bytes 57376 | tf_op jit(solution)/shard_map/ppermute | solution.py:488
  6.4 0.0 collective-permute-start.9
  6.5 3.9 %collective-permute-start.10 = (f32[144,8,128]{2,1,0:T(8,128)S(1)}, f32[144,8,128]{2,1,0:T(8,128)S(1)}, u32[]{:S(2)}, u32[]{:S(2)}) collective-permute-start(f32[144,8,128]{2,1,0:T(8,128)S(1)} %get-tuple-element.35), channel_id=1, source_target_pairs={{0,7},{1,0},{2,1},{3,2},{4,3},{5,4},{6,5},{7,6},{8,15},{9,8},{10,9... | collective-permute-start | bytes 1769480 | tf_op jit(solution)/shard_map/ppermute | solution.py:488
  10.4 1.2 %collective-permute-start.1 = (f32[7,8,128]{2,1,0:T(8,128)S(1)}, f32[7,8,128]{2,1,0:T(8,128)S(1)}, u32[]{:S(2)}, u32[]{:S(2)}) collective-permute-start(f32[7,8,128]{2,1,0:T(8,128)S(1)} %get-tuple-element.49), channel_id=1, source_target_pairs={{0,16},{1,17},{2,18},{3,19},{4,20},{5,21},{6,22},{7,23},{8,24},{9,... | collective-permute-start | bytes 86024 | tf_op jit(solution)/shard_map/ppermute | solution.py:488
  11.6 1.3 %collective-permute-start.3 = (f32[7,8,128]{2,1,0:T(8,128)S(1)}, f32[7,8,128]{2,1,0:T(8,128)S(1)}, u32[]{:S(2)}, u32[]{:S(2)}) collective-permute-start(f32[7,8,128]{2,1,0:T(8,128)S(1)} %get-tuple-element.50), channel_id=1, source_target_pairs={{0,17},{1,18},{2,19},{3,20},{4,21},{5,22},{6,23},{7,16},{8,31},{9,... | collective-permute-start | bytes 86024 | tf_op jit(solution)/shard_map/ppermute | solution.py:488
  13.0 0.7 collective-permute-start.2
  13.7 0.0 collective-permute-done.1
  13.7 9.6 %collective-permute-done.3 = f32[7,8,128]{2,1,0:T(8,128)S(1)} collective-permute-done((f32[7,8,128]{2,1,0:T(8,128)S(1)}, f32[7,8,128]{2,1,0:T(8,128)S(1)}, u32[]{:S(2)}, u32[]{:S(2)}) %collective-permute-start.3) | collective-permute-done | bytes 28704 | tf_op jit(solution)/shard_map/ppermute | solution.py:488
  23.3 0.6 collective-permute-done.2
  23.9 2.6 %collective-permute-start.4 = (f32[7,8,128]{2,1,0:T(8,128)S(1)}, f32[7,8,128]{2,1,0:T(8,128)S(1)}, u32[]{:S(2)}, u32[]{:S(2)}) collective-permute-start(f32[7,8,128]{2,1,0:T(8,128)S(1)} %add_add_fusion.3), channel_id=1, source_target_pairs={{0,48},{1,49},{2,50},{3,51},{4,52},{5,53},{6,54},{7,55},{8,56},{9,... | collective-permute-start | bytes 86024 | tf_op jit(solution)/shard_map/ppermute | solution.py:488
  26.5 1.4 %collective-permute-done.4 = f32[7,8,128]{2,1,0:T(8,128)S(1)} collective-permute-done((f32[7,8,128]{2,1,0:T(8,128)S(1)}, f32[7,8,128]{2,1,0:T(8,128)S(1)}, u32[]{:S(2)}, u32[]{:S(2)}) %collective-permute-start.4) | collective-permute-done | bytes 28704 | tf_op jit(solution)/shard_map/ppermute | solution.py:488
  28.0 2.8 %collective-permute-start.7 = (f32[7,8,128]{2,1,0:T(8,128)S(1)}, f32[7,8,128]{2,1,0:T(8,128)S(1)}, u32[]{:S(2)}, u32[]{:S(2)}) collective-permute-start(f32[7,8,128]{2,1,0:T(8,128)S(1)} %add.52), channel_id=1, source_target_pairs={{0,192},{1,193},{2,194},{3,195},{4,196},{5,197},{6,198},{7,199},{8... | collective-permute-start | bytes 86024 | tf_op jit(solution)/shard_map/ppermute | solution.py:488
  30.7 0.3 collective-permute-start.6
  31.1 0.3 collective-permute-start.5
  31.4 0.6 collective-permute-done.7
  32.0 3.0 %collective-permute-done.6 = f32[7,8,128]{2,1,0:T(8,128)S(1)} collective-permute-done((f32[7,8,128]{2,1,0:T(8,128)S(1)}, f32[7,8,128]{2,1,0:T(8,128)S(1)}, u32[]{:S(2)}, u32[]{:S(2)}) %collective-permute-start.6) | collective-permute-done | bytes 28704 | tf_op jit(solution)/shard_map/ppermute | solution.py:488
  35.0 0.0 collective-permute-done.5
  35.0 4.6 %collective-permute-start.8 = (f32[7,8,128]{2,1,0:T(8,128)S(1)}, f32[7,8,128]{2,1,0:T(8,128)S(1)}, u32[]{:S(2)}, u32[]{:S(2)}) collective-permute-start(f32[7,8,128]{2,1,0:T(8,128)S(1)} %add_add_fusion.2.refs_2_), channel_id=1, source_target_pairs={{0,8},{1,9},{2,10},{3,11},{4,12},{5,13},{6,14},{7,15},{8,0},{9,1},... | collective-permute-start | bytes 86024 | tf_op jit(solution)/shard_map/ppermute | solution.py:488
  39.6 2.1 %sweep.2.refs_1_ = f32[432,8,128]{2,1,0:T(8,128)S(1)} custom-call(f32[3,8,128]{2,1,0:T(8,128)S(1)} %get-tuple-element.26.tiles_ref.refs_0_, f32[432,8,128]{2,1,0:T(8,128)S(1)} %get-tuple-element.30.f_ref), custom_call_target="tpu_custom_call" | custom-call | tf_op jit(solution)/shard_map/sweep/pallas_call | solution.py:441
  41.7 0.0 collective-permute-done.10.refs_2_
  41.7 0.8 rise.2.refs_4_
  42.5 0.0 copy-start
  42.5 1.5 %fall.2.refs_5_ = f32[288,8,128]{2,1,0:T(8,128)S(1)} custom-call(f32[3,8,128]{2,1,0:T(8,128)S(1)} %get-tuple-element.26.tiles_ref.refs_0_, f32[432,8,128]{2,1,0:T(8,128)S(1)} %sweep.2.refs_1_, f32[144,8,128]{2,1,0:T(8,128)S(1)} %collective-permute-done.10.refs_2_), custom_call_target="tpu_custom_call" | custom-call | tf_op jit(solution)/shard_map/fall/pallas_call | solution.py:455
  44.0 1.8 %shard_map.37 = (f32[432,8,128]{2,1,0:T(8,128)S(1)}, f32[14,8,128]{2,1,0:T(8,128)S(1)}, f32[14,8,128]{2,1,0:T(8,128)S(1)}, f32[144,8,128]{2,1,0:T(8,128)S(1)}, f32[144,8,128]{2,1,0:T(8,128)S(1)}) custom-call(f32[3,8,128]{2,1,0:T(8,128)S(1)} %get-tuple-element.26.tiles_ref.refs_0_, s32[8,128]{1,0:T(8,128)S(1)} %bitcast.3, ...), custom_call_target="tpu_custom_call" | custom-call | tf_op jit(solution)/shard_map/pallas_call | solution.py:475
  45.8 0.1 collective-permute-start.11
  45.9 1.2 %collective-permute-done.11 = f32[14,8,128]{2,1,0:T(8,128)S(1)} collective-permute-done((f32[14,8,128]{2,1,0:T(8,128)S(1)}, f32[14,8,128]{2,1,0:T(8,128)S(1)}, u32[]{:S(2)}, u32[]{:S(2)}) %collective-permute-start.11) | collective-permute-done | bytes 57376 | tf_op jit(solution)/shard_map/ppermute | solution.py:488
  47.2 0.1 collective-permute-start.20
  47.3 2.7 %collective-permute-start.21 = (f32[144,8,128]{2,1,0:T(8,128)S(1)}, f32[144,8,128]{2,1,0:T(8,128)S(1)}, u32[]{:S(2)}, u32[]{:S(2)}) collective-permute-start(f32[144,8,128]{2,1,0:T(8,128)S(1)} %get-tuple-element.45), channel_id=1, source_target_pairs={{0,7},{1,0},{2,1},{3,2},{4,3},{5,4},{6,5},{7,6},{8,15},{9,8},{10,9... | collective-permute-start | bytes 1769480 | tf_op jit(solution)/shard_map/ppermute | solution.py:488
  49.9 0.0 collective-permute-start.12
  49.9 1.4 %collective-permute-start.14 = (f32[7,8,128]{2,1,0:T(8,128)S(1)}, f32[7,8,128]{2,1,0:T(8,128)S(1)}, u32[]{:S(2)}, u32[]{:S(2)}) collective-permute-start(f32[7,8,128]{2,1,0:T(8,128)S(1)} %get-tuple-element.48), channel_id=1, source_target_pairs={{0,17},{1,18},{2,19},{3,20},{4,21},{5,22},{6,23},{7,16},{8,31},{9,... | collective-permute-start | bytes 86024 | tf_op jit(solution)/shard_map/ppermute | solution.py:488
  51.4 0.8 collective-permute-start.13
  52.2 0.7 collective-permute-done.12
  52.9 9.9 %collective-permute-done.14 = f32[7,8,128]{2,1,0:T(8,128)S(1)} collective-permute-done((f32[7,8,128]{2,1,0:T(8,128)S(1)}, f32[7,8,128]{2,1,0:T(8,128)S(1)}, u32[]{:S(2)}, u32[]{:S(2)}) %collective-permute-start.14) | collective-permute-done | bytes 28704 | tf_op jit(solution)/shard_map/ppermute | solution.py:488
  62.8 0.6 collective-permute-done.13
  63.4 1.9 %collective-permute-start.15 = (f32[7,8,128]{2,1,0:T(8,128)S(1)}, f32[7,8,128]{2,1,0:T(8,128)S(1)}, u32[]{:S(2)}, u32[]{:S(2)}) collective-permute-start(f32[7,8,128]{2,1,0:T(8,128)S(1)} %add_add_fusion.1), channel_id=1, source_target_pairs={{0,48},{1,49},{2,50},{3,51},{4,52},{5,53},{6,54},{7,55},{8,56},{9,... | collective-permute-start | bytes 86024 | tf_op jit(solution)/shard_map/ppermute | solution.py:488
  65.4 2.1 %collective-permute-done.15 = f32[7,8,128]{2,1,0:T(8,128)S(1)} collective-permute-done((f32[7,8,128]{2,1,0:T(8,128)S(1)}, f32[7,8,128]{2,1,0:T(8,128)S(1)}, u32[]{:S(2)}, u32[]{:S(2)}) %collective-permute-start.15) | collective-permute-done | bytes 28704 | tf_op jit(solution)/shard_map/ppermute | solution.py:488
  67.5 1.2 %collective-permute-start.18 = (f32[7,8,128]{2,1,0:T(8,128)S(1)}, f32[7,8,128]{2,1,0:T(8,128)S(1)}, u32[]{:S(2)}, u32[]{:S(2)}) collective-permute-start(f32[7,8,128]{2,1,0:T(8,128)S(1)} %add.60), channel_id=1, source_target_pairs={{0,192},{1,193},{2,194},{3,195},{4,196},{5,197},{6,198},{7,199},{8... | collective-permute-start | bytes 86024 | tf_op jit(solution)/shard_map/ppermute | solution.py:488
  68.6 0.8 collective-permute-start.17
  69.4 1.3 %collective-permute-start.16 = (f32[7,8,128]{2,1,0:T(8,128)S(1)}, f32[7,8,128]{2,1,0:T(8,128)S(1)}, u32[]{:S(2)}, u32[]{:S(2)}) collective-permute-start(f32[7,8,128]{2,1,0:T(8,128)S(1)} %add.60), channel_id=1, source_target_pairs={{0,64},{1,65},{2,66},{3,67},{4,68},{5,69},{6,70},{7,71},{8,72},{9,... | collective-permute-start | bytes 86024 | tf_op jit(solution)/shard_map/ppermute | solution.py:488
  70.7 0.7 collective-permute-done.18
  71.4 1.5 %collective-permute-done.17 = f32[7,8,128]{2,1,0:T(8,128)S(1)} collective-permute-done((f32[7,8,128]{2,1,0:T(8,128)S(1)}, f32[7,8,128]{2,1,0:T(8,128)S(1)}, u32[]{:S(2)}, u32[]{:S(2)}) %collective-permute-start.17) | collective-permute-done | bytes 28704 | tf_op jit(solution)/shard_map/ppermute | solution.py:488
  72.9 4.0 %collective-permute-start.19 = (f32[7,8,128]{2,1,0:T(8,128)S(1)}, f32[7,8,128]{2,1,0:T(8,128)S(1)}, u32[]{:S(2)}, u32[]{:S(2)}) collective-permute-start(f32[7,8,128]{2,1,0:T(8,128)S(1)} %add_add_fusion.refs_2_), channel_id=1, source_target_pairs={{0,8},{1,9},{2,10},{3,11},{4,12},{5,13},{6,14},{7,15},{8,0},{9,1},... | collective-permute-start | bytes 86024 | tf_op jit(solution)/shard_map/ppermute | solution.py:488
  76.9 2.1 %sweep.3.refs_1_ = f32[432,8,128]{2,1,0:T(8,128)S(1)} custom-call(f32[3,8,128]{2,1,0:T(8,128)S(1)} %get-tuple-element.26.tiles_ref.refs_0_, f32[432,8,128]{2,1,0:T(8,128)S(1)} %get-tuple-element.40.f_ref), custom_call_target="tpu_custom_call" | custom-call | tf_op jit(solution)/shard_map/sweep/pallas_call | solution.py:441
  79.1 0.8 rise.3.refs_4_
  79.9 1.5 %fall.3.refs_5_ = f32[288,8,128]{2,1,0:T(8,128)S(1)} custom-call(f32[3,8,128]{2,1,0:T(8,128)S(1)} %get-tuple-element.26.tiles_ref.refs_0_, f32[432,8,128]{2,1,0:T(8,128)S(1)} %sweep.3.refs_1_, f32[144,8,128]{2,1,0:T(8,128)S(1)} %collective-permute-done.21.refs_2_), custom_call_target="tpu_custom_call" | custom-call | tf_op jit(solution)/shard_map/fall/pallas_call | solution.py:455
  81.4 1.7 %shard_map.38 = f32[432,8,128]{2,1,0:T(8,128)} custom-call(f32[3,8,128]{2,1,0:T(8,128)S(1)} %get-tuple-element.26.tiles_ref.refs_0_, s32[8,128]{1,0:T(8,128)S(1)} %bitcast.4, f32[7,8,128]{2,1,0:T(8,128)S(1)} %add_add_fusion.refs_2_, f32[7,8,128]{2,1,0:T(8,128)S(1)} %collective-permute-done.19.refs_3_, f32[288,8,128]{2,1,0:T(8,128)S(1)} %rise.3.refs_4_, ...), custom_call_target="tpu_custom_call" | custom-call | tf_op jit(solution)/shard_map/pallas_call | solution.py:475
  (17 shorter events, 0.1 us)
Async XLA Ops:
  2.3 4.2 %collective-permute-start = (f32[14,8,128]{2,1,0:T(8,128)S(1)}, f32[14,8,128]{2,1,0:T(8,128)S(1)}, u32[]{:S(2)}, u32[]{:S(2)}) collective-permute-start(f32[14,8,128]{2,1,0:T(8,128)S(1)} %get-tuple-element.28), channel_id=1, source_target_pairs={{0,8},{1,9},{2,10},{3,11},{4,12},{5,13},{6,14},{7,15},{8,0},{9,1},... | collective-permute-start | bytes 172040 | tf_op jit(solution)/shard_map/ppermute | solution.py:488
  6.4 35.3 %collective-permute-start.9 = (f32[144,8,128]{2,1,0:T(8,128)S(1)}, f32[144,8,128]{2,1,0:T(8,128)S(1)}, u32[]{:S(2)}, u32[]{:S(2)}) collective-permute-start(f32[144,8,128]{2,1,0:T(8,128)S(1)} %get-tuple-element.32), channel_id=1, source_target_pairs={{0,1},{1,2},{2,3},{3,4},{4,5},{5,6},{6,7},{7,0},{8,9},{9,10},{10,1... | collective-permute-start | bytes 1769480 | tf_op jit(solution)/shard_map/ppermute | solution.py:488
  6.5 35.2 %collective-permute-start.10 = (f32[144,8,128]{2,1,0:T(8,128)S(1)}, f32[144,8,128]{2,1,0:T(8,128)S(1)}, u32[]{:S(2)}, u32[]{:S(2)}) collective-permute-start(f32[144,8,128]{2,1,0:T(8,128)S(1)} %get-tuple-element.35), channel_id=1, source_target_pairs={{0,7},{1,0},{2,1},{3,2},{4,3},{5,4},{6,5},{7,6},{8,15},{9,8},{10,9... | collective-permute-start | bytes 1769480 | tf_op jit(solution)/shard_map/ppermute | solution.py:488
  10.4 3.3 %collective-permute-start.1 = (f32[7,8,128]{2,1,0:T(8,128)S(1)}, f32[7,8,128]{2,1,0:T(8,128)S(1)}, u32[]{:S(2)}, u32[]{:S(2)}) collective-permute-start(f32[7,8,128]{2,1,0:T(8,128)S(1)} %get-tuple-element.49), channel_id=1, source_target_pairs={{0,16},{1,17},{2,18},{3,19},{4,20},{5,21},{6,22},{7,23},{8,24},{9,... | collective-permute-start | bytes 86024 | tf_op jit(solution)/shard_map/ppermute | solution.py:488
  11.6 11.7 %collective-permute-start.3 = (f32[7,8,128]{2,1,0:T(8,128)S(1)}, f32[7,8,128]{2,1,0:T(8,128)S(1)}, u32[]{:S(2)}, u32[]{:S(2)}) collective-permute-start(f32[7,8,128]{2,1,0:T(8,128)S(1)} %get-tuple-element.50), channel_id=1, source_target_pairs={{0,17},{1,18},{2,19},{3,20},{4,21},{5,22},{6,23},{7,16},{8,31},{9,... | collective-permute-start | bytes 86024 | tf_op jit(solution)/shard_map/ppermute | solution.py:488
  13.0 11.0 %collective-permute-start.2 = (f32[7,8,128]{2,1,0:T(8,128)S(1)}, f32[7,8,128]{2,1,0:T(8,128)S(1)}, u32[]{:S(2)}, u32[]{:S(2)}) collective-permute-start(f32[7,8,128]{2,1,0:T(8,128)S(1)} %get-tuple-element.50), channel_id=1, source_target_pairs={{0,1},{1,2},{2,3},{3,4},{4,5},{5,6},{6,7},{7,0},{8,15},{9,8},{10,9... | collective-permute-start | bytes 86024 | tf_op jit(solution)/shard_map/ppermute | solution.py:488
  23.9 4.0 %collective-permute-start.4 = (f32[7,8,128]{2,1,0:T(8,128)S(1)}, f32[7,8,128]{2,1,0:T(8,128)S(1)}, u32[]{:S(2)}, u32[]{:S(2)}) collective-permute-start(f32[7,8,128]{2,1,0:T(8,128)S(1)} %add_add_fusion.3), channel_id=1, source_target_pairs={{0,48},{1,49},{2,50},{3,51},{4,52},{5,53},{6,54},{7,55},{8,56},{9,... | collective-permute-start | bytes 86024 | tf_op jit(solution)/shard_map/ppermute | solution.py:488
  28.0 4.0 %collective-permute-start.7 = (f32[7,8,128]{2,1,0:T(8,128)S(1)}, f32[7,8,128]{2,1,0:T(8,128)S(1)}, u32[]{:S(2)}, u32[]{:S(2)}) collective-permute-start(f32[7,8,128]{2,1,0:T(8,128)S(1)} %add.52), channel_id=1, source_target_pairs={{0,192},{1,193},{2,194},{3,195},{4,196},{5,197},{6,198},{7,199},{8... | collective-permute-start | bytes 86024 | tf_op jit(solution)/shard_map/ppermute | solution.py:488
  30.7 4.2 %collective-permute-start.6 = (f32[7,8,128]{2,1,0:T(8,128)S(1)}, f32[7,8,128]{2,1,0:T(8,128)S(1)}, u32[]{:S(2)}, u32[]{:S(2)}) collective-permute-start(f32[7,8,128]{2,1,0:T(8,128)S(1)} %add.52), channel_id=1, source_target_pairs={{0,128},{1,129},{2,130},{3,131},{4,132},{5,133},{6,134},{7,135},{8... | collective-permute-start | bytes 86024 | tf_op jit(solution)/shard_map/ppermute | solution.py:488
  31.1 3.9 %collective-permute-start.5 = (f32[7,8,128]{2,1,0:T(8,128)S(1)}, f32[7,8,128]{2,1,0:T(8,128)S(1)}, u32[]{:S(2)}, u32[]{:S(2)}) collective-permute-start(f32[7,8,128]{2,1,0:T(8,128)S(1)} %add.52), channel_id=1, source_target_pairs={{0,64},{1,65},{2,66},{3,67},{4,68},{5,69},{6,70},{7,71},{8,72},{9,... | collective-permute-start | bytes 86024 | tf_op jit(solution)/shard_map/ppermute | solution.py:488
  35.0 9.1 %collective-permute-start.8 = (f32[7,8,128]{2,1,0:T(8,128)S(1)}, f32[7,8,128]{2,1,0:T(8,128)S(1)}, u32[]{:S(2)}, u32[]{:S(2)}) collective-permute-start(f32[7,8,128]{2,1,0:T(8,128)S(1)} %add_add_fusion.2.refs_2_), channel_id=1, source_target_pairs={{0,8},{1,9},{2,10},{3,11},{4,12},{5,13},{6,14},{7,15},{8,0},{9,1},... | collective-permute-start | bytes 86024 | tf_op jit(solution)/shard_map/ppermute | solution.py:488
  42.5 1.5 %copy-start = (s32[2,4,128]{2,1,0:T(4,128)S(1)}, s32[2,4,128]{2,1,0:T(4,128)}, u32[]{:S(2)}) copy-start(s32[2,4,128]{2,1,0:T(4,128)} %param.4) | copy-start | bytes 12292
  45.8 1.3 %collective-permute-start.11 = (f32[14,8,128]{2,1,0:T(8,128)S(1)}, f32[14,8,128]{2,1,0:T(8,128)S(1)}, u32[]{:S(2)}, u32[]{:S(2)}) collective-permute-start(f32[14,8,128]{2,1,0:T(8,128)S(1)} %get-tuple-element.38), channel_id=1, source_target_pairs={{0,8},{1,9},{2,10},{3,11},{4,12},{5,13},{6,14},{7,15},{8,0},{9,1},... | collective-permute-start | bytes 172040 | tf_op jit(solution)/shard_map/ppermute | solution.py:488
  47.2 31.9 %collective-permute-start.20 = (f32[144,8,128]{2,1,0:T(8,128)S(1)}, f32[144,8,128]{2,1,0:T(8,128)S(1)}, u32[]{:S(2)}, u32[]{:S(2)}) collective-permute-start(f32[144,8,128]{2,1,0:T(8,128)S(1)} %get-tuple-element.42), channel_id=1, source_target_pairs={{0,1},{1,2},{2,3},{3,4},{4,5},{5,6},{6,7},{7,0},{8,9},{9,10},{10,1... | collective-permute-start | bytes 1769480 | tf_op jit(solution)/shard_map/ppermute | solution.py:488
  47.3 31.8 %collective-permute-start.21 = (f32[144,8,128]{2,1,0:T(8,128)S(1)}, f32[144,8,128]{2,1,0:T(8,128)S(1)}, u32[]{:S(2)}, u32[]{:S(2)}) collective-permute-start(f32[144,8,128]{2,1,0:T(8,128)S(1)} %get-tuple-element.45), channel_id=1, source_target_pairs={{0,7},{1,0},{2,1},{3,2},{4,3},{5,4},{6,5},{7,6},{8,15},{9,8},{10,9... | collective-permute-start | bytes 1769480 | tf_op jit(solution)/shard_map/ppermute | solution.py:488
  49.9 3.0 %collective-permute-start.12 = (f32[7,8,128]{2,1,0:T(8,128)S(1)}, f32[7,8,128]{2,1,0:T(8,128)S(1)}, u32[]{:S(2)}, u32[]{:S(2)}) collective-permute-start(f32[7,8,128]{2,1,0:T(8,128)S(1)} %get-tuple-element.47), channel_id=1, source_target_pairs={{0,16},{1,17},{2,18},{3,19},{4,20},{5,21},{6,22},{7,23},{8,24},{9,... | collective-permute-start | bytes 86024 | tf_op jit(solution)/shard_map/ppermute | solution.py:488
  49.9 12.9 %collective-permute-start.14 = (f32[7,8,128]{2,1,0:T(8,128)S(1)}, f32[7,8,128]{2,1,0:T(8,128)S(1)}, u32[]{:S(2)}, u32[]{:S(2)}) collective-permute-start(f32[7,8,128]{2,1,0:T(8,128)S(1)} %get-tuple-element.48), channel_id=1, source_target_pairs={{0,17},{1,18},{2,19},{3,20},{4,21},{5,22},{6,23},{7,16},{8,31},{9,... | collective-permute-start | bytes 86024 | tf_op jit(solution)/shard_map/ppermute | solution.py:488
  51.4 12.1 %collective-permute-start.13 = (f32[7,8,128]{2,1,0:T(8,128)S(1)}, f32[7,8,128]{2,1,0:T(8,128)S(1)}, u32[]{:S(2)}, u32[]{:S(2)}) collective-permute-start(f32[7,8,128]{2,1,0:T(8,128)S(1)} %get-tuple-element.48), channel_id=1, source_target_pairs={{0,1},{1,2},{2,3},{3,4},{4,5},{5,6},{6,7},{7,0},{8,15},{9,8},{10,9... | collective-permute-start | bytes 86024 | tf_op jit(solution)/shard_map/ppermute | solution.py:488
  63.4 4.0 %collective-permute-start.15 = (f32[7,8,128]{2,1,0:T(8,128)S(1)}, f32[7,8,128]{2,1,0:T(8,128)S(1)}, u32[]{:S(2)}, u32[]{:S(2)}) collective-permute-start(f32[7,8,128]{2,1,0:T(8,128)S(1)} %add_add_fusion.1), channel_id=1, source_target_pairs={{0,48},{1,49},{2,50},{3,51},{4,52},{5,53},{6,54},{7,55},{8,56},{9,... | collective-permute-start | bytes 86024 | tf_op jit(solution)/shard_map/ppermute | solution.py:488
  67.5 3.9 %collective-permute-start.18 = (f32[7,8,128]{2,1,0:T(8,128)S(1)}, f32[7,8,128]{2,1,0:T(8,128)S(1)}, u32[]{:S(2)}, u32[]{:S(2)}) collective-permute-start(f32[7,8,128]{2,1,0:T(8,128)S(1)} %add.60), channel_id=1, source_target_pairs={{0,192},{1,193},{2,194},{3,195},{4,196},{5,197},{6,198},{7,199},{8... | collective-permute-start | bytes 86024 | tf_op jit(solution)/shard_map/ppermute | solution.py:488
  68.6 4.2 %collective-permute-start.17 = (f32[7,8,128]{2,1,0:T(8,128)S(1)}, f32[7,8,128]{2,1,0:T(8,128)S(1)}, u32[]{:S(2)}, u32[]{:S(2)}) collective-permute-start(f32[7,8,128]{2,1,0:T(8,128)S(1)} %add.60), channel_id=1, source_target_pairs={{0,128},{1,129},{2,130},{3,131},{4,132},{5,133},{6,134},{7,135},{8... | collective-permute-start | bytes 86024 | tf_op jit(solution)/shard_map/ppermute | solution.py:488
  69.4 3.4 %collective-permute-start.16 = (f32[7,8,128]{2,1,0:T(8,128)S(1)}, f32[7,8,128]{2,1,0:T(8,128)S(1)}, u32[]{:S(2)}, u32[]{:S(2)}) collective-permute-start(f32[7,8,128]{2,1,0:T(8,128)S(1)} %add.60), channel_id=1, source_target_pairs={{0,64},{1,65},{2,66},{3,67},{4,68},{5,69},{6,70},{7,71},{8,72},{9,... | collective-permute-start | bytes 86024 | tf_op jit(solution)/shard_map/ppermute | solution.py:488
  72.9 8.5 %collective-permute-start.19 = (f32[7,8,128]{2,1,0:T(8,128)S(1)}, f32[7,8,128]{2,1,0:T(8,128)S(1)}, u32[]{:S(2)}, u32[]{:S(2)}) collective-permute-start(f32[7,8,128]{2,1,0:T(8,128)S(1)} %add_add_fusion.refs_2_), channel_id=1, source_target_pairs={{0,8},{1,9},{2,10},{3,11},{4,12},{5,13},{6,14},{7,15},{8,0},{9,1},... | collective-permute-start | bytes 86024 | tf_op jit(solution)/shard_map/ppermute | solution.py:488

commit v5 on v4

--- a/solution.py
+++ b/solution.py
@@ -78,11 +78,12 @@
 
                 @pl.when(up == up_now)
                 def _(up_now=up_now):
-                    def block_loop(k, c):
-                        body(PER * group + k, slot * SLOT + HALF * k, a_slot, right, up_now)
+                    def block_loop(n, c):
+                        for k in (3 * n, 3 * n + 1, 3 * n + 2):
+                            body(PER * group + k, slot * SLOT + HALF * k, a_slot, right, up_now)
                         return c
 
-                    lax.fori_loop(0, PER, block_loop, 0)
+                    lax.fori_loop(0, PER // 3, block_loop, 0)
                     if finish is not None:
                         finish(group, a_slot, right, up_now)
 
@@ -499,15 +500,15 @@
 def communicate(tiles, f, keep, send, up, down):
     both = keep + permute(send, 1)
     mom, cross = both[:NPACK], both[NPACK:]
-    near = permute(mom, 2)
+    near = permute(mom, 8)
     side = permute(cross, 0, by_core)
-    diagonal = permute(cross, 2, by_core)
+    diagonal = permute(cross, 8, by_core)
     up = permute(tie(up, both), 0, lambda v: 1)
     down = permute(tie(down, both), 0, lambda v: -1)
     mom = (mom + near) + (side + diagonal)
     swept = sweep_call(tiles, tie(f, mom))
-    mom = mom + permute(mom, 6)
-    first, second, third = (permute(mom, k) for k in (16, 8, 24))
+    mom = mom + permute(mom, 24)
+    first, second, third = (permute(mom, k) for k in (4, 2, 6))
     rise = move_call(True, tiles, swept, tie(up, mom))
     mom = (mom + second) + (first + third)
     fall = move_call(False, tiles, swept, tie(down, mom))

time: 83.4 us -> 81.2 us (0.974)
  Pallas kernels: 14.6 us -> 12.4 us
    pallas_call x4, Pallas kernels: 4.53 us -> 2.67 us  [move_call(): pl.pallas_call(kernel, out_shape=MOVED, in_specs=[VMEM, VMEM, VMEM], out_...]
  transfers between devices with their start and end apart: 22 -> 22, of which waited for: 13 -> 13; matrix products, arithmetic and copies ran while one was open for 0% -> 0% of each run, Pallas kernels for 11% -> 9%
where the time goes in v5:
time: 81.2 us; the launch traced here: 81 us
  starting transfers between devices  35.8 us (44%)
  waiting for transfers between devices  32.4 us (40%)
  Pallas kernels  12.4 us (15%)
    ppermute x22, starting transfers between devices, permute(): return lax.ppermute(values, ('vel', 'gy'), pairs)  35.8 us
    ppermute x22, waiting for transfers between devices, permute(): return lax.ppermute(values, ('vel', 'gy'), pairs)  32.4 us
    pallas_call x2, Pallas kernels, sweep_call(): pl.pallas_call(sweep_kernel, out_shape=STATE, in_specs=[VMEM, VMEM], out_...  4.29 us
    pallas_call x2, Pallas kernels, relax_call(): pl.pallas_call(kernel, out_shape=out_shape, in_specs=[VMEM] * 6, out_spec...  3.25 us
    pallas_call x4, Pallas kernels, move_call(): pl.pallas_call(kernel, out_shape=MOVED, in_specs=[VMEM, VMEM, VMEM], out_...  2.67 us
    pallas_call x1, Pallas kernels, first_call(): pl.pallas_call(first_kernel, out_shape=(STATE, SUMS, SUMS, HALO, HALO, TI...  2.18 us
  transfers between devices with their start and end apart: 22, of which 13 were waited for; matrix products, arithmetic and copies ran while one was open for 0% of the time, Pallas kernels for 9%

profile of v5, /device:TPU:1, one launch (start us, length us, event | category | flops | bytes accessed | tf_op | source)
XLA Modules:
  0.0 81.0 jit_solution(5075918632227462592)
XLA Ops:
  0.0 2.2 %first.1 = (f32[432,8,128]{2,1,0:T(8,128)S(1)}, f32[14,8,128]{2,1,0:T(8,128)S(1)}, f32[14,8,128]{2,1,0:T(8,128)S(1)}, f32[144,8,128]{2,1,0:T(8,128)S(1)}, f32[14...) custom-call(s32[2,32]{1,0:T(2,128)} %flags_hbm.1, f32[432,8,128]{2,1,0:T(8,128)} %bitcast.5), custom_call_target="tpu_custom_call" | custom-call | tf_op jit(solution)/shard_map/first/pallas_call | solution.py:430
  2.2 3.3 %collective-permute-start = (f32[14,8,128]{2,1,0:T(8,128)S(1)}, f32[14,8,128]{2,1,0:T(8,128)S(1)}, u32[]{:S(2)}, u32[]{:S(2)}) collective-permute-start(f32[14,8,128]{2,1,0:T(8,128)S(1)} %get-tuple-element.28), channel_id=1, source_target_pairs={{0,8},{1,9},{2,10},{3,11},{4,12},{5,13},{6,14},{7,15},{8,0},{9,1},... | collective-permute-start | bytes 172040 | tf_op jit(solution)/shard_map/ppermute | solution.py:489
  5.5 0.9 %collective-permute-done = f32[14,8,128]{2,1,0:T(8,128)S(1)} collective-permute-done((f32[14,8,128]{2,1,0:T(8,128)S(1)}, f32[14,8,128]{2,1,0:T(8,128)S(1)}, u32[]{:S(2)}, u32[]{:S(2)}) %collective-permute-start) | collective-permute-done | bytes 57376 | tf_op jit(solution)/shard_map/ppermute | solution.py:489
  6.4 0.0 collective-permute-start.9
  6.4 3.9 %collective-permute-start.10 = (f32[144,8,128]{2,1,0:T(8,128)S(1)}, f32[144,8,128]{2,1,0:T(8,128)S(1)}, u32[]{:S(2)}, u32[]{:S(2)}) collective-permute-start(f32[144,8,128]{2,1,0:T(8,128)S(1)} %get-tuple-element.35), channel_id=1, source_target_pairs={{0,7},{1,0},{2,1},{3,2},{4,3},{5,4},{6,5},{7,6},{8,15},{9,8},{10,9... | collective-permute-start | bytes 1769480 | tf_op jit(solution)/shard_map/ppermute | solution.py:489
  10.4 1.3 %collective-permute-start.1 = (f32[7,8,128]{2,1,0:T(8,128)S(1)}, f32[7,8,128]{2,1,0:T(8,128)S(1)}, u32[]{:S(2)}, u32[]{:S(2)}) collective-permute-start(f32[7,8,128]{2,1,0:T(8,128)S(1)} %get-tuple-element.49), channel_id=1, source_target_pairs={{0,64},{1,65},{2,66},{3,67},{4,68},{5,69},{6,70},{7,71},{8,72},{9,... | collective-permute-start | bytes 86024 | tf_op jit(solution)/shard_map/ppermute | solution.py:489
  11.7 1.3 %collective-permute-start.3 = (f32[7,8,128]{2,1,0:T(8,128)S(1)}, f32[7,8,128]{2,1,0:T(8,128)S(1)}, u32[]{:S(2)}, u32[]{:S(2)}) collective-permute-start(f32[7,8,128]{2,1,0:T(8,128)S(1)} %get-tuple-element.50), channel_id=1, source_target_pairs={{0,65},{1,66},{2,67},{3,68},{4,69},{5,70},{6,71},{7,64},{8,79},{9,... | collective-permute-start | bytes 86024 | tf_op jit(solution)/shard_map/ppermute | solution.py:489
  12.9 0.7 collective-permute-start.2
  13.7 0.0 collective-permute-done.1
  13.7 9.6 %collective-permute-done.3 = f32[7,8,128]{2,1,0:T(8,128)S(1)} collective-permute-done((f32[7,8,128]{2,1,0:T(8,128)S(1)}, f32[7,8,128]{2,1,0:T(8,128)S(1)}, u32[]{:S(2)}, u32[]{:S(2)}) %collective-permute-start.3) | collective-permute-done | bytes 28704 | tf_op jit(solution)/shard_map/ppermute | solution.py:489
  23.3 0.6 collective-permute-done.2
  23.9 2.8 %collective-permute-start.4 = (f32[7,8,128]{2,1,0:T(8,128)S(1)}, f32[7,8,128]{2,1,0:T(8,128)S(1)}, u32[]{:S(2)}, u32[]{:S(2)}) collective-permute-start(f32[7,8,128]{2,1,0:T(8,128)S(1)} %add_add_fusion.3), channel_id=1, source_target_pairs={{0,192},{1,193},{2,194},{3,195},{4,196},{5,197},{6,198},{7,199},{8... | collective-permute-start | bytes 86024 | tf_op jit(solution)/shard_map/ppermute | solution.py:489
  26.7 1.3 %collective-permute-done.4 = f32[7,8,128]{2,1,0:T(8,128)S(1)} collective-permute-done((f32[7,8,128]{2,1,0:T(8,128)S(1)}, f32[7,8,128]{2,1,0:T(8,128)S(1)}, u32[]{:S(2)}, u32[]{:S(2)}) %collective-permute-start.4) | collective-permute-done | bytes 28704 | tf_op jit(solution)/shard_map/ppermute | solution.py:489
  28.0 2.5 %collective-permute-start.7 = (f32[7,8,128]{2,1,0:T(8,128)S(1)}, f32[7,8,128]{2,1,0:T(8,128)S(1)}, u32[]{:S(2)}, u32[]{:S(2)}) collective-permute-start(f32[7,8,128]{2,1,0:T(8,128)S(1)} %add.52), channel_id=1, source_target_pairs={{0,48},{1,49},{2,50},{3,51},{4,52},{5,53},{6,54},{7,55},{8,56},{9,... | collective-permute-start | bytes 86024 | tf_op jit(solution)/shard_map/ppermute | solution.py:489
  30.5 0.5 collective-permute-start.6
  31.0 0.3 collective-permute-start.5
  31.3 0.7 collective-permute-done.7
  31.9 2.8 %collective-permute-done.6 = f32[7,8,128]{2,1,0:T(8,128)S(1)} collective-permute-done((f32[7,8,128]{2,1,0:T(8,128)S(1)}, f32[7,8,128]{2,1,0:T(8,128)S(1)}, u32[]{:S(2)}, u32[]{:S(2)}) %collective-permute-start.6) | collective-permute-done | bytes 28704 | tf_op jit(solution)/shard_map/ppermute | solution.py:489
  34.7 4.6 %collective-permute-start.8 = (f32[7,8,128]{2,1,0:T(8,128)S(1)}, f32[7,8,128]{2,1,0:T(8,128)S(1)}, u32[]{:S(2)}, u32[]{:S(2)}) collective-permute-start(f32[7,8,128]{2,1,0:T(8,128)S(1)} %add_add_fusion.2.refs_2_), channel_id=1, source_target_pairs={{0,8},{1,9},{2,10},{3,11},{4,12},{5,13},{6,14},{7,15},{8,0},{9,1},... | collective-permute-start | bytes 86024 | tf_op jit(solution)/shard_map/ppermute | solution.py:489
  39.3 2.1 %sweep.2.refs_1_ = f32[432,8,128]{2,1,0:T(8,128)S(1)} custom-call(f32[3,8,128]{2,1,0:T(8,128)S(1)} %get-tuple-element.26.tiles_ref.refs_0_, f32[432,8,128]{2,1,0:T(8,128)S(1)} %get-tuple-element.30.f_ref), custom_call_target="tpu_custom_call" | custom-call | tf_op jit(solution)/shard_map/sweep/pallas_call | solution.py:442
  41.5 0.0 collective-permute-done.9.refs_2_
  41.5 0.5 rise.2.refs_4_
  42.0 0.0 copy-start
  42.0 0.9 %fall.2.refs_5_ = f32[288,8,128]{2,1,0:T(8,128)S(1)} custom-call(f32[3,8,128]{2,1,0:T(8,128)S(1)} %get-tuple-element.26.tiles_ref.refs_0_, f32[432,8,128]{2,1,0:T(8,128)S(1)} %sweep.2.refs_1_, f32[144,8,128]{2,1,0:T(8,128)S(1)} %collective-permute-done.10.refs_2_), custom_call_target="tpu_custom_call" | custom-call | tf_op jit(solution)/shard_map/fall/pallas_call | solution.py:456
  42.8 0.0 collective-permute-done.8.refs_3_
  42.9 1.6 %shard_map.37 = (f32[432,8,128]{2,1,0:T(8,128)S(1)}, f32[14,8,128]{2,1,0:T(8,128)S(1)}, f32[14,8,128]{2,1,0:T(8,128)S(1)}, f32[144,8,128]{2,1,0:T(8,128)S(1)}, f32[144,8,128]{2,1,0:T(8,128)S(1)}) custom-call(f32[3,8,128]{2,1,0:T(8,128)S(1)} %get-tuple-element.26.tiles_ref.refs_0_, s32[8,128]{1,0:T(8,128)S(1)} %bitcast.3, ...), custom_call_target="tpu_custom_call" | custom-call | tf_op jit(solution)/shard_map/pallas_call | solution.py:476
  44.5 0.1 collective-permute-start.11
  44.6 1.2 %collective-permute-done.11 = f32[14,8,128]{2,1,0:T(8,128)S(1)} collective-permute-done((f32[14,8,128]{2,1,0:T(8,128)S(1)}, f32[14,8,128]{2,1,0:T(8,128)S(1)}, u32[]{:S(2)}, u32[]{:S(2)}) %collective-permute-start.11) | collective-permute-done | bytes 57376 | tf_op jit(solution)/shard_map/ppermute | solution.py:489
  45.8 0.1 collective-permute-start.20
  45.9 2.7 %collective-permute-start.21 = (f32[144,8,128]{2,1,0:T(8,128)S(1)}, f32[144,8,128]{2,1,0:T(8,128)S(1)}, u32[]{:S(2)}, u32[]{:S(2)}) collective-permute-start(f32[144,8,128]{2,1,0:T(8,128)S(1)} %get-tuple-element.45), channel_id=1, source_target_pairs={{0,7},{1,0},{2,1},{3,2},{4,3},{5,4},{6,5},{7,6},{8,15},{9,8},{10,9... | collective-permute-start | bytes 1769480 | tf_op jit(solution)/shard_map/ppermute | solution.py:489
  48.6 0.0 collective-permute-start.12
  48.6 1.4 %collective-permute-start.14 = (f32[7,8,128]{2,1,0:T(8,128)S(1)}, f32[7,8,128]{2,1,0:T(8,128)S(1)}, u32[]{:S(2)}, u32[]{:S(2)}) collective-permute-start(f32[7,8,128]{2,1,0:T(8,128)S(1)} %get-tuple-element.48), channel_id=1, source_target_pairs={{0,65},{1,66},{2,67},{3,68},{4,69},{5,70},{6,71},{7,64},{8,79},{9,... | collective-permute-start | bytes 86024 | tf_op jit(solution)/shard_map/ppermute | solution.py:489
  50.0 0.8 %collective-permute-start.13 = (f32[7,8,128]{2,1,0:T(8,128)S(1)}, f32[7,8,128]{2,1,0:T(8,128)S(1)}, u32[]{:S(2)}, u32[]{:S(2)}) collective-permute-start(f32[7,8,128]{2,1,0:T(8,128)S(1)} %get-tuple-element.48), channel_id=1, source_target_pairs={{0,1},{1,2},{2,3},{3,4},{4,5},{5,6},{6,7},{7,0},{8,15},{9,8},{10,9... | collective-permute-start | bytes 86024 | tf_op jit(solution)/shard_map/ppermute | solution.py:489
  50.9 0.7 collective-permute-done.12
  51.6 9.9 %collective-permute-done.14 = f32[7,8,128]{2,1,0:T(8,128)S(1)} collective-permute-done((f32[7,8,128]{2,1,0:T(8,128)S(1)}, f32[7,8,128]{2,1,0:T(8,128)S(1)}, u32[]{:S(2)}, u32[]{:S(2)}) %collective-permute-start.14) | collective-permute-done | bytes 28704 | tf_op jit(solution)/shard_map/ppermute | solution.py:489
  61.5 0.7 collective-permute-done.13
  62.2 2.2 %collective-permute-start.15 = (f32[7,8,128]{2,1,0:T(8,128)S(1)}, f32[7,8,128]{2,1,0:T(8,128)S(1)}, u32[]{:S(2)}, u32[]{:S(2)}) collective-permute-start(f32[7,8,128]{2,1,0:T(8,128)S(1)} %add_add_fusion.1), channel_id=1, source_target_pairs={{0,192},{1,193},{2,194},{3,195},{4,196},{5,197},{6,198},{7,199},{8... | collective-permute-start | bytes 86024 | tf_op jit(solution)/shard_map/ppermute | solution.py:489
  64.4 1.8 %collective-permute-done.15 = f32[7,8,128]{2,1,0:T(8,128)S(1)} collective-permute-done((f32[7,8,128]{2,1,0:T(8,128)S(1)}, f32[7,8,128]{2,1,0:T(8,128)S(1)}, u32[]{:S(2)}, u32[]{:S(2)}) %collective-permute-start.15) | collective-permute-done | bytes 28704 | tf_op jit(solution)/shard_map/ppermute | solution.py:489
  66.2 1.3 %collective-permute-start.18 = (f32[7,8,128]{2,1,0:T(8,128)S(1)}, f32[7,8,128]{2,1,0:T(8,128)S(1)}, u32[]{:S(2)}, u32[]{:S(2)}) collective-permute-start(f32[7,8,128]{2,1,0:T(8,128)S(1)} %add.60), channel_id=1, source_target_pairs={{0,48},{1,49},{2,50},{3,51},{4,52},{5,53},{6,54},{7,55},{8,56},{9,... | collective-permute-start | bytes 86024 | tf_op jit(solution)/shard_map/ppermute | solution.py:489
  67.5 0.6 collective-permute-start.17
  68.1 1.4 %collective-permute-start.16 = (f32[7,8,128]{2,1,0:T(8,128)S(1)}, f32[7,8,128]{2,1,0:T(8,128)S(1)}, u32[]{:S(2)}, u32[]{:S(2)}) collective-permute-start(f32[7,8,128]{2,1,0:T(8,128)S(1)} %add.60), channel_id=1, source_target_pairs={{0,16},{1,17},{2,18},{3,19},{4,20},{5,21},{6,22},{7,23},{8,24},{9,... | collective-permute-start | bytes 86024 | tf_op jit(solution)/shard_map/ppermute | solution.py:489
  69.5 0.7 collective-permute-done.18
  70.1 1.6 %collective-permute-done.17 = f32[7,8,128]{2,1,0:T(8,128)S(1)} collective-permute-done((f32[7,8,128]{2,1,0:T(8,128)S(1)}, f32[7,8,128]{2,1,0:T(8,128)S(1)}, u32[]{:S(2)}, u32[]{:S(2)}) %collective-permute-start.17) | collective-permute-done | bytes 28704 | tf_op jit(solution)/shard_map/ppermute | solution.py:489
  71.7 4.0 %collective-permute-start.19 = (f32[7,8,128]{2,1,0:T(8,128)S(1)}, f32[7,8,128]{2,1,0:T(8,128)S(1)}, u32[]{:S(2)}, u32[]{:S(2)}) collective-permute-start(f32[7,8,128]{2,1,0:T(8,128)S(1)} %add_add_fusion.refs_2_), channel_id=1, source_target_pairs={{0,8},{1,9},{2,10},{3,11},{4,12},{5,13},{6,14},{7,15},{8,0},{9,1},... | collective-permute-start | bytes 86024 | tf_op jit(solution)/shard_map/ppermute | solution.py:489
  75.7 2.1 %sweep.3.refs_1_ = f32[432,8,128]{2,1,0:T(8,128)S(1)} custom-call(f32[3,8,128]{2,1,0:T(8,128)S(1)} %get-tuple-element.26.tiles_ref.refs_0_, f32[432,8,128]{2,1,0:T(8,128)S(1)} %get-tuple-element.40.f_ref), custom_call_target="tpu_custom_call" | custom-call | tf_op jit(solution)/shard_map/sweep/pallas_call | solution.py:442
  77.9 0.5 rise.3.refs_4_
  78.4 0.9 %fall.3.refs_5_ = f32[288,8,128]{2,1,0:T(8,128)S(1)} custom-call(f32[3,8,128]{2,1,0:T(8,128)S(1)} %get-tuple-element.26.tiles_ref.refs_0_, f32[432,8,128]{2,1,0:T(8,128)S(1)} %sweep.3.refs_1_, f32[144,8,128]{2,1,0:T(8,128)S(1)} %collective-permute-done.21.refs_2_), custom_call_target="tpu_custom_call" | custom-call | tf_op jit(solution)/shard_map/fall/pallas_call | solution.py:456
  79.2 1.6 %shard_map.38 = f32[432,8,128]{2,1,0:T(8,128)} custom-call(f32[3,8,128]{2,1,0:T(8,128)S(1)} %get-tuple-element.26.tiles_ref.refs_0_, s32[8,128]{1,0:T(8,128)S(1)} %bitcast.4, f32[7,8,128]{2,1,0:T(8,128)S(1)} %add_add_fusion.refs_2_, f32[7,8,128]{2,1,0:T(8,128)S(1)} %collective-permute-done.19.refs_3_, f32[288,8,128]{2,1,0:T(8,128)S(1)} %rise.3.refs_4_, ...), custom_call_target="tpu_custom_call" | custom-call | tf_op jit(solution)/shard_map/pallas_call | solution.py:476
  (17 shorter events, 0.1 us)
Async XLA Ops:
  2.2 4.2 %collective-permute-start = (f32[14,8,128]{2,1,0:T(8,128)S(1)}, f32[14,8,128]{2,1,0:T(8,128)S(1)}, u32[]{:S(2)}, u32[]{:S(2)}) collective-permute-start(f32[14,8,128]{2,1,0:T(8,128)S(1)} %get-tuple-element.28), channel_id=1, source_target_pairs={{0,8},{1,9},{2,10},{3,11},{4,12},{5,13},{6,14},{7,15},{8,0},{9,1},... | collective-permute-start | bytes 172040 | tf_op jit(solution)/shard_map/ppermute | solution.py:489
  6.4 35.1 %collective-permute-start.9 = (f32[144,8,128]{2,1,0:T(8,128)S(1)}, f32[144,8,128]{2,1,0:T(8,128)S(1)}, u32[]{:S(2)}, u32[]{:S(2)}) collective-permute-start(f32[144,8,128]{2,1,0:T(8,128)S(1)} %get-tuple-element.32), channel_id=1, source_target_pairs={{0,1},{1,2},{2,3},{3,4},{4,5},{5,6},{6,7},{7,0},{8,9},{9,10},{10,1... | collective-permute-start | bytes 1769480 | tf_op jit(solution)/shard_map/ppermute | solution.py:489
  6.4 35.1 %collective-permute-start.10 = (f32[144,8,128]{2,1,0:T(8,128)S(1)}, f32[144,8,128]{2,1,0:T(8,128)S(1)}, u32[]{:S(2)}, u32[]{:S(2)}) collective-permute-start(f32[144,8,128]{2,1,0:T(8,128)S(1)} %get-tuple-element.35), channel_id=1, source_target_pairs={{0,7},{1,0},{2,1},{3,2},{4,3},{5,4},{6,5},{7,6},{8,15},{9,8},{10,9... | collective-permute-start | bytes 1769480 | tf_op jit(solution)/shard_map/ppermute | solution.py:489
  10.4 3.3 %collective-permute-start.1 = (f32[7,8,128]{2,1,0:T(8,128)S(1)}, f32[7,8,128]{2,1,0:T(8,128)S(1)}, u32[]{:S(2)}, u32[]{:S(2)}) collective-permute-start(f32[7,8,128]{2,1,0:T(8,128)S(1)} %get-tuple-element.49), channel_id=1, source_target_pairs={{0,64},{1,65},{2,66},{3,67},{4,68},{5,69},{6,70},{7,71},{8,72},{9,... | collective-permute-start | bytes 86024 | tf_op jit(solution)/shard_map/ppermute | solution.py:489
  11.7 11.6 %collective-permute-start.3 = (f32[7,8,128]{2,1,0:T(8,128)S(1)}, f32[7,8,128]{2,1,0:T(8,128)S(1)}, u32[]{:S(2)}, u32[]{:S(2)}) collective-permute-start(f32[7,8,128]{2,1,0:T(8,128)S(1)} %get-tuple-element.50), channel_id=1, source_target_pairs={{0,65},{1,66},{2,67},{3,68},{4,69},{5,70},{6,71},{7,64},{8,79},{9,... | collective-permute-start | bytes 86024 | tf_op jit(solution)/shard_map/ppermute | solution.py:489
  12.9 11.0 %collective-permute-start.2 = (f32[7,8,128]{2,1,0:T(8,128)S(1)}, f32[7,8,128]{2,1,0:T(8,128)S(1)}, u32[]{:S(2)}, u32[]{:S(2)}) collective-permute-start(f32[7,8,128]{2,1,0:T(8,128)S(1)} %get-tuple-element.50), channel_id=1, source_target_pairs={{0,1},{1,2},{2,3},{3,4},{4,5},{5,6},{6,7},{7,0},{8,15},{9,8},{10,9... | collective-permute-start | bytes 86024 | tf_op jit(solution)/shard_map/ppermute | solution.py:489
  23.9 4.1 %collective-permute-start.4 = (f32[7,8,128]{2,1,0:T(8,128)S(1)}, f32[7,8,128]{2,1,0:T(8,128)S(1)}, u32[]{:S(2)}, u32[]{:S(2)}) collective-permute-start(f32[7,8,128]{2,1,0:T(8,128)S(1)} %add_add_fusion.3), channel_id=1, source_target_pairs={{0,192},{1,193},{2,194},{3,195},{4,196},{5,197},{6,198},{7,199},{8... | collective-permute-start | bytes 86024 | tf_op jit(solution)/shard_map/ppermute | solution.py:489
  28.0 3.9 %collective-permute-start.7 = (f32[7,8,128]{2,1,0:T(8,128)S(1)}, f32[7,8,128]{2,1,0:T(8,128)S(1)}, u32[]{:S(2)}, u32[]{:S(2)}) collective-permute-start(f32[7,8,128]{2,1,0:T(8,128)S(1)} %add.52), channel_id=1, source_target_pairs={{0,48},{1,49},{2,50},{3,51},{4,52},{5,53},{6,54},{7,55},{8,56},{9,... | collective-permute-start | bytes 86024 | tf_op jit(solution)/shard_map/ppermute | solution.py:489
  30.5 4.2 %collective-permute-start.6 = (f32[7,8,128]{2,1,0:T(8,128)S(1)}, f32[7,8,128]{2,1,0:T(8,128)S(1)}, u32[]{:S(2)}, u32[]{:S(2)}) collective-permute-start(f32[7,8,128]{2,1,0:T(8,128)S(1)} %add.52), channel_id=1, source_target_pairs={{0,32},{1,33},{2,34},{3,35},{4,36},{5,37},{6,38},{7,39},{8,40},{9,... | collective-permute-start | bytes 86024 | tf_op jit(solution)/shard_map/ppermute | solution.py:489
  31.0 3.7 %collective-permute-start.5 = (f32[7,8,128]{2,1,0:T(8,128)S(1)}, f32[7,8,128]{2,1,0:T(8,128)S(1)}, u32[]{:S(2)}, u32[]{:S(2)}) collective-permute-start(f32[7,8,128]{2,1,0:T(8,128)S(1)} %add.52), channel_id=1, source_target_pairs={{0,16},{1,17},{2,18},{3,19},{4,20},{5,21},{6,22},{7,23},{8,24},{9,... | collective-permute-start | bytes 86024 | tf_op jit(solution)/shard_map/ppermute | solution.py:489
  34.7 8.1 %collective-permute-start.8 = (f32[7,8,128]{2,1,0:T(8,128)S(1)}, f32[7,8,128]{2,1,0:T(8,128)S(1)}, u32[]{:S(2)}, u32[]{:S(2)}) collective-permute-start(f32[7,8,128]{2,1,0:T(8,128)S(1)} %add_add_fusion.2.refs_2_), channel_id=1, source_target_pairs={{0,8},{1,9},{2,10},{3,11},{4,12},{5,13},{6,14},{7,15},{8,0},{9,1},... | collective-permute-start | bytes 86024 | tf_op jit(solution)/shard_map/ppermute | solution.py:489
  42.0 0.9 %copy-start = (s32[2,4,128]{2,1,0:T(4,128)S(1)}, s32[2,4,128]{2,1,0:T(4,128)}, u32[]{:S(2)}) copy-start(s32[2,4,128]{2,1,0:T(4,128)} %param.4) | copy-start | bytes 12292
  44.5 1.3 %collective-permute-start.11 = (f32[14,8,128]{2,1,0:T(8,128)S(1)}, f32[14,8,128]{2,1,0:T(8,128)S(1)}, u32[]{:S(2)}, u32[]{:S(2)}) collective-permute-start(f32[14,8,128]{2,1,0:T(8,128)S(1)} %get-tuple-element.38), channel_id=1, source_target_pairs={{0,8},{1,9},{2,10},{3,11},{4,12},{5,13},{6,14},{7,15},{8,0},{9,1},... | collective-permute-start | bytes 172040 | tf_op jit(solution)/shard_map/ppermute | solution.py:489
  45.8 32.0 %collective-permute-start.20 = (f32[144,8,128]{2,1,0:T(8,128)S(1)}, f32[144,8,128]{2,1,0:T(8,128)S(1)}, u32[]{:S(2)}, u32[]{:S(2)}) collective-permute-start(f32[144,8,128]{2,1,0:T(8,128)S(1)} %get-tuple-element.42), channel_id=1, source_target_pairs={{0,1},{1,2},{2,3},{3,4},{4,5},{5,6},{6,7},{7,0},{8,9},{9,10},{10,1... | collective-permute-start | bytes 1769480 | tf_op jit(solution)/shard_map/ppermute | solution.py:489
  45.9 31.9 %collective-permute-start.21 = (f32[144,8,128]{2,1,0:T(8,128)S(1)}, f32[144,8,128]{2,1,0:T(8,128)S(1)}, u32[]{:S(2)}, u32[]{:S(2)}) collective-permute-start(f32[144,8,128]{2,1,0:T(8,128)S(1)} %get-tuple-element.45), channel_id=1, source_target_pairs={{0,7},{1,0},{2,1},{3,2},{4,3},{5,4},{6,5},{7,6},{8,15},{9,8},{10,9... | collective-permute-start | bytes 1769480 | tf_op jit(solution)/shard_map/ppermute | solution.py:489
  48.6 3.0 %collective-permute-start.12 = (f32[7,8,128]{2,1,0:T(8,128)S(1)}, f32[7,8,128]{2,1,0:T(8,128)S(1)}, u32[]{:S(2)}, u32[]{:S(2)}) collective-permute-start(f32[7,8,128]{2,1,0:T(8,128)S(1)} %get-tuple-element.47), channel_id=1, source_target_pairs={{0,64},{1,65},{2,66},{3,67},{4,68},{5,69},{6,70},{7,71},{8,72},{9,... | collective-permute-start | bytes 86024 | tf_op jit(solution)/shard_map/ppermute | solution.py:489
  48.6 12.9 %collective-permute-start.14 = (f32[7,8,128]{2,1,0:T(8,128)S(1)}, f32[7,8,128]{2,1,0:T(8,128)S(1)}, u32[]{:S(2)}, u32[]{:S(2)}) collective-permute-start(f32[7,8,128]{2,1,0:T(8,128)S(1)} %get-tuple-element.48), channel_id=1, source_target_pairs={{0,65},{1,66},{2,67},{3,68},{4,69},{5,70},{6,71},{7,64},{8,79},{9,... | collective-permute-start | bytes 86024 | tf_op jit(solution)/shard_map/ppermute | solution.py:489
  50.0 12.1 %collective-permute-start.13 = (f32[7,8,128]{2,1,0:T(8,128)S(1)}, f32[7,8,128]{2,1,0:T(8,128)S(1)}, u32[]{:S(2)}, u32[]{:S(2)}) collective-permute-start(f32[7,8,128]{2,1,0:T(8,128)S(1)} %get-tuple-element.48), channel_id=1, source_target_pairs={{0,1},{1,2},{2,3},{3,4},{4,5},{5,6},{6,7},{7,0},{8,15},{9,8},{10,9... | collective-permute-start | bytes 86024 | tf_op jit(solution)/shard_map/ppermute | solution.py:489
  62.2 4.0 %collective-permute-start.15 = (f32[7,8,128]{2,1,0:T(8,128)S(1)}, f32[7,8,128]{2,1,0:T(8,128)S(1)}, u32[]{:S(2)}, u32[]{:S(2)}) collective-permute-start(f32[7,8,128]{2,1,0:T(8,128)S(1)} %add_add_fusion.1), channel_id=1, source_target_pairs={{0,192},{1,193},{2,194},{3,195},{4,196},{5,197},{6,198},{7,199},{8... | collective-permute-start | bytes 86024 | tf_op jit(solution)/shard_map/ppermute | solution.py:489
  66.2 3.9 %collective-permute-start.18 = (f32[7,8,128]{2,1,0:T(8,128)S(1)}, f32[7,8,128]{2,1,0:T(8,128)S(1)}, u32[]{:S(2)}, u32[]{:S(2)}) collective-permute-start(f32[7,8,128]{2,1,0:T(8,128)S(1)} %add.60), channel_id=1, source_target_pairs={{0,48},{1,49},{2,50},{3,51},{4,52},{5,53},{6,54},{7,55},{8,56},{9,... | collective-permute-start | bytes 86024 | tf_op jit(solution)/shard_map/ppermute | solution.py:489
  67.5 4.2 %collective-permute-start.17 = (f32[7,8,128]{2,1,0:T(8,128)S(1)}, f32[7,8,128]{2,1,0:T(8,128)S(1)}, u32[]{:S(2)}, u32[]{:S(2)}) collective-permute-start(f32[7,8,128]{2,1,0:T(8,128)S(1)} %add.60), channel_id=1, source_target_pairs={{0,32},{1,33},{2,34},{3,35},{4,36},{5,37},{6,38},{7,39},{8,40},{9,... | collective-permute-start | bytes 86024 | tf_op jit(solution)/shard_map/ppermute | solution.py:489
  68.1 3.6 %collective-permute-start.16 = (f32[7,8,128]{2,1,0:T(8,128)S(1)}, f32[7,8,128]{2,1,0:T(8,128)S(1)}, u32[]{:S(2)}, u32[]{:S(2)}) collective-permute-start(f32[7,8,128]{2,1,0:T(8,128)S(1)} %add.60), channel_id=1, source_target_pairs={{0,16},{1,17},{2,18},{3,19},{4,20},{5,21},{6,22},{7,23},{8,24},{9,... | collective-permute-start | bytes 86024 | tf_op jit(solution)/shard_map/ppermute | solution.py:489
  71.7 7.5 %collective-permute-start.19 = (f32[7,8,128]{2,1,0:T(8,128)S(1)}, f32[7,8,128]{2,1,0:T(8,128)S(1)}, u32[]{:S(2)}, u32[]{:S(2)}) collective-permute-start(f32[7,8,128]{2,1,0:T(8,128)S(1)} %add_add_fusion.refs_2_), channel_id=1, source_target_pairs={{0,8},{1,9},{2,10},{3,11},{4,12},{5,13},{6,14},{7,15},{8,0},{9,1},... | collective-permute-start | bytes 86024 | tf_op jit(solution)/shard_map/ppermute | solution.py:489

commit v6 on v5

--- a/solution.py
+++ b/solution.py
@@ -78,12 +78,12 @@
 
                 @pl.when(up == up_now)
                 def _(up_now=up_now):
-                    def block_loop(n, c):
-                        for k in (3 * n, 3 * n + 1, 3 * n + 2):
+                    def block_loop(c):
+                        for k in range(PER):
                             body(PER * group + k, slot * SLOT + HALF * k, a_slot, right, up_now)
                         return c
 
-                    lax.fori_loop(0, PER // 3, block_loop, 0)
+                    block_loop(0)
                     if finish is not None:
                         finish(group, a_slot, right, up_now)
 

time: 81.2 us -> 80.6 us (level)
  transfers between devices with their start and end apart: 22 -> 22, of which waited for: 13 -> 13; matrix products, arithmetic and copies ran while one was open for 0% -> 0% of each run, Pallas kernels for 9% -> 8%
where the time goes in v6:
time: 80.6 us; the launch traced here: 80.5 us
  starting transfers between devices  36.1 us (45%)
  waiting for transfers between devices  32.4 us (40%)
  Pallas kernels  11.6 us (14%)
    ppermute x22, starting transfers between devices, permute(): return lax.ppermute(values, ('vel', 'gy'), pairs)  36.1 us
    ppermute x22, waiting for transfers between devices, permute(): return lax.ppermute(values, ('vel', 'gy'), pairs)  32.4 us
    pallas_call x2, Pallas kernels, sweep_call(): pl.pallas_call(sweep_kernel, out_shape=STATE, in_specs=[VMEM, VMEM], out_...  4.29 us
    pallas_call x2, Pallas kernels, relax_call(): pl.pallas_call(kernel, out_shape=out_shape, in_specs=[VMEM] * 6, out_spec...  2.97 us
    pallas_call x4, Pallas kernels, move_call(): pl.pallas_call(kernel, out_shape=MOVED, in_specs=[VMEM, VMEM, VMEM], out_...  2.23 us
    pallas_call x1, Pallas kernels, first_call(): pl.pallas_call(first_kernel, out_shape=(STATE, SUMS, SUMS, HALO, HALO, TI...  2.09 us
  transfers between devices with their start and end apart: 22, of which 13 were waited for; matrix products, arithmetic and copies ran while one was open for 0% of the time, Pallas kernels for 8%

profile of v6, /device:TPU:1, one launch (start us, length us, event | category | flops | bytes accessed | tf_op | source)
XLA Modules:
  0.0 80.5 jit_solution(1056305602053952904)
XLA Ops:
  0.0 2.1 %first.1 = (f32[432,8,128]{2,1,0:T(8,128)S(1)}, f32[14,8,128]{2,1,0:T(8,128)S(1)}, f32[14,8,128]{2,1,0:T(8,128)S(1)}, f32[144,8,128]{2,1,0:T(8,128)S(1)}, f32[14...) custom-call(s32[2,32]{1,0:T(2,128)} %flags_hbm.1, f32[432,8,128]{2,1,0:T(8,128)} %bitcast.5), custom_call_target="tpu_custom_call" | custom-call | tf_op jit(solution)/shard_map/first/pallas_call | solution.py:430
  2.1 3.3 %collective-permute-start = (f32[14,8,128]{2,1,0:T(8,128)S(1)}, f32[14,8,128]{2,1,0:T(8,128)S(1)}, u32[]{:S(2)}, u32[]{:S(2)}) collective-permute-start(f32[14,8,128]{2,1,0:T(8,128)S(1)} %get-tuple-element.28), channel_id=1, source_target_pairs={{0,8},{1,9},{2,10},{3,11},{4,12},{5,13},{6,14},{7,15},{8,0},{9,1},... | collective-permute-start | bytes 172040 | tf_op jit(solution)/shard_map/ppermute | solution.py:489
  5.4 0.9 %collective-permute-done = f32[14,8,128]{2,1,0:T(8,128)S(1)} collective-permute-done((f32[14,8,128]{2,1,0:T(8,128)S(1)}, f32[14,8,128]{2,1,0:T(8,128)S(1)}, u32[]{:S(2)}, u32[]{:S(2)}) %collective-permute-start) | collective-permute-done | bytes 57376 | tf_op jit(solution)/shard_map/ppermute | solution.py:489
  6.3 0.0 collective-permute-start.9
  6.3 3.9 %collective-permute-start.10 = (f32[144,8,128]{2,1,0:T(8,128)S(1)}, f32[144,8,128]{2,1,0:T(8,128)S(1)}, u32[]{:S(2)}, u32[]{:S(2)}) collective-permute-start(f32[144,8,128]{2,1,0:T(8,128)S(1)} %get-tuple-element.35), channel_id=1, source_target_pairs={{0,7},{1,0},{2,1},{3,2},{4,3},{5,4},{6,5},{7,6},{8,15},{9,8},{10,9... | collective-permute-start | bytes 1769480 | tf_op jit(solution)/shard_map/ppermute | solution.py:489
  10.3 1.3 %collective-permute-start.1 = (f32[7,8,128]{2,1,0:T(8,128)S(1)}, f32[7,8,128]{2,1,0:T(8,128)S(1)}, u32[]{:S(2)}, u32[]{:S(2)}) collective-permute-start(f32[7,8,128]{2,1,0:T(8,128)S(1)} %get-tuple-element.49), channel_id=1, source_target_pairs={{0,64},{1,65},{2,66},{3,67},{4,68},{5,69},{6,70},{7,71},{8,72},{9,... | collective-permute-start | bytes 86024 | tf_op jit(solution)/shard_map/ppermute | solution.py:489
  11.6 1.3 %collective-permute-start.3 = (f32[7,8,128]{2,1,0:T(8,128)S(1)}, f32[7,8,128]{2,1,0:T(8,128)S(1)}, u32[]{:S(2)}, u32[]{:S(2)}) collective-permute-start(f32[7,8,128]{2,1,0:T(8,128)S(1)} %get-tuple-element.50), channel_id=1, source_target_pairs={{0,65},{1,66},{2,67},{3,68},{4,69},{5,70},{6,71},{7,64},{8,79},{9,... | collective-permute-start | bytes 86024 | tf_op jit(solution)/shard_map/ppermute | solution.py:489
  12.8 0.7 collective-permute-start.2
  13.6 9.6 %collective-permute-done.3 = f32[7,8,128]{2,1,0:T(8,128)S(1)} collective-permute-done((f32[7,8,128]{2,1,0:T(8,128)S(1)}, f32[7,8,128]{2,1,0:T(8,128)S(1)}, u32[]{:S(2)}, u32[]{:S(2)}) %collective-permute-start.3) | collective-permute-done | bytes 28704 | tf_op jit(solution)/shard_map/ppermute | solution.py:489
  23.2 0.6 collective-permute-done.2
  23.8 2.8 %collective-permute-start.4 = (f32[7,8,128]{2,1,0:T(8,128)S(1)}, f32[7,8,128]{2,1,0:T(8,128)S(1)}, u32[]{:S(2)}, u32[]{:S(2)}) collective-permute-start(f32[7,8,128]{2,1,0:T(8,128)S(1)} %add_add_fusion.3), channel_id=1, source_target_pairs={{0,192},{1,193},{2,194},{3,195},{4,196},{5,197},{6,198},{7,199},{8... | collective-permute-start | bytes 86024 | tf_op jit(solution)/shard_map/ppermute | solution.py:489
  26.6 1.3 %collective-permute-done.4 = f32[7,8,128]{2,1,0:T(8,128)S(1)} collective-permute-done((f32[7,8,128]{2,1,0:T(8,128)S(1)}, f32[7,8,128]{2,1,0:T(8,128)S(1)}, u32[]{:S(2)}, u32[]{:S(2)}) %collective-permute-start.4) | collective-permute-done | bytes 28704 | tf_op jit(solution)/shard_map/ppermute | solution.py:489
  27.9 2.5 %collective-permute-start.7 = (f32[7,8,128]{2,1,0:T(8,128)S(1)}, f32[7,8,128]{2,1,0:T(8,128)S(1)}, u32[]{:S(2)}, u32[]{:S(2)}) collective-permute-start(f32[7,8,128]{2,1,0:T(8,128)S(1)} %add.52), channel_id=1, source_target_pairs={{0,48},{1,49},{2,50},{3,51},{4,52},{5,53},{6,54},{7,55},{8,56},{9,... | collective-permute-start | bytes 86024 | tf_op jit(solution)/shard_map/ppermute | solution.py:489
  30.4 0.5 collective-permute-start.6
  30.9 0.3 collective-permute-start.5
  31.2 0.7 collective-permute-done.7
  31.8 2.8 %collective-permute-done.6 = f32[7,8,128]{2,1,0:T(8,128)S(1)} collective-permute-done((f32[7,8,128]{2,1,0:T(8,128)S(1)}, f32[7,8,128]{2,1,0:T(8,128)S(1)}, u32[]{:S(2)}, u32[]{:S(2)}) %collective-permute-start.6) | collective-permute-done | bytes 28704 | tf_op jit(solution)/shard_map/ppermute | solution.py:489
  34.6 0.0 collective-permute-done.5
  34.6 4.6 %collective-permute-start.8 = (f32[7,8,128]{2,1,0:T(8,128)S(1)}, f32[7,8,128]{2,1,0:T(8,128)S(1)}, u32[]{:S(2)}, u32[]{:S(2)}) collective-permute-start(f32[7,8,128]{2,1,0:T(8,128)S(1)} %add_add_fusion.2.refs_2_), channel_id=1, source_target_pairs={{0,8},{1,9},{2,10},{3,11},{4,12},{5,13},{6,14},{7,15},{8,0},{9,1},... | collective-permute-start | bytes 86024 | tf_op jit(solution)/shard_map/ppermute | solution.py:489
  39.2 2.1 %sweep.2.refs_1_ = f32[432,8,128]{2,1,0:T(8,128)S(1)} custom-call(f32[3,8,128]{2,1,0:T(8,128)S(1)} %get-tuple-element.26.tiles_ref.refs_0_, f32[432,8,128]{2,1,0:T(8,128)S(1)} %get-tuple-element.30.f_ref), custom_call_target="tpu_custom_call" | custom-call | tf_op jit(solution)/shard_map/sweep/pallas_call | solution.py:442
  41.4 0.0 collective-permute-done.9.refs_2_
  41.4 0.4 rise.2.refs_4_
  41.8 0.0 copy-start
  41.8 0.7 fall.2.refs_5_
  42.6 1.4 %shard_map.37 = (f32[432,8,128]{2,1,0:T(8,128)S(1)}, f32[14,8,128]{2,1,0:T(8,128)S(1)}, f32[14,8,128]{2,1,0:T(8,128)S(1)}, f32[144,8,128]{2,1,0:T(8,128)S(1)}, f32[144,8,128]{2,1,0:T(8,128)S(1)}) custom-call(f32[3,8,128]{2,1,0:T(8,128)S(1)} %get-tuple-element.26.tiles_ref.refs_0_, s32[8,128]{1,0:T(8,128)S(1)} %bitcast.3, ...), custom_call_target="tpu_custom_call" | custom-call | tf_op jit(solution)/shard_map/pallas_call | solution.py:476
  44.0 0.3 collective-permute-start.11
  44.3 1.2 %collective-permute-done.11 = f32[14,8,128]{2,1,0:T(8,128)S(1)} collective-permute-done((f32[14,8,128]{2,1,0:T(8,128)S(1)}, f32[14,8,128]{2,1,0:T(8,128)S(1)}, u32[]{:S(2)}, u32[]{:S(2)}) %collective-permute-start.11) | collective-permute-done | bytes 57376 | tf_op jit(solution)/shard_map/ppermute | solution.py:489
  45.5 0.1 collective-permute-start.20
  45.6 2.7 %collective-permute-start.21 = (f32[144,8,128]{2,1,0:T(8,128)S(1)}, f32[144,8,128]{2,1,0:T(8,128)S(1)}, u32[]{:S(2)}, u32[]{:S(2)}) collective-permute-start(f32[144,8,128]{2,1,0:T(8,128)S(1)} %get-tuple-element.45), channel_id=1, source_target_pairs={{0,7},{1,0},{2,1},{3,2},{4,3},{5,4},{6,5},{7,6},{8,15},{9,8},{10,9... | collective-permute-start | bytes 1769480 | tf_op jit(solution)/shard_map/ppermute | solution.py:489
  48.3 0.0 collective-permute-start.12
  48.3 1.4 %collective-permute-start.14 = (f32[7,8,128]{2,1,0:T(8,128)S(1)}, f32[7,8,128]{2,1,0:T(8,128)S(1)}, u32[]{:S(2)}, u32[]{:S(2)}) collective-permute-start(f32[7,8,128]{2,1,0:T(8,128)S(1)} %get-tuple-element.48), channel_id=1, source_target_pairs={{0,65},{1,66},{2,67},{3,68},{4,69},{5,70},{6,71},{7,64},{8,79},{9,... | collective-permute-start | bytes 86024 | tf_op jit(solution)/shard_map/ppermute | solution.py:489
  49.7 0.8 %collective-permute-start.13 = (f32[7,8,128]{2,1,0:T(8,128)S(1)}, f32[7,8,128]{2,1,0:T(8,128)S(1)}, u32[]{:S(2)}, u32[]{:S(2)}) collective-permute-start(f32[7,8,128]{2,1,0:T(8,128)S(1)} %get-tuple-element.48), channel_id=1, source_target_pairs={{0,1},{1,2},{2,3},{3,4},{4,5},{5,6},{6,7},{7,0},{8,15},{9,8},{10,9... | collective-permute-start | bytes 86024 | tf_op jit(solution)/shard_map/ppermute | solution.py:489
  50.5 0.7 collective-permute-done.12
  51.3 9.9 %collective-permute-done.14 = f32[7,8,128]{2,1,0:T(8,128)S(1)} collective-permute-done((f32[7,8,128]{2,1,0:T(8,128)S(1)}, f32[7,8,128]{2,1,0:T(8,128)S(1)}, u32[]{:S(2)}, u32[]{:S(2)}) %collective-permute-start.14) | collective-permute-done | bytes 28704 | tf_op jit(solution)/shard_map/ppermute | solution.py:489
  61.2 0.6 collective-permute-done.13
  61.8 2.2 %collective-permute-start.15 = (f32[7,8,128]{2,1,0:T(8,128)S(1)}, f32[7,8,128]{2,1,0:T(8,128)S(1)}, u32[]{:S(2)}, u32[]{:S(2)}) collective-permute-start(f32[7,8,128]{2,1,0:T(8,128)S(1)} %add_add_fusion.1), channel_id=1, source_target_pairs={{0,192},{1,193},{2,194},{3,195},{4,196},{5,197},{6,198},{7,199},{8... | collective-permute-start | bytes 86024 | tf_op jit(solution)/shard_map/ppermute | solution.py:489
  64.0 1.8 %collective-permute-done.15 = f32[7,8,128]{2,1,0:T(8,128)S(1)} collective-permute-done((f32[7,8,128]{2,1,0:T(8,128)S(1)}, f32[7,8,128]{2,1,0:T(8,128)S(1)}, u32[]{:S(2)}, u32[]{:S(2)}) %collective-permute-start.15) | collective-permute-done | bytes 28704 | tf_op jit(solution)/shard_map/ppermute | solution.py:489
  65.8 1.3 %collective-permute-start.18 = (f32[7,8,128]{2,1,0:T(8,128)S(1)}, f32[7,8,128]{2,1,0:T(8,128)S(1)}, u32[]{:S(2)}, u32[]{:S(2)}) collective-permute-start(f32[7,8,128]{2,1,0:T(8,128)S(1)} %add.60), channel_id=1, source_target_pairs={{0,48},{1,49},{2,50},{3,51},{4,52},{5,53},{6,54},{7,55},{8,56},{9,... | collective-permute-start | bytes 86024 | tf_op jit(solution)/shard_map/ppermute | solution.py:489
  67.1 0.6 collective-permute-start.17
  67.8 1.3 %collective-permute-start.16 = (f32[7,8,128]{2,1,0:T(8,128)S(1)}, f32[7,8,128]{2,1,0:T(8,128)S(1)}, u32[]{:S(2)}, u32[]{:S(2)}) collective-permute-start(f32[7,8,128]{2,1,0:T(8,128)S(1)} %add.60), channel_id=1, source_target_pairs={{0,16},{1,17},{2,18},{3,19},{4,20},{5,21},{6,22},{7,23},{8,24},{9,... | collective-permute-start | bytes 86024 | tf_op jit(solution)/shard_map/ppermute | solution.py:489
  69.1 0.7 collective-permute-done.18
  69.7 1.6 %collective-permute-done.17 = f32[7,8,128]{2,1,0:T(8,128)S(1)} collective-permute-done((f32[7,8,128]{2,1,0:T(8,128)S(1)}, f32[7,8,128]{2,1,0:T(8,128)S(1)}, u32[]{:S(2)}, u32[]{:S(2)}) %collective-permute-start.17) | collective-permute-done | bytes 28704 | tf_op jit(solution)/shard_map/ppermute | solution.py:489
  71.4 0.0 collective-permute-done.16
  71.4 4.0 %collective-permute-start.19 = (f32[7,8,128]{2,1,0:T(8,128)S(1)}, f32[7,8,128]{2,1,0:T(8,128)S(1)}, u32[]{:S(2)}, u32[]{:S(2)}) collective-permute-start(f32[7,8,128]{2,1,0:T(8,128)S(1)} %add_add_fusion.refs_2_), channel_id=1, source_target_pairs={{0,8},{1,9},{2,10},{3,11},{4,12},{5,13},{6,14},{7,15},{8,0},{9,1},... | collective-permute-start | bytes 86024 | tf_op jit(solution)/shard_map/ppermute | solution.py:489
  75.4 2.1 %sweep.3.refs_1_ = f32[432,8,128]{2,1,0:T(8,128)S(1)} custom-call(f32[3,8,128]{2,1,0:T(8,128)S(1)} %get-tuple-element.26.tiles_ref.refs_0_, f32[432,8,128]{2,1,0:T(8,128)S(1)} %get-tuple-element.40.f_ref), custom_call_target="tpu_custom_call" | custom-call | tf_op jit(solution)/shard_map/sweep/pallas_call | solution.py:442
  77.6 0.4 rise.3.refs_4_
  78.0 0.7 fall.3.refs_5_
  78.8 1.6 %shard_map.38 = f32[432,8,128]{2,1,0:T(8,128)} custom-call(f32[3,8,128]{2,1,0:T(8,128)S(1)} %get-tuple-element.26.tiles_ref.refs_0_, s32[8,128]{1,0:T(8,128)S(1)} %bitcast.4, f32[7,8,128]{2,1,0:T(8,128)S(1)} %add_add_fusion.refs_2_, f32[7,8,128]{2,1,0:T(8,128)S(1)} %collective-permute-done.19.refs_3_, f32[288,8,128]{2,1,0:T(8,128)S(1)} %rise.3.refs_4_, ...), custom_call_target="tpu_custom_call" | custom-call | tf_op jit(solution)/shard_map/pallas_call | solution.py:476
  (17 shorter events, 0.1 us)
Async XLA Ops:
  2.1 4.2 %collective-permute-start = (f32[14,8,128]{2,1,0:T(8,128)S(1)}, f32[14,8,128]{2,1,0:T(8,128)S(1)}, u32[]{:S(2)}, u32[]{:S(2)}) collective-permute-start(f32[14,8,128]{2,1,0:T(8,128)S(1)} %get-tuple-element.28), channel_id=1, source_target_pairs={{0,8},{1,9},{2,10},{3,11},{4,12},{5,13},{6,14},{7,15},{8,0},{9,1},... | collective-permute-start | bytes 172040 | tf_op jit(solution)/shard_map/ppermute | solution.py:489
  6.3 35.1 %collective-permute-start.9 = (f32[144,8,128]{2,1,0:T(8,128)S(1)}, f32[144,8,128]{2,1,0:T(8,128)S(1)}, u32[]{:S(2)}, u32[]{:S(2)}) collective-permute-start(f32[144,8,128]{2,1,0:T(8,128)S(1)} %get-tuple-element.32), channel_id=1, source_target_pairs={{0,1},{1,2},{2,3},{3,4},{4,5},{5,6},{6,7},{7,0},{8,9},{9,10},{10,1... | collective-permute-start | bytes 1769480 | tf_op jit(solution)/shard_map/ppermute | solution.py:489
  6.3 35.1 %collective-permute-start.10 = (f32[144,8,128]{2,1,0:T(8,128)S(1)}, f32[144,8,128]{2,1,0:T(8,128)S(1)}, u32[]{:S(2)}, u32[]{:S(2)}) collective-permute-start(f32[144,8,128]{2,1,0:T(8,128)S(1)} %get-tuple-element.35), channel_id=1, source_target_pairs={{0,7},{1,0},{2,1},{3,2},{4,3},{5,4},{6,5},{7,6},{8,15},{9,8},{10,9... | collective-permute-start | bytes 1769480 | tf_op jit(solution)/shard_map/ppermute | solution.py:489
  10.3 3.3 %collective-permute-start.1 = (f32[7,8,128]{2,1,0:T(8,128)S(1)}, f32[7,8,128]{2,1,0:T(8,128)S(1)}, u32[]{:S(2)}, u32[]{:S(2)}) collective-permute-start(f32[7,8,128]{2,1,0:T(8,128)S(1)} %get-tuple-element.49), channel_id=1, source_target_pairs={{0,64},{1,65},{2,66},{3,67},{4,68},{5,69},{6,70},{7,71},{8,72},{9,... | collective-permute-start | bytes 86024 | tf_op jit(solution)/shard_map/ppermute | solution.py:489
  11.6 11.6 %collective-permute-start.3 = (f32[7,8,128]{2,1,0:T(8,128)S(1)}, f32[7,8,128]{2,1,0:T(8,128)S(1)}, u32[]{:S(2)}, u32[]{:S(2)}) collective-permute-start(f32[7,8,128]{2,1,0:T(8,128)S(1)} %get-tuple-element.50), channel_id=1, source_target_pairs={{0,65},{1,66},{2,67},{3,68},{4,69},{5,70},{6,71},{7,64},{8,79},{9,... | collective-permute-start | bytes 86024 | tf_op jit(solution)/shard_map/ppermute | solution.py:489
  12.8 11.0 %collective-permute-start.2 = (f32[7,8,128]{2,1,0:T(8,128)S(1)}, f32[7,8,128]{2,1,0:T(8,128)S(1)}, u32[]{:S(2)}, u32[]{:S(2)}) collective-permute-start(f32[7,8,128]{2,1,0:T(8,128)S(1)} %get-tuple-element.50), channel_id=1, source_target_pairs={{0,1},{1,2},{2,3},{3,4},{4,5},{5,6},{6,7},{7,0},{8,15},{9,8},{10,9... | collective-permute-start | bytes 86024 | tf_op jit(solution)/shard_map/ppermute | solution.py:489
  23.8 4.1 %collective-permute-start.4 = (f32[7,8,128]{2,1,0:T(8,128)S(1)}, f32[7,8,128]{2,1,0:T(8,128)S(1)}, u32[]{:S(2)}, u32[]{:S(2)}) collective-permute-start(f32[7,8,128]{2,1,0:T(8,128)S(1)} %add_add_fusion.3), channel_id=1, source_target_pairs={{0,192},{1,193},{2,194},{3,195},{4,196},{5,197},{6,198},{7,199},{8... | collective-permute-start | bytes 86024 | tf_op jit(solution)/shard_map/ppermute | solution.py:489
  27.9 3.9 %collective-permute-start.7 = (f32[7,8,128]{2,1,0:T(8,128)S(1)}, f32[7,8,128]{2,1,0:T(8,128)S(1)}, u32[]{:S(2)}, u32[]{:S(2)}) collective-permute-start(f32[7,8,128]{2,1,0:T(8,128)S(1)} %add.52), channel_id=1, source_target_pairs={{0,48},{1,49},{2,50},{3,51},{4,52},{5,53},{6,54},{7,55},{8,56},{9,... | collective-permute-start | bytes 86024 | tf_op jit(solution)/shard_map/ppermute | solution.py:489
  30.4 4.2 %collective-permute-start.6 = (f32[7,8,128]{2,1,0:T(8,128)S(1)}, f32[7,8,128]{2,1,0:T(8,128)S(1)}, u32[]{:S(2)}, u32[]{:S(2)}) collective-permute-start(f32[7,8,128]{2,1,0:T(8,128)S(1)} %add.52), channel_id=1, source_target_pairs={{0,32},{1,33},{2,34},{3,35},{4,36},{5,37},{6,38},{7,39},{8,40},{9,... | collective-permute-start | bytes 86024 | tf_op jit(solution)/shard_map/ppermute | solution.py:489
  30.9 3.7 %collective-permute-start.5 = (f32[7,8,128]{2,1,0:T(8,128)S(1)}, f32[7,8,128]{2,1,0:T(8,128)S(1)}, u32[]{:S(2)}, u32[]{:S(2)}) collective-permute-start(f32[7,8,128]{2,1,0:T(8,128)S(1)} %add.52), channel_id=1, source_target_pairs={{0,16},{1,17},{2,18},{3,19},{4,20},{5,21},{6,22},{7,23},{8,24},{9,... | collective-permute-start | bytes 86024 | tf_op jit(solution)/shard_map/ppermute | solution.py:489
  34.6 7.9 %collective-permute-start.8 = (f32[7,8,128]{2,1,0:T(8,128)S(1)}, f32[7,8,128]{2,1,0:T(8,128)S(1)}, u32[]{:S(2)}, u32[]{:S(2)}) collective-permute-start(f32[7,8,128]{2,1,0:T(8,128)S(1)} %add_add_fusion.2.refs_2_), channel_id=1, source_target_pairs={{0,8},{1,9},{2,10},{3,11},{4,12},{5,13},{6,14},{7,15},{8,0},{9,1},... | collective-permute-start | bytes 86024 | tf_op jit(solution)/shard_map/ppermute | solution.py:489
  41.8 0.7 copy-start
  44.0 1.5 %collective-permute-start.11 = (f32[14,8,128]{2,1,0:T(8,128)S(1)}, f32[14,8,128]{2,1,0:T(8,128)S(1)}, u32[]{:S(2)}, u32[]{:S(2)}) collective-permute-start(f32[14,8,128]{2,1,0:T(8,128)S(1)} %get-tuple-element.38), channel_id=1, source_target_pairs={{0,8},{1,9},{2,10},{3,11},{4,12},{5,13},{6,14},{7,15},{8,0},{9,1},... | collective-permute-start | bytes 172040 | tf_op jit(solution)/shard_map/ppermute | solution.py:489
  45.5 32.1 %collective-permute-start.20 = (f32[144,8,128]{2,1,0:T(8,128)S(1)}, f32[144,8,128]{2,1,0:T(8,128)S(1)}, u32[]{:S(2)}, u32[]{:S(2)}) collective-permute-start(f32[144,8,128]{2,1,0:T(8,128)S(1)} %get-tuple-element.42), channel_id=1, source_target_pairs={{0,1},{1,2},{2,3},{3,4},{4,5},{5,6},{6,7},{7,0},{8,9},{9,10},{10,1... | collective-permute-start | bytes 1769480 | tf_op jit(solution)/shard_map/ppermute | solution.py:489
  45.6 32.0 %collective-permute-start.21 = (f32[144,8,128]{2,1,0:T(8,128)S(1)}, f32[144,8,128]{2,1,0:T(8,128)S(1)}, u32[]{:S(2)}, u32[]{:S(2)}) collective-permute-start(f32[144,8,128]{2,1,0:T(8,128)S(1)} %get-tuple-element.45), channel_id=1, source_target_pairs={{0,7},{1,0},{2,1},{3,2},{4,3},{5,4},{6,5},{7,6},{8,15},{9,8},{10,9... | collective-permute-start | bytes 1769480 | tf_op jit(solution)/shard_map/ppermute | solution.py:489
  48.3 3.0 %collective-permute-start.12 = (f32[7,8,128]{2,1,0:T(8,128)S(1)}, f32[7,8,128]{2,1,0:T(8,128)S(1)}, u32[]{:S(2)}, u32[]{:S(2)}) collective-permute-start(f32[7,8,128]{2,1,0:T(8,128)S(1)} %get-tuple-element.47), channel_id=1, source_target_pairs={{0,64},{1,65},{2,66},{3,67},{4,68},{5,69},{6,70},{7,71},{8,72},{9,... | collective-permute-start | bytes 86024 | tf_op jit(solution)/shard_map/ppermute | solution.py:489
  48.3 12.9 %collective-permute-start.14 = (f32[7,8,128]{2,1,0:T(8,128)S(1)}, f32[7,8,128]{2,1,0:T(8,128)S(1)}, u32[]{:S(2)}, u32[]{:S(2)}) collective-permute-start(f32[7,8,128]{2,1,0:T(8,128)S(1)} %get-tuple-element.48), channel_id=1, source_target_pairs={{0,65},{1,66},{2,67},{3,68},{4,69},{5,70},{6,71},{7,64},{8,79},{9,... | collective-permute-start | bytes 86024 | tf_op jit(solution)/shard_map/ppermute | solution.py:489
  49.7 12.1 %collective-permute-start.13 = (f32[7,8,128]{2,1,0:T(8,128)S(1)}, f32[7,8,128]{2,1,0:T(8,128)S(1)}, u32[]{:S(2)}, u32[]{:S(2)}) collective-permute-start(f32[7,8,128]{2,1,0:T(8,128)S(1)} %get-tuple-element.48), channel_id=1, source_target_pairs={{0,1},{1,2},{2,3},{3,4},{4,5},{5,6},{6,7},{7,0},{8,15},{9,8},{10,9... | collective-permute-start | bytes 86024 | tf_op jit(solution)/shard_map/ppermute | solution.py:489
  61.8 4.0 %collective-permute-start.15 = (f32[7,8,128]{2,1,0:T(8,128)S(1)}, f32[7,8,128]{2,1,0:T(8,128)S(1)}, u32[]{:S(2)}, u32[]{:S(2)}) collective-permute-start(f32[7,8,128]{2,1,0:T(8,128)S(1)} %add_add_fusion.1), channel_id=1, source_target_pairs={{0,192},{1,193},{2,194},{3,195},{4,196},{5,197},{6,198},{7,199},{8... | collective-permute-start | bytes 86024 | tf_op jit(solution)/shard_map/ppermute | solution.py:489
  65.8 3.9 %collective-permute-start.18 = (f32[7,8,128]{2,1,0:T(8,128)S(1)}, f32[7,8,128]{2,1,0:T(8,128)S(1)}, u32[]{:S(2)}, u32[]{:S(2)}) collective-permute-start(f32[7,8,128]{2,1,0:T(8,128)S(1)} %add.60), channel_id=1, source_target_pairs={{0,48},{1,49},{2,50},{3,51},{4,52},{5,53},{6,54},{7,55},{8,56},{9,... | collective-permute-start | bytes 86024 | tf_op jit(solution)/shard_map/ppermute | solution.py:489
  67.1 4.2 %collective-permute-start.17 = (f32[7,8,128]{2,1,0:T(8,128)S(1)}, f32[7,8,128]{2,1,0:T(8,128)S(1)}, u32[]{:S(2)}, u32[]{:S(2)}) collective-permute-start(f32[7,8,128]{2,1,0:T(8,128)S(1)} %add.60), channel_id=1, source_target_pairs={{0,32},{1,33},{2,34},{3,35},{4,36},{5,37},{6,38},{7,39},{8,40},{9,... | collective-permute-start | bytes 86024 | tf_op jit(solution)/shard_map/ppermute | solution.py:489
  67.8 3.6 %collective-permute-start.16 = (f32[7,8,128]{2,1,0:T(8,128)S(1)}, f32[7,8,128]{2,1,0:T(8,128)S(1)}, u32[]{:S(2)}, u32[]{:S(2)}) collective-permute-start(f32[7,8,128]{2,1,0:T(8,128)S(1)} %add.60), channel_id=1, source_target_pairs={{0,16},{1,17},{2,18},{3,19},{4,20},{5,21},{6,22},{7,23},{8,24},{9,... | collective-permute-start | bytes 86024 | tf_op jit(solution)/shard_map/ppermute | solution.py:489
  71.4 7.4 %collective-permute-start.19 = (f32[7,8,128]{2,1,0:T(8,128)S(1)}, f32[7,8,128]{2,1,0:T(8,128)S(1)}, u32[]{:S(2)}, u32[]{:S(2)}) collective-permute-start(f32[7,8,128]{2,1,0:T(8,128)S(1)} %add_add_fusion.refs_2_), channel_id=1, source_target_pairs={{0,8},{1,9},{2,10},{3,11},{4,12},{5,13},{6,14},{7,15},{8,0},{9,1},... | collective-permute-start | bytes 86024 | tf_op jit(solution)/shard_map/ppermute | solution.py:489
